TPU v7x, 32 devices: a whole 2x2x4 slice. The times are simulated.
32 devices in a mesh: batch: 8 (over z, x), mp: 4 (over y, core).
Axes of the slice: x: 2, y: 2, z: 4, core: 2. Of those that a mesh axis runs over, the one named last changes fastest.
Arguments:
- tokens: bfloat16 [2048, 2048], P('batch'), may hold values from -6 to 6
- lengths: int32 [8], P('batch'), may hold values from 64 to 256, as said below
- cotangent: bfloat16 [2048, 2048], P('batch'), may hold values from -6 to 6
- norm1_gain: float32 [2048], replicated, may hold values from 0.25 to 1.75
- norm1_shift: float32 [2048], replicated, may hold values from -1 to 1
- qkv_weight: bfloat16 [2048, 3, 2048], P(None, None, 'mp'), may hold values from -0.125 to 0.125
- qkv_bias: float32 [3, 32, 64], P(None, 'mp'), may hold values from -1 to 1
- sub1_gain: float32 [32, 64], P('mp'), may hold values from 0.25 to 1.75
- sub1_shift: float32 [32, 64], P('mp'), may hold values from -1 to 1
- out_weight: bfloat16 [2048, 2048], P('mp'), may hold values from -0.125 to 0.125
- out_bias: float32 [2048], replicated, may hold values from -1 to 1
- norm2_gain: float32 [2048], replicated, may hold values from 0.25 to 1.75
- norm2_shift: float32 [2048], replicated, may hold values from -1 to 1
- up_weight: bfloat16 [2048, 8192], P(None, 'mp'), may hold values from -0.125 to 0.125
- up_bias: float32 [8192], P('mp'), may hold values from -1 to 1
- sub2_gain: float32 [8192], P('mp'), may hold values from 0.25 to 1.75
- sub2_shift: float32 [8192], P('mp'), may hold values from -1 to 1
- down_weight: bfloat16 [8192, 2048], P('mp'), may hold values from -0.0625 to 0.0625
- down_bias: float32 [2048], replicated, may hold values from -1 to 1
Outputs:
- result: bfloat16 [2048, 2048], P('batch')
- tokens_grad: bfloat16 [2048, 2048], P('batch')
- norm1_gain_grad: float32 [2048], P('batch')
- norm1_shift_grad: float32 [2048], P('batch')
- qkv_weight_grad: float32 [2048, 3, 2048], P('batch', None, 'mp')
- qkv_bias_grad: float32 [3, 32, 64], P(None, 'mp', 'batch')
- sub1_gain_grad: float32 [32, 64], P('mp', 'batch')
- sub1_shift_grad: float32 [32, 64], P('mp', 'batch')
- out_weight_grad: float32 [2048, 2048], P('mp', 'batch')
- out_bias_grad: float32 [2048], P('batch')
- norm2_gain_grad: float32 [2048], P('batch')
- norm2_shift_grad: float32 [2048], P('batch')
- up_weight_grad: float32 [2048, 8192], P('batch', 'mp')
- up_bias_grad: float32 [64, 128], P('mp', 'batch')
- sub2_gain_grad: float32 [64, 128], P('mp', 'batch')
- sub2_shift_grad: float32 [64, 128], P('mp', 'batch')
- down_weight_grad: float32 [8192, 2048], P('mp', 'batch')
- down_bias_grad: float32 [2048], P('batch')
Inputs may be any that keep to these rules, and one draw needn't show every extreme that they name: lengths[r] counts the valid leading tokens of sequence r; some sequence has exactly 256.
All inputs are finite; a program needn't handle non-finite values.
Results may differ from a plain program's by a relative error of at most 0.015.
Values sent between devices are 32-bit elements; how exact they have to be, the bound alone decides.
No kernel may reach another device: no remote copies, remote signals or barrier semaphores. Data moves between devices by JAX's collectives and lax.ppermute only.
A program may use at most 256 MiB of HBM per device.

v0:
```python
import math

import jax
import jax.numpy as jnp
from jax import lax
from jax.sharding import PartitionSpec as P

D = 2048
HEADS = 32
HD = 64
FF = 8192
QBLOCK = 256


norm_eps = 1e-05
rope_base = 10000.0
xpos_base = 512.0
masked_score = -1e30


def normalize(values, gain_row, shift_row):
    center = values - jnp.mean(values, axis=-1, keepdims=True)
    spread = jnp.mean(center * center, axis=-1, keepdims=True)
    return center * lax.rsqrt(spread + norm_eps) * gain_row + shift_row


def exact_gelu(values):
    return jax.nn.gelu(values, approximate=False)


def xpos_tables(count_rows, head_width):
    half_width = head_width // 2
    places = jnp.arange(count_rows, dtype=jnp.float32)
    pair_index = jnp.arange(half_width, dtype=jnp.float32)
    frequency = jnp.exp(-math.log(rope_base) * pair_index / half_width)
    angles = places[:, None] * frequency[None, :]
    zeta_base = (2.0 * pair_index + 0.4 * head_width) / (1.4 * head_width)
    powers = (places[:, None] - count_rows // 2) / xpos_base
    factor = jnp.exp(powers * jnp.log(zeta_base)[None, :])
    return (jnp.cos(angles), jnp.sin(angles), factor)


def rotate(values, cosine, sine_table, factor):
    half_width = values.shape[-1] // 2
    first_half = values[..., :half_width]
    second_half = values[..., half_width:]
    cos_rows = cosine[:, None, :]
    sin_rows = sine_table[:, None, :]
    scale_rows = factor[:, None, :]
    return jnp.concatenate(
        [
            (first_half * cos_rows - second_half * sin_rows) * scale_rows,
            (second_half * cos_rows + first_half * sin_rows) * scale_rows,
        ],
        axis=-1,
    )


def split_norm(values, gain_row, shift_row, full_width):
    totals = lax.psum(jnp.sum(values, axis=-1), "mp")
    center = values - (totals / full_width)[:, None]
    spread = lax.psum(jnp.sum(center * center, axis=-1), "mp") / full_width
    inverse = lax.rsqrt(spread + norm_eps)[:, None]
    unit_rows = center * inverse
    return (unit_rows * gain_row + shift_row, unit_rows, inverse)


def split_norm_back(grad_out, unit_rows, inverse, gain_row, full_width):
    scaled = grad_out * gain_row
    first_sum, second_sum = lax.psum(
        (jnp.sum(scaled, axis=-1), jnp.sum(scaled * unit_rows, axis=-1)), "mp"
    )
    grad_in = inverse * (
        scaled - (first_sum / full_width)[:, None] - unit_rows * (second_sum / full_width)[:, None]
    )
    return (grad_in, jnp.sum(grad_out * unit_rows, axis=0), jnp.sum(grad_out, axis=0))


def branch_total(partial_rows):
    return lax.psum(partial_rows, "mp")


def input_total(partial_rows):
    return lax.psum(partial_rows, "mp")


def local(
    tokens,
    lengths,
    cotangent,
    norm1_gain,
    norm1_shift,
    qkv_weight,
    qkv_bias,
    sub1_gain,
    sub1_shift,
    out_weight,
    out_bias,
    norm2_gain,
    norm2_shift,
    up_weight,
    up_bias,
    sub2_gain,
    sub2_shift,
    down_weight,
    down_bias,
):
    seq_length = lengths[0]
    slot_count = tokens.shape[0]
    local_width = out_weight.shape[0]
    local_heads = local_width // HD
    hidden_local = up_weight.shape[1]
    attn_width = HEADS * HD
    inv_root = 1.0 / math.sqrt(HD)
    inputs = tokens.astype(jnp.float32)
    normed_full, norm1_pull = jax.vjp(normalize, inputs, norm1_gain, norm1_shift)
    normed = normed_full.astype(jnp.bfloat16)
    qkv_flat = qkv_weight.reshape(D, 3 * local_width)
    mixed_qkv = jnp.dot(normed, qkv_flat, preferred_element_type=jnp.float32) + qkv_bias.reshape(
        3 * local_width
    )
    mixed_qkv = mixed_qkv.reshape(slot_count, 3, local_heads, HD)
    cosine, sine_table, factor = xpos_tables(slot_count, HD)

    def turn_query(values):
        return rotate(values, cosine, sine_table, factor)

    def turn_key(values):
        return rotate(values, cosine, sine_table, 1.0 / factor)

    query_rot, query_pull = jax.vjp(turn_query, mixed_qkv[:, 0])
    key_rot, key_pull = jax.vjp(turn_key, mixed_qkv[:, 1])
    queries = query_rot.astype(jnp.bfloat16)
    key_rows = key_rot.astype(jnp.bfloat16)
    value_rows = mixed_qkv[:, 2].astype(jnp.bfloat16)
    places = jnp.arange(slot_count, dtype=jnp.int32)
    key_valid = places < seq_length
    starts = jnp.arange(slot_count // QBLOCK, dtype=jnp.int32) * QBLOCK

    def block_scores(block_start):
        scores = (
            jnp.einsum("qhd,khd->hqk", queries, key_rows, preferred_element_type=jnp.float32)
            * inv_root
        )
        rows_here = block_start + jnp.arange(QBLOCK, dtype=jnp.int32)
        allowed = (places[None, :] <= rows_here[:, None]) & key_valid[None, :]
        return (queries, jnp.where(allowed[None], scores, masked_score))

    def attend_block(block_start):
        block_q, scores = block_scores(block_start)
        row_peak = jnp.max(scores, axis=-1, keepdims=True)
        exp_scores = jnp.exp(scores - row_peak)
        exp_total = jnp.sum(exp_scores, axis=-1, keepdims=True)
        attn_probs = (exp_scores / exp_total).astype(jnp.bfloat16)
        block_out = jnp.einsum(
            "hqk,khd->qhd", attn_probs, value_rows, preferred_element_type=jnp.float32
        )
        return (block_out, row_peak + jnp.log(exp_total))

    attended, log_totals = lax.map(attend_block, starts)
    attended = attended.reshape(slot_count, local_width)
    sub1_gain_row = sub1_gain.reshape(local_width)
    sub1_out, sub1_unit, sub1_inverse = split_norm(
        attended, sub1_gain_row, sub1_shift.reshape(local_width), attn_width
    )
    sub1_low = sub1_out.astype(jnp.bfloat16)
    middle = (
        inputs
        + branch_total(jnp.dot(sub1_low, out_weight, preferred_element_type=jnp.float32))
        + out_bias
    )
    normed2_full, norm2_pull = jax.vjp(normalize, middle, norm2_gain, norm2_shift)
    normed2 = normed2_full.astype(jnp.bfloat16)
    upper_pre = jnp.dot(normed2, up_weight, preferred_element_type=jnp.float32) + up_bias
    active, gelu_pull = jax.vjp(exact_gelu, upper_pre)
    sub2_out, sub2_unit, sub2_inverse = split_norm(active, sub2_gain, sub2_shift, FF)
    sub2_low = sub2_out.astype(jnp.bfloat16)
    result = (
        middle
        + branch_total(jnp.dot(sub2_low, down_weight, preferred_element_type=jnp.float32))
        + down_bias
    ).astype(jnp.bfloat16)
    keep_rows = (places < seq_length).astype(jnp.float32)[:, None]
    grad_out = cotangent.astype(jnp.float32) * keep_rows
    grad_branch2 = grad_out.astype(jnp.bfloat16)
    grad_down_weight = jnp.einsum(
        "tf,td->fd", sub2_low, grad_branch2, preferred_element_type=jnp.float32
    )
    grad_down_bias = jnp.sum(grad_out, axis=0)
    grad_sub2 = jnp.einsum(
        "td,fd->tf", grad_branch2, down_weight, preferred_element_type=jnp.float32
    )
    grad_active, grad_sub2_gain, grad_sub2_shift = split_norm_back(
        grad_sub2, sub2_unit, sub2_inverse, sub2_gain, FF
    )
    grad_upper = gelu_pull(grad_active)[0].astype(jnp.bfloat16)
    grad_up_weight = jnp.einsum(
        "td,tf->df", normed2, grad_upper, preferred_element_type=jnp.float32
    )
    grad_up_bias = jnp.sum(grad_upper, axis=0, dtype=jnp.float32)
    grad_normed2 = input_total(
        jnp.einsum("tf,df->td", grad_upper, up_weight, preferred_element_type=jnp.float32)
    )
    grad_middle_ln, grad_norm2_gain, grad_norm2_shift = norm2_pull(grad_normed2)
    grad_middle = grad_out + grad_middle_ln
    lane_rows = hidden_local // 128
    grad_branch = grad_middle.astype(jnp.bfloat16)
    grad_out_bias = jnp.sum(grad_middle, axis=0)
    grad_out_weight = jnp.einsum(
        "tw,td->wd", sub1_low, grad_branch, preferred_element_type=jnp.float32
    )
    grad_sub1 = jnp.einsum("td,wd->tw", grad_branch, out_weight, preferred_element_type=jnp.float32)
    grad_attended, grad_sub1_gain, grad_sub1_shift = split_norm_back(
        grad_sub1, sub1_unit, sub1_inverse, sub1_gain_row, attn_width
    )
    grad_heads = grad_attended.astype(jnp.bfloat16).reshape(slot_count, local_heads, HD)

    def back_block(carried, block_item):
        grad_keys, grad_values = carried
        block_start, block_total = block_item
        block_q, scores = block_scores(block_start)
        attn_probs = jnp.exp(scores - block_total)
        probs_low = attn_probs.astype(jnp.bfloat16)
        grad_probs = jnp.einsum(
            "qhd,khd->hqk", grad_heads, value_rows, preferred_element_type=jnp.float32
        )
        grad_values = grad_values + jnp.einsum(
            "hqk,qhd->khd", probs_low, grad_heads, preferred_element_type=jnp.float32
        )
        inner_sum = jnp.sum(attn_probs * grad_probs, axis=-1, keepdims=True)
        grad_scores = (attn_probs * (grad_probs - inner_sum)).astype(jnp.bfloat16)
        grad_block_q = (
            jnp.einsum("hqk,khd->qhd", grad_scores, key_rows, preferred_element_type=jnp.float32)
            * inv_root
        )
        grad_keys = (
            grad_keys
            + jnp.einsum("hqk,qhd->khd", grad_scores, block_q, preferred_element_type=jnp.float32)
            * inv_root
        )
        return ((grad_keys, grad_values), grad_block_q)

    zero_heads = jnp.zeros((slot_count, local_heads, HD), jnp.float32)
    (grad_keys, grad_values), grad_queries = lax.scan(
        back_block, (zero_heads, zero_heads), (starts, log_totals)
    )
    grad_queries = grad_queries.reshape(slot_count, local_heads, HD)
    grad_mixed = jnp.stack(
        [query_pull(grad_queries)[0], key_pull(grad_keys)[0], grad_values], axis=1
    )
    grad_mixed = grad_mixed.reshape(slot_count, 3 * local_width).astype(jnp.bfloat16)
    grad_qkv_weight = jnp.einsum(
        "td,tc->dc", normed, grad_mixed, preferred_element_type=jnp.float32
    ).reshape(D, 3, local_width)
    grad_qkv_bias = jnp.sum(grad_mixed, axis=0, dtype=jnp.float32).reshape(3, local_heads, HD)
    grad_normed = input_total(
        jnp.einsum("tc,dc->td", grad_mixed, qkv_flat, preferred_element_type=jnp.float32)
    )
    grad_inputs_ln, grad_norm1_gain, grad_norm1_shift = norm1_pull(grad_normed)
    tokens_grad = (grad_middle + grad_inputs_ln).astype(jnp.bfloat16)
    grad_parts = (
        lax.psum_scatter(grad_norm1_gain, "batch", scatter_dimension=0, tiled=True),
        lax.psum_scatter(grad_norm1_shift, "batch", scatter_dimension=0, tiled=True),
        lax.psum_scatter(grad_qkv_weight, "batch", scatter_dimension=0, tiled=True),
        lax.psum_scatter(grad_qkv_bias, "batch", scatter_dimension=2, tiled=True),
        lax.psum_scatter(
            grad_sub1_gain.reshape(local_heads, HD), "batch", scatter_dimension=1, tiled=True
        ),
        lax.psum_scatter(
            grad_sub1_shift.reshape(local_heads, HD), "batch", scatter_dimension=1, tiled=True
        ),
        lax.psum_scatter(grad_out_weight, "batch", scatter_dimension=1, tiled=True),
        lax.psum_scatter(grad_out_bias, "batch", scatter_dimension=0, tiled=True),
        lax.psum_scatter(grad_norm2_gain, "batch", scatter_dimension=0, tiled=True),
        lax.psum_scatter(grad_norm2_shift, "batch", scatter_dimension=0, tiled=True),
        lax.psum_scatter(grad_up_weight, "batch", scatter_dimension=0, tiled=True),
        lax.psum_scatter(
            grad_up_bias.reshape(lane_rows, 128), "batch", scatter_dimension=1, tiled=True
        ),
        lax.psum_scatter(
            grad_sub2_gain.reshape(lane_rows, 128), "batch", scatter_dimension=1, tiled=True
        ),
        lax.psum_scatter(
            grad_sub2_shift.reshape(lane_rows, 128), "batch", scatter_dimension=1, tiled=True
        ),
        lax.psum_scatter(grad_down_weight, "batch", scatter_dimension=1, tiled=True),
        lax.psum_scatter(grad_down_bias, "batch", scatter_dimension=0, tiled=True),
    )
    return (result, tokens_grad) + tuple(grad_parts)


def solution(mesh):
    in_specs = (
        P("batch", None),
        P("batch"),
        P("batch", None),
        P(),
        P(),
        P(None, None, "mp"),
        P(None, "mp", None),
        P("mp", None),
        P("mp", None),
        P("mp", None),
        P(),
        P(),
        P(),
        P(None, "mp"),
        P("mp"),
        P("mp"),
        P("mp"),
        P("mp", None),
        P(),
    )
    out_specs = (
        P("batch", None),
        P("batch", None),
        P("batch"),
        P("batch"),
        P("batch", None, "mp"),
        P(None, "mp", "batch"),
        P("mp", "batch"),
        P("mp", "batch"),
        P("mp", "batch"),
        P("batch"),
        P("batch"),
        P("batch"),
        P("batch", "mp"),
        P("mp", "batch"),
        P("mp", "batch"),
        P("mp", "batch"),
        P("mp", "batch"),
        P("batch"),
    )
    return jax.shard_map(local, mesh=mesh, in_specs=in_specs, out_specs=out_specs, check_vma=False)
```

profile of v0, /device:TPU:0, one launch (start us, length us, event | category | flops | bytes accessed | tf_op | source)
XLA Modules:
  0.0 1379.8 jit_solution(3245404687226244780)
XLA Ops:
  12.2 8.9 copy.57
  21.1 5.8 convolution_add_fusion
  35.9 8.3 psum.84
  56.5 51.9 %all-reduce.21.cloned.1.call-done = f32[256,2048]{1,0:T(8,128)} async-done(((f32[256,2048]{1,0:T(8,128)}), f32[256,2048]{1,0:T(8,128)}) %all-reduce.21.cloned.1.call-update) | async-done | bytes 2097168 | tf_op jit(solution)/shard_map/psum | solution.py:80
  111.1 10.9 fusion.61
  122.0 5.8 psum.87
  129.8 5.8 psum.88
  135.6 8.4 multiply_reduce_fusion
  144.0 6.4 all-reduce.15
  156.0 7.1 fusion.67
  164.7 7.8 fusion.57
  173.3 41.9 %all-reduce.23.cloned.1.call-done = f32[256,2048]{1,0:T(8,128)} async-done(((f32[256,2048]{1,0:T(8,128)}), f32[256,2048]{1,0:T(8,128)}) %all-reduce.23.cloned.1.call-update) | async-done | bytes 2097168 | tf_op jit(solution)/shard_map/psum | solution.py:84
  222.7 6.0 all-reduce.14
  248.4 6.5 fusion.25
  256.5 9.5 fusion.56
  267.6 9.5 fusion.35
  281.3 62.2 %reduce-scatter.27.cloned.1.call-done = f32[16,16]{1,0:T(8,128)} async-done(((f32[128,16]{1,0:T(8,128)}), f32[16,16]{1,0:T(8,128)}) %reduce-scatter.27.cloned.1.call-update) | async-done | bytes 1040
  344.9 62.2 %reduce-scatter.29.cloned.1.call-done = f32[16,16]{1,0:T(8,128)} async-done(((f32[128,16]{1,0:T(8,128)}), f32[16,16]{1,0:T(8,128)}) %reduce-scatter.29.cloned.1.call-update) | async-done | bytes 1040
  408.6 85.5 %all-reduce.25.cloned.1.call-done = (f32[256,2048]{1,0:T(8,128)}, f32[256,2048]{1,0:T(8,128)}) async-done(((f32[256,2048]{1,0:T(8,128)}, f32[256,2048]{1,0:T(8,128)}), (f32[256,2048]{1,0:T(8,128)}, f32[256,2048]{1,0:T(8,128)})) %all-reduce.25.cloned.1.call-update) | async-done | bytes 4194320 | tf_op jit(solution)/shard_map/psum | solution.py:80
  500.6 40.7 %all-reduce.13 = (f32[2048]{0:T(1024)S(1)}, f32[2048]{0:T(1024)S(1)}, f32[3,8,64]{2,1,0:T(8,128)S(1)}, f32[8,64]{1,0:T(8,128)S(1)}, f32[8,64]{1,0:T(8,128)S(1)},...) all-reduce(f32[2048]{0:T(1024)S(1)} %get-tuple-element.79, ...), channel_id=2, replica_groups=mesh['batch'=8,'mp'=4] {'batch'}, use_global_device_ids=true, to_apply=%region_32.33.clone | all-reduce | flops 14848 | bytes 118784
  550.8 38.1 %reduce-scatter.19.cloned.1.call-done = f32[512,256]{1,0:T(8,128)} async-done(((f32[512,2048]{1,0:T(8,128)}), f32[512,256]{1,0:T(8,128)}) %reduce-scatter.19.cloned.1.call-update) | async-done | bytes 524304 | tf_op jit(solution)/shard_map/reduce_scatter | solution.py:272
  588.9 211.7 %reduce-scatter.17.cloned.1.call-done = f32[256,3,512]{2,0,1:T(8,128)} async-done(((f32[2048,3,512]{2,0,1:T(8,128)}), f32[256,3,512]{2,0,1:T(8,128)}) %reduce-scatter.17.cloned.1.call-update) | async-done | bytes 1572880 | tf_op jit(solution)/shard_map/reduce_scatter | solution.py:264
  800.6 285.4 %reduce-scatter.21.cloned.1.call-done = f32[256,2048]{1,0:T(8,128)} async-done(((f32[2048,2048]{1,0:T(8,128)}), f32[256,2048]{1,0:T(8,128)}) %reduce-scatter.21.cloned.1.call-update) | async-done | bytes 2097168 | tf_op jit(solution)/shard_map/reduce_scatter | solution.py:276
  1086.0 286.5 %reduce-scatter.23.cloned.1.call-done = f32[2048,256]{1,0:T(8,128)} async-done(((f32[2048,2048]{1,0:T(8,128)}), f32[2048,256]{1,0:T(8,128)}) %reduce-scatter.23.cloned.1.call-update) | async-done | bytes 2097168 | tf_op jit(solution)/shard_map/reduce_scatter | solution.py:286
  (271 shorter events, 89.5 us)
Async XLA Ops:
  7.2 46.0 %copy-start = (bf16[512,2048]{1,0:T(8,128)(2,1)S(1)}, bf16[512,2048]{1,0:T(8,128)(2,1)}, u32[]{:S(2)}) copy-start(bf16[512,2048]{1,0:T(8,128)(2,1)} %param.28) | copy-start | bytes 6291460
  7.2 101.1 %all-reduce.21.cloned.1.call-start = ((), (), s32[]{:S(2)}) async-start(), calls=%async_computation.7 | async-start | bytes 4194304 | tf_op jit(solution)/shard_map/psum | solution.py:80
  11.9 216.8 %copy-start.39 = (f32[512]{0:T(512)}, f32[512]{0:T(512)S(1)}, u32[]{:S(2)}) copy-start(f32[512]{0:T(512)S(1)} %mul.689) | copy-start | bytes 6148
  12.0 41.3 %copy-start.51 = (f32[512]{0:T(512)}, f32[512]{0:T(512)S(1)}, u32[]{:S(2)}) copy-start(f32[512]{0:T(512)S(1)} %add.243) | copy-start | bytes 6148
  44.3 184.3 %copy-start.35 = (f32[256]{0:T(256)}, f32[256]{0:T(256)S(1)}, u32[]{:S(2)}) copy-start(f32[256]{0:T(256)S(1)} %broadcast_multiply_fusion.6) | copy-start | bytes 3076
  51.2 177.5 %copy-start.43 = (f32[256]{0:T(256)}, f32[256]{0:T(256)S(1)}, u32[]{:S(2)}) copy-start(f32[256]{0:T(256)S(1)} %add_rsqrt_fusion.1) | copy-start | bytes 3076
  56.4 52.0 %copy-start.70 = (f32[2048]{0:T(1024)S(1)}, f32[2048]{0:T(1024)}, u32[]{:S(2)}) copy-start(f32[2048]{0:T(1024)} %param.29) | copy-start | bytes 24580
  56.4 158.9 %all-reduce.23.cloned.1.call-start = ((), (), s32[]{:S(2)}) async-start(), calls=%async_computation.8 | async-start | bytes 4194304 | tf_op jit(solution)/shard_map/psum | solution.py:84
  56.5 163.2 %copy-start.63 = (f32[256]{0:T(256)}, f32[256]{0:T(256)S(1)}, u32[]{:S(2)}) copy-start(f32[256]{0:T(256)S(1)} %fusion.51) | copy-start | bytes 3076
  110.4 108.6 %copy-start.47 = (f32[256]{0:T(256)}, f32[256]{0:T(256)S(1)}, u32[]{:S(2)}) copy-start(f32[256]{0:T(256)S(1)} %broadcast_multiply_fusion.5) | copy-start | bytes 3076
  111.1 107.8 %copy-start.57 = (f32[256]{0:T(256)}, f32[256]{0:T(256)S(1)}, u32[]{:S(2)}) copy-start(f32[256]{0:T(256)S(1)} %fusion.47) | copy-start | bytes 3076
  163.0 116.9 %reduce-scatter.25.cloned.1.call-start = ((), (), s32[]{:S(2)}) async-start(), calls=%async_computation.13 | async-start | bytes 73728
  163.9 179.7 %reduce-scatter.27.cloned.1.call-start = ((), (), s32[]{:S(2)}) async-start(), calls=%async_computation.14 | async-start | bytes 73728
  164.7 242.4 %reduce-scatter.29.cloned.1.call-start = ((), (), s32[]{:S(2)}) async-start(), calls=%async_computation.15 | async-start | bytes 73728
  173.3 320.9 %all-reduce.25.cloned.1.call-start = ((), (), s32[]{:S(2)}) async-start(), calls=%async_computation.16 | async-start | bytes 8388608 | tf_op jit(solution)/shard_map/psum | solution.py:80
  241.4 347.5 %reduce-scatter.19.cloned.1.call-start = ((), (), s32[]{:S(2)}) async-start(), calls=%async_computation.10 | async-start | bytes 4718592 | tf_op jit(solution)/shard_map/reduce_scatter | solution.py:272
  247.3 553.3 %reduce-scatter.17.cloned.1.call-start = ((), (), s32[]{:S(2)}) async-start(), calls=%async_computation.9 | async-start | bytes 14155776 | tf_op jit(solution)/shard_map/reduce_scatter | solution.py:264
  254.9 831.1 %reduce-scatter.21.cloned.1.call-start = ((), (), s32[]{:S(2)}) async-start(), calls=%async_computation.11 | async-start | bytes 18874368 | tf_op jit(solution)/shard_map/reduce_scatter | solution.py:276
  266.0 1106.5 %reduce-scatter.23.cloned.1.call-start = ((), (), s32[]{:S(2)}) async-start(), calls=%async_computation.12 | async-start | bytes 18874368 | tf_op jit(solution)/shard_map/reduce_scatter | solution.py:286
  277.1 131.3 %copy-start.77 = (f32[512]{0:T(512)S(1)}, f32[512]{0:T(512)}, u32[]{:S(2)}) copy-start(f32[512]{0:T(512)} %get-tuple-element.86) | copy-start | bytes 6148
  277.1 131.4 %copy-start.76 = (f32[512]{0:T(512)S(1)}, f32[512]{0:T(512)}, u32[]{:S(2)}) copy-start(f32[512]{0:T(512)} %get-tuple-element.91) | copy-start | bytes 6148
  277.2 219.3 %copy-start.69 = (f32[256]{0:T(256)S(1)}, f32[256]{0:T(256)}, u32[]{:S(2)}) copy-start(f32[256]{0:T(256)} %copy-done.68) | copy-start | bytes 3076
  498.3 48.8 %copy-start.75 = (f32[2048]{0:T(1024)S(1)}, f32[2048]{0:T(1024)}, u32[]{:S(2)}) copy-start(f32[2048]{0:T(1024)} %param.37) | copy-start | bytes 24580
  547.1 825.4 %copy-start.1 = (bf16[512,2048]{1,0:T(8,128)(2,1)S(1)}, bf16[512,2048]{1,0:T(8,128)(2,1)}, u32[]{:S(2)}) copy-start(bf16[512,2048]{1,0:T(8,128)(2,1)} %param.28) | copy-start | bytes 6291460
  (70 other events, 250.4 us)
Sparse Core Ops, SparseCore 0:
  56.5 51.7 all-reduce.20
  163.2 52.0 all-reduce.22
  218.6 61.2 reduce-scatter.24
  283.2 60.2 reduce-scatter.26
  346.8 60.2 reduce-scatter.28
  409.4 84.7 all-reduce.24
  498.8 90.0 reduce-scatter.18
  593.1 207.4 reduce-scatter.16
  805.0 281.0 reduce-scatter.20
  1090.7 281.7 reduce-scatter.22
where the time goes:
time: 1390 us; the launch traced here: 1380 us
  waiting for transfers between devices  1130 us (81%)
  matrix products  86 us (6%)
  blocking collectives  78.7 us (6%)
  local copies, waits for them, and re-layouts  40.3 us (3%)
  other arithmetic  30.7 us (2%)
  between operations  17.5 us (1%)
    reduce_scatter x1, waiting for transfers between devices, local(): lax.psum_scatter(grad_down_weight, 'batch', scatter_dimension=1, tiled=True)  286 us
    reduce_scatter x1, waiting for transfers between devices, local(): lax.psum_scatter(grad_up_weight, 'batch', scatter_dimension=0, tiled=True)  285 us
    reduce_scatter x1, waiting for transfers between devices, local(): lax.psum_scatter(grad_qkv_weight, 'batch', scatter_dimension=0, tiled=True)  212 us
    psum x2, waiting for transfers between devices, branch_total(): return lax.psum(partial_rows, 'mp')  137 us
    unnamed x13, waiting for transfers between devices  125 us
    psum x1, waiting for transfers between devices, input_total(): return lax.psum(partial_rows, 'mp')  41.9 us
    unnamed x1, blocking collectives  40.7 us
    reduce_scatter x1, waiting for transfers between devices, local(): lax.psum_scatter(grad_out_weight, 'batch', scatter_dimension=1, tiled=True)  38.1 us
  transfers between devices with their start and end apart: 10, of which 10 were waited for; matrix products, arithmetic and copies ran while one was open for 6% of the time, Pallas kernels for 0%

commit v1 on v0

v1 whole, which is shorter than its diff:
```python
import math

import jax
import jax.numpy as jnp
from jax import lax
from jax.sharding import PartitionSpec as P

D = 2048
HEADS = 32
HD = 64
FF = 8192

norm_eps = 1e-05
rope_base = 10000.0
xpos_base = 512.0
masked_score = -1e30
f32 = jnp.float32
bf16 = jnp.bfloat16
highest = lax.Precision.HIGHEST


def dot(a, b, dims):
    return lax.dot_general(a, b, (dims, ((), ())), preferred_element_type=f32)


def mm(a, b):
    return dot(a, b, ((1,), (0,)))


def mm_nt(a, b):
    return dot(a, b, ((1,), (1,)))


def mm_tn(a, b):
    return dot(a, b, ((0,), (0,)))


def norm_stats(values):
    mean = jnp.mean(values, axis=-1, keepdims=True)
    center = values - mean
    inverse = lax.rsqrt(jnp.mean(center * center, axis=-1, keepdims=True) + norm_eps)
    return center * inverse, inverse


def norm_back(grad, unit, inverse, gain):
    scaled = grad * gain
    return inverse * (
        scaled
        - jnp.mean(scaled, axis=-1, keepdims=True)
        - unit * jnp.mean(scaled * unit, axis=-1, keepdims=True)
    )


def hold(value):
    return lax.optimization_barrier(value)


def swap(axis, value, perm):
    return lax.ppermute(value, axis, perm)


def xpos_tables(places, head_width, center):
    half_width = head_width // 2
    pair_index = jnp.arange(half_width, dtype=f32)
    frequency = jnp.exp(-math.log(rope_base) * pair_index / half_width)
    angles = places[:, None] * frequency[None, :]
    zeta_base = (2.0 * pair_index + 0.4 * head_width) / (1.4 * head_width)
    powers = (places[:, None] - center) / xpos_base
    factor = jnp.exp(powers * jnp.log(zeta_base)[None, :])
    return (jnp.cos(angles), jnp.sin(angles), factor)


def turn(values, cosine, sine, factor):
    half = values.shape[-1] // 2
    one, two = values[..., :half], values[..., half:]
    c, s, e = cosine[:, None, :], sine[:, None, :], factor[:, None, :]
    return jnp.concatenate([(one * c - two * s) * e, (two * c + one * s) * e], axis=-1)


def turn_back(grads, cosine, sine, factor):
    half = grads.shape[-1] // 2
    c, s, e = cosine[:, None, :], sine[:, None, :], factor[:, None, :]
    one, two = grads[..., :half] * e, grads[..., half:] * e
    return jnp.concatenate([one * c + two * s, two * c - one * s], axis=-1)


def gelu_parts(values):
    cdf = 0.5 * (1.0 + lax.erf(values * (2.0**-0.5)))
    density = jnp.exp(-0.5 * values * values) * (1.0 / math.sqrt(2.0 * math.pi))
    return values * cdf, cdf + values * density


def make_local(nb, nm):
    pair = [(i, i ^ 1) for i in range(nm)]
    cross = [(i, i ^ 2) for i in range(nm)]
    full = nb == 8 and nm == 4
    zs = nb // 2

    def zx(moves):
        return [(s * 2 + x, d * 2 + x) for s, d in moves for x in range(2)]

    x_flip = [(i, i ^ 1) for i in range(nb)]
    z_flip = [(i, i ^ 2) for i in range(nb)]
    z_half = [(i, i ^ 4) for i in range(nb)]
    up = zx([(z, z + 1) for z in range(zs - 1)])
    down = zx([(z + 1, z) for z in range(zs - 1)])

    def local(
        tokens,
        lengths,
        cotangent,
        norm1_gain,
        norm1_shift,
        qkv_weight,
        qkv_bias,
        sub1_gain,
        sub1_shift,
        out_weight,
        out_bias,
        norm2_gain,
        norm2_shift,
        up_weight,
        up_bias,
        sub2_gain,
        sub2_shift,
        down_weight,
        down_bias,
    ):
        length = lengths[0]
        rows = tokens.shape[0]
        half = rows // 2
        width = out_weight.shape[0]
        heads = width // HD
        hidden = up_weight.shape[1]
        attn_width = width * nm
        ff_width = hidden * nm
        inv_root = 1.0 / math.sqrt(HD)
        block = D // nb
        index = lax.axis_index("batch")
        odd = lax.axis_index("mp") % 2

        def roll(value):
            return jnp.concatenate(
                [
                    lax.dynamic_slice_in_dim(value, odd * half, half, 0),
                    lax.dynamic_slice_in_dim(value, (1 - odd) * half, half, 0),
                ],
                axis=0,
            )

        def unroll(mine, other):
            return jnp.concatenate(
                [jnp.where(odd == 0, mine, other), jnp.where(odd == 0, other, mine)], axis=0
            )

        def reduce_half(value):
            total = value[:half] + swap("mp", value[half:], pair)
            return total + swap("mp", total, cross)

        def pair_join(value):
            return jnp.concatenate([value, swap("mp", value, pair)], axis=0)

        def mp_sum(value):
            value = value + swap("mp", value, pair)
            return value + swap("mp", value, cross)

        places = (jnp.arange(rows, dtype=jnp.int32) + odd * half) % rows
        keep = (places < length).astype(f32)[:, None]
        x = roll(tokens).astype(f32)
        dy = roll(cotangent).astype(f32) * keep
        dyl = dy.astype(bf16)

        one = jnp.where(length < 0, 2.0, 1.0).astype(f32)

        def narrow(value):
            return (value * one).astype(bf16)

        g1 = sub1_gain.reshape(width)
        c1 = sub1_shift.reshape(width)
        vecs = jnp.stack([g1, c1])
        own_vecs = lax.dot_general(
            vecs, out_weight.astype(f32), (((1,), (0,)), ((), ())), precision=highest
        )
        w_vecs = mp_sum(own_vecs)
        gain_out, shift_out = w_vecs[0], w_vecs[1]

        a_unit, a_inverse = norm_stats(x)
        a_wide = a_unit * norm1_gain + norm1_shift
        a = a_wide.astype(bf16)
        mixed = [
            mm(a, qkv_weight[:, j, :]) + qkv_bias[j].reshape(width) for j in range(3)
        ]
        cosine, sine, factor = xpos_tables(places.astype(f32), HD, rows // 2)
        q = turn(mixed[0].reshape(rows, heads, HD), cosine, sine, factor).astype(bf16)
        k = turn(mixed[1].reshape(rows, heads, HD), cosine, sine, 1.0 / factor).astype(bf16)
        v = mixed[2].reshape(rows, heads, HD).astype(bf16)
        allowed = (places[None, :] <= places[:, None]) & (places < length)[None, :]
        scores = jnp.einsum("qhd,khd->hqk", q, k, preferred_element_type=f32) * inv_root
        scores = jnp.where(allowed[None], scores, masked_score)
        peak = jnp.max(scores, axis=-1, keepdims=True)
        weights = jnp.exp(scores - peak)
        probs = weights / jnp.sum(weights, axis=-1, keepdims=True)
        probs_low = probs.astype(bf16)
        o = jnp.einsum("hqk,khd->qhd", probs_low, v, preferred_element_type=f32).reshape(
            rows, width
        )
        mean_loc = jnp.mean(o, axis=-1, keepdims=True)
        o_center = o - mean_loc
        stats = jnp.concatenate(
            [mean_loc, jnp.sum(o_center * o_center, axis=-1, keepdims=True)], axis=1
        )

        def flip(value):
            return jnp.concatenate([value[half:], value[:half]], axis=0)

        def join_o(stats, other, count):
            gap = stats[:, 0:1] - other[:, 0:1]
            return jnp.concatenate(
                [
                    0.5 * (stats[:, 0:1] + other[:, 0:1]),
                    stats[:, 1:2] + other[:, 1:2] + (0.5 * count) * gap * gap,
                ],
                axis=1,
            )

        stats = join_o(stats, swap("mp", flip(stats), pair), width)
        stats = join_o(stats, swap("mp", stats, cross), 2 * width)
        mu1 = stats[:, 0:1]
        inv1 = lax.rsqrt(stats[:, 1:2] / attn_width + norm_eps)
        partial = mm((o_center * g1).astype(bf16), out_weight) + mean_loc * own_vecs[0]
        branch = inv1[:half] * (reduce_half(partial) - mu1[:half] * gain_out)
        h1 = x[:half] + (branch + shift_out) + out_bias
        z_unit = (o - mu1) * inv1
        z_wide = z_unit * g1 + c1
        z = z_wide.astype(bf16)
        b_unit, b_inverse = norm_stats(h1)
        b_half = b_unit * norm2_gain + norm2_shift

        def first_pass(b_rows, dyl_rows):
            u = mm(b_rows, up_weight) + up_bias
            g, slope = gelu_parts(u)
            dw = mm_nt(dyl_rows, down_weight)
            scaled = dw * sub2_gain
            mean = jnp.mean(g, axis=-1)
            center = g - mean[:, None]
            stats = jnp.stack(
                [
                    mean,
                    jnp.sum(center * center, axis=-1),
                    jnp.sum(scaled, axis=-1),
                    jnp.sum(scaled * center, axis=-1),
                ]
            )
            return g, slope, dw, stats

        def join_g(one, two, count):
            mean = 0.5 * (one[0] + two[0])
            gap = one[0] - two[0]
            return jnp.stack(
                [
                    mean,
                    one[1] + two[1] + (0.5 * count) * gap * gap,
                    one[2] + two[2],
                    one[3] + two[3] + one[2] * (one[0] - mean) + two[2] * (two[0] - mean),
                ]
            )

        def all_stats(stats):
            turned = stats.reshape(4, -1, 2, half)[:, :, ::-1, :].reshape(stats.shape)
            stats = join_g(stats, swap("mp", turned, pair), hidden)
            return join_g(stats, swap("mp", stats, cross), 2 * hidden)

        def second_pass(g, slope, dw, stats):
            inverse = lax.rsqrt(stats[1] / ff_width + norm_eps)[:, None]
            unit = (g - stats[0][:, None]) * inverse
            w = (unit * sub2_gain + sub2_shift).astype(bf16)
            dg = inverse * (
                dw * sub2_gain
                - stats[2][:, None] / ff_width
                - unit * (inverse * (stats[3][:, None] / ff_width))
            )
            du = (dg * slope).astype(bf16)
            return w, du, jnp.sum(dw * unit, axis=0), jnp.sum(dw, axis=0)

        def gather_rows(mine):
            near_x = swap("batch", mine, x_flip)
            u0 = swap("batch", mine, up)
            d0 = swap("batch", mine, down)
            at = index // 2
            got_a = jnp.where(at == 0, d0, u0)
            far_a = swap("batch", got_a, x_flip)
            u1 = swap("batch", u0, [p for p in up if p[0] >= 2])
            d1 = swap("batch", d0, [p for p in down if p[0] < 2 * zs - 2])
            got_b = jnp.where(at >= 2, u1, d1)
            far_b = swap("batch", got_b, x_flip)
            u2 = swap("batch", u1, [p for p in up if p[0] >= 4])
            d2 = swap("batch", d1, [p for p in down if p[0] < 2 * zs - 4])
            got_c = jnp.where(at == 0, d2, jnp.where(at == 3, u2, d0))
            far_c = swap("batch", got_c, x_flip)
            parts = []
            for piece in (near_x, got_a, far_a, got_b, far_b, got_c, far_c):
                parts += [piece, swap("mp", piece, pair)]
            return narrow(jnp.concatenate(parts, axis=0))

        if full:
            dyl_far = gather_rows(dy[:half])
            b_far = gather_rows(b_half)
        b = narrow(pair_join(b_half))
        g, slope, dw, stats = first_pass(b, dyl)
        w, du, sub2_gain_sum, sub2_shift_sum = second_pass(g, slope, dw, all_stats(stats))

        db = reduce_half(mm_nt(du, up_weight))
        dh1_half = dy[:half] + norm_back(db, b_unit, b_inverse, norm2_gain)
        sums = [
            jnp.sum(db * b_unit, axis=0),
            jnp.sum(db, axis=0),
            jnp.sum(dh1_half, axis=0),
        ]
        dhl_half = dh1_half.astype(bf16).astype(f32)
        row_sums = pair_join(
            jnp.concatenate(
                [
                    jnp.sum(dhl_half * gain_out, axis=-1, keepdims=True),
                    jnp.sum(dhl_half * branch, axis=-1, keepdims=True),
                ],
                axis=1,
            )
        )
        dh1 = pair_join(dh1_half)
        dhl = narrow(dh1)
        dz = mm_nt(dhl, out_weight)
        do = inv1 * (
            dz * g1
            - row_sums[:, 0:1] / attn_width
            - z_unit * (row_sums[:, 1:2] / attn_width)
        )
        sub1_gain_sum = jnp.sum(dz * z_unit, axis=0)
        sub1_shift_sum = jnp.sum(dz, axis=0)
        do = do.astype(bf16).reshape(rows, heads, HD)

        dprobs = jnp.einsum("qhd,khd->hqk", do, v, preferred_element_type=f32)
        dv = jnp.einsum("hqk,qhd->khd", probs_low, do, preferred_element_type=f32)
        inner = jnp.sum(probs * dprobs, axis=-1, keepdims=True)
        dscores = (probs * (dprobs - inner)).astype(bf16)
        dq = jnp.einsum("hqk,khd->qhd", dscores, k, preferred_element_type=f32) * inv_root
        dk = jnp.einsum("hqk,qhd->khd", dscores, q, preferred_element_type=f32) * inv_root
        dm = [
            turn_back(dq, cosine, sine, factor).reshape(rows, width),
            turn_back(dk, cosine, sine, 1.0 / factor).reshape(rows, width),
            dv.reshape(rows, width),
        ]
        dm_low = [member.astype(bf16) for member in dm]
        bias_sum = jnp.concatenate([jnp.sum(member.astype(f32), axis=0) for member in dm_low])
        da = reduce_half(sum(mm_nt(dm_low[j], qkv_weight[:, j, :]) for j in range(3)))
        sums += [jnp.sum(da * a_unit[:half], axis=0), jnp.sum(da, axis=0)]
        tokens_half = dh1_half + norm_back(da, a_unit[:half], a_inverse[:half], norm1_gain)
        tokens_grad = narrow(unroll(tokens_half, swap("mp", tokens_half, pair)))

        result_half = h1 + reduce_half(mm(w, down_weight)) + down_bias
        result = narrow(unroll(result_half, swap("mp", result_half, pair)))

        lanes = hidden // 128
        d_sums = jnp.stack(sums)
        d_sums = d_sums + swap("mp", d_sums, pair)
        h_sums = jnp.concatenate([sub1_gain_sum, sub1_shift_sum, bias_sum])
        if not full:

            def scatter(value, axis):
                return lax.psum_scatter(value, "batch", scatter_dimension=axis, tiled=True)

            d_sums = scatter(d_sums, 1)
            down_bias_sum = scatter(jnp.sum(dy, axis=0), 0)
            h_sums = lax.psum(h_sums, "batch")
            wide = jnp.stack(
                [jnp.sum(du.astype(f32), axis=0), sub2_gain_sum, sub2_shift_sum]
            ).reshape(3, lanes, 128)
            wide = scatter(wide, 2)
            grad_qkv = scatter(jnp.stack([mm_tn(a, m) for m in dm_low], axis=1), 0)
            grad_out = scatter(mm_tn(z, dhl), 1)
            grad_up = scatter(mm_tn(b, du), 0)
            grad_down = scatter(mm_tn(w, dyl), 1)
        else:

            def column(value, at):
                return lax.dynamic_slice_in_dim(value, at * block, block, 1)

            for perm in (x_flip, z_flip, z_half):
                h_sums = h_sums + swap("batch", h_sums, perm)
                d_sums = d_sums + swap("batch", d_sums, perm)
            d_sums = column(d_sums, index)
            b_all = jnp.concatenate([b, b_far], axis=0)
            dyl_all = jnp.concatenate([dyl, dyl_far], axis=0)
            g2, slope2, dw2, stats2 = first_pass(b_far, dyl_far)
            w2, du2, gain2, shift2 = second_pass(g2, slope2, dw2, all_stats(stats2))
            w_all = jnp.concatenate([w, w2], axis=0)
            du_all = jnp.concatenate([du, du2], axis=0)
            wide = jnp.stack(
                [
                    jnp.sum(du_all.astype(f32), axis=0),
                    sub2_gain_sum + gain2,
                    sub2_shift_sum + shift2,
                ]
            ).reshape(3, lanes, 128)
            wide = lax.dynamic_slice_in_dim(wide, index * (128 // nb), 128 // nb, 2)
            dyl_mine = column(dyl_all, index)
            down_bias_sum = jnp.sum(dyl_mine.astype(f32), axis=0)
            grad_up = mm_tn(column(b_all, index), du_all)
            grad_down = mm_tn(w_all, dyl_mine)

            def square_rows(value):
                near = swap("batch", value, z_flip)
                return [value, swap("batch", value, x_flip), near, swap("batch", near, x_flip)]

            def square_pieces(value):
                def both(at):
                    return jnp.concatenate([column(value, at), column(value, at ^ 4)], axis=1)

                sent = jnp.concatenate(
                    [
                        swap("batch", both(index ^ s)[:half], [(i, i ^ s) for i in range(nb)])
                        for s in (1, 2, 3)
                    ],
                    axis=1,
                )
                other = swap("mp", sent, pair)
                out = [both(index)]
                for s in range(3):
                    cols = slice(s * 2 * block, (s + 1) * 2 * block)
                    out += [sent[:, cols], other[:, cols]]
                return narrow(jnp.concatenate(out, axis=0))

            a_sq = square_pieces(a_wide)
            z_sq = narrow(jnp.concatenate(square_rows(z_wide), axis=0))
            dhl_sq = square_pieces(dh1)
            grad_out = mm_tn(z_sq, dhl_sq[:, :block]) + swap(
                "batch", mm_tn(z_sq, dhl_sq[:, block:]), z_half
            )
            grads = []
            for j in (2, 0, 1):
                m_sq = narrow(jnp.concatenate(square_rows(dm[j]), axis=0))
                grads.append(
                    mm_tn(a_sq[:, :block], m_sq)
                    + swap("batch", mm_tn(a_sq[:, block:], m_sq), z_half)
                )
            grad_qkv = jnp.stack([grads[1], grads[2], grads[0]], axis=1)
        per = HD // nb

        def own_part(value, shape):
            return lax.dynamic_slice_in_dim(value.reshape(shape), index * per, per, len(shape) - 1)

        return (
            result,
            tokens_grad,
            d_sums[3],
            d_sums[4],
            grad_qkv,
            own_part(h_sums[2 * width :], (3, heads, HD)),
            own_part(h_sums[:width], (heads, HD)),
            own_part(h_sums[width : 2 * width], (heads, HD)),
            grad_out,
            d_sums[2],
            d_sums[0],
            d_sums[1],
            grad_up,
            wide[0],
            wide[1],
            wide[2],
            grad_down,
            down_bias_sum,
        )

    return local


def solution(mesh):
    in_specs = (
        P("batch", None),
        P("batch"),
        P("batch", None),
        P(),
        P(),
        P(None, None, "mp"),
        P(None, "mp", None),
        P("mp", None),
        P("mp", None),
        P("mp", None),
        P(),
        P(),
        P(),
        P(None, "mp"),
        P("mp"),
        P("mp"),
        P("mp"),
        P("mp", None),
        P(),
    )
    out_specs = (
        P("batch", None),
        P("batch", None),
        P("batch"),
        P("batch"),
        P("batch", None, "mp"),
        P(None, "mp", "batch"),
        P("mp", "batch"),
        P("mp", "batch"),
        P("mp", "batch"),
        P("batch"),
        P("batch"),
        P("batch"),
        P("batch", "mp"),
        P("mp", "batch"),
        P("mp", "batch"),
        P("mp", "batch"),
        P("mp", "batch"),
        P("batch"),
    )
    local = make_local(mesh.shape["batch"], mesh.shape["mp"])
    return jax.shard_map(local, mesh=mesh, in_specs=in_specs, out_specs=out_specs, check_vma=False)
```

time: 1390 us -> 662 us (0.48)
  waiting for transfers between devices: 1130 us -> 265 us
  starting transfers between devices: 0.67 us -> 87.7 us
  blocking collectives: 78.7 us -> 0 us
  other arithmetic: 30.7 us -> 102 us
  matrix products: 86 us -> 122 us
  local copies, waits for them, and re-layouts: 40.3 us -> 71.2 us
    reduce_scatter x4 -> x0, waiting for transfers between devices: 822 us -> none  [the longest x1 286 us: local(): lax.psum_scatter(grad_down_weight, 'batch', scatter_dimension=1, tiled=True)]
    ppermute x0 -> x86, waiting for transfers between devices: none -> 265 us  [swap(): return lax.ppermute(value, axis, perm)]
    psum x3 -> x0, waiting for transfers between devices: 179 us -> none  [the longest x2 137 us: branch_total(): return lax.psum(partial_rows, 'mp')]
    unnamed x13 -> x0, waiting for transfers between devices: 125 us -> none
    ppermute x0 -> x86, starting transfers between devices: none -> 87.7 us  [swap(): return lax.ppermute(value, axis, perm)]
    unnamed x1 -> x0, blocking collectives: 40.7 us -> none
    psum x6 -> x0, blocking collectives: 38 us -> none  [the longest x2 14.1 us: split_norm(): totals = lax.psum(jnp.sum(values, axis=-1), 'mp')]
    dot_general x18 -> x30, matrix products: 86 us -> 118 us  [the longest x24 111 us: dot(): return lax.dot_general(a, b, (dims, ((), ())), preferred_element_type=f32)]
  transfers between devices with their start and end apart: 10 -> 86, of which waited for: 10 -> 32; matrix products, arithmetic and copies ran while one was open for 6% -> 33% of each run, Pallas kernels for 0% -> 0%
where the time goes in v1:
time: 662 us; the launch traced here: 651 us
  waiting for transfers between devices  265 us (40%)
  matrix products  122 us (18%)
  other arithmetic  102 us (15%)
  starting transfers between devices  87.7 us (13%)
  local copies, waits for them, and re-layouts  71.2 us (11%)
    ppermute x86, waiting for transfers between devices, swap(): return lax.ppermute(value, axis, perm)  265 us
    dot_general x24, matrix products, dot(): return lax.dot_general(a, b, (dims, ((), ())), preferred_element_type=f32)  111 us
    ppermute x86, starting transfers between devices, swap(): return lax.ppermute(value, axis, perm)  87.7 us
    unnamed x295, local copies, waits for them, and re-layouts  43.7 us
    convert_element_type x7, other arithmetic, narrow(): return (value * one).astype(bf16)  28 us
    reduce_sum x2, other arithmetic, second_pass(): return (w, du, jnp.sum(dw * unit, axis=0), jnp.sum(dw, axis=0))  22.5 us
    unnamed x12, other arithmetic  15.2 us
  transfers between devices with their start and end apart: 86, of which 32 were waited for; matrix products, arithmetic and copies ran while one was open for 33% of the time, Pallas kernels for 0%

profile of v1, /device:TPU:0, one launch (start us, length us, event | category | flops | bytes accessed | tf_op | source)
XLA Modules:
  0.0 651.5 jit_solution(11488394824578006778)
XLA Ops:
  58.1 21.6 %collective-permute-done.5 = f32[2,2048]{1,0:T(2,128)S(1)} collective-permute-done((f32[2,2048]{1,0:T(2,128)S(1)}, f32[2,2048]{1,0:T(2,128)S(1)}, u32[]{:S(2)}, u32[]{:S(2)}) %collective-permute-start.5) | collective-permute-done | bytes 16416 | tf_op jit(solution)/shard_map/ppermute | solution.py:59
  99.0 7.9 %fusion.161 = (f32[256]{0:T(256)S(1)}, f32[256,2048]{1,0:T(8,128)S(1)}, f32[256,2048]{1,0:T(8,128)}) fusion(f32[2048]{0:T(1024)S(1)} %copy-done.96, bf16[256,2048]{1,0:T(8,128)(2,1)S(1)} %fusion.20, bf16[2048,2048]{1,0:T(8,128)(2,1)} %param.32), kind=kOutput, calls=%fused_computation.420 | convolution fusion | flops 2150629120 | bytes 13640704 | tf_op jit(solution)/shard_map/dot_general | solution.py:23
  129.4 6.5 %fusion.174 = f32[256,2048]{1,0:T(8,128)S(1)} fusion(bf16[256,2048]{1,0:T(8,128)(2,1)S(1)} %get-tuple-element.86, bf16[2048,2048]{1,0:T(8,128)(2,1)} %param.32), kind=kOutput, calls=%fused_computation.431 | convolution fusion | flops 2147483648 | bytes 11534336 | tf_op jit(solution)/shard_map/dot_general | solution.py:23
  152.3 17.7 %collective-permute-done.55 = f32[128,2048]{1,0:T(8,128)S(1)} collective-permute-done((f32[128,2048]{1,0:T(8,128)S(1)}, f32[128,2048]{1,0:T(8,128)S(1)}, u32[]{:S(2)}, u32[]{:S(2)}) %collective-permute-start.55) | collective-permute-done | bytes 1048608 | tf_op jit(solution)/shard_map/ppermute | solution.py:59
  174.0 20.5 %collective-permute-done.10 = f32[128,2048]{1,0:T(8,128)S(1)} collective-permute-done((f32[128,2048]{1,0:T(8,128)S(1)}, f32[128,2048]{1,0:T(8,128)S(1)}, u32[]{:S(2)}, u32[]{:S(2)}) %collective-permute-start.10) | collective-permute-done | bytes 1048608 | tf_op jit(solution)/shard_map/ppermute | solution.py:59
  236.7 22.2 %collective-permute-done.39 = f32[2560]{0:T(1024)S(1)} collective-permute-done((f32[2560]{0:T(1024)S(1)}, f32[2560]{0:T(1024)S(1)}, u32[]{:S(2)}, u32[]{:S(2)}) %collective-permute-start.39) | collective-permute-done | bytes 10272 | tf_op jit(solution)/shard_map/ppermute | solution.py:59
  289.5 10.0 %collective-permute-done.69 = f32[128,2048]{1,0:T(8,128)} collective-permute-done((f32[128,2048]{1,0:T(8,128)}, f32[128,2048]{1,0:T(8,128)}, u32[]{:S(2)}, u32[]{:S(2)}) %collective-permute-start.69) | collective-permute-done | bytes 1048608 | tf_op jit(solution)/shard_map/ppermute | solution.py:59
  306.0 6.8 %collective-permute-done.43 = f32[256,512]{1,0:T(8,128)S(1)} collective-permute-done((f32[256,512]{1,0:T(8,128)S(1)}, f32[256,512]{1,0:T(8,128)S(1)}, u32[]{:S(2)}, u32[]{:S(2)}) %collective-permute-start.43) | collective-permute-done | bytes 524320 | tf_op jit(solution)/shard_map/ppermute | solution.py:59
  317.9 6.1 collective-permute-done.36
  325.8 9.5 %collective-permute-done.32 = f32[256,512]{1,0:T(8,128)S(1)} collective-permute-done((f32[256,512]{1,0:T(8,128)S(1)}, f32[256,512]{1,0:T(8,128)S(1)}, u32[]{:S(2)}, u32[]{:S(2)}) %collective-permute-start.32) | collective-permute-done | bytes 524320 | tf_op jit(solution)/shard_map/ppermute | solution.py:59
  338.6 6.6 %collective-permute-done.28 = f32[256,512]{1,0:T(8,128)S(1)} collective-permute-done((f32[256,512]{1,0:T(8,128)S(1)}, f32[256,512]{1,0:T(8,128)S(1)}, u32[]{:S(2)}, u32[]{:S(2)}) %collective-permute-start.28) | collective-permute-done | bytes 524320 | tf_op jit(solution)/shard_map/ppermute | solution.py:59
  354.1 9.9 %collective-permute-done.33 = f32[256,512]{1,0:T(8,128)S(1)} collective-permute-done((f32[256,512]{1,0:T(8,128)S(1)}, f32[256,512]{1,0:T(8,128)S(1)}, u32[]{:S(2)}, u32[]{:S(2)}) %collective-permute-start.33) | collective-permute-done | bytes 524320 | tf_op jit(solution)/shard_map/ppermute | solution.py:59
  367.0 8.3 %collective-permute-done.27 = f32[256,512]{1,0:T(8,128)S(1)} collective-permute-done((f32[256,512]{1,0:T(8,128)S(1)}, f32[256,512]{1,0:T(8,128)S(1)}, u32[]{:S(2)}, u32[]{:S(2)}) %collective-permute-start.27) | collective-permute-done | bytes 524320 | tf_op jit(solution)/shard_map/ppermute | solution.py:59
  375.3 10.8 %collective-permute-done.29 = f32[256,512]{1,0:T(8,128)S(1)} collective-permute-done((f32[256,512]{1,0:T(8,128)S(1)}, f32[256,512]{1,0:T(8,128)S(1)}, u32[]{:S(2)}, u32[]{:S(2)}) %collective-permute-start.29) | collective-permute-done | bytes 524320 | tf_op jit(solution)/shard_map/ppermute | solution.py:59
  391.7 32.6 %collective-permute-done.49 = f32[512,256]{1,0:T(8,128)S(1)} collective-permute-done((f32[512,256]{1,0:T(8,128)S(1)}, f32[512,256]{1,0:T(8,128)S(1)}, u32[]{:S(2)}, u32[]{:S(2)}) %collective-permute-start.49) | collective-permute-done | bytes 524320 | tf_op jit(solution)/shard_map/ppermute | solution.py:59
  426.9 8.7 %collective-permute-done.34 = f32[256,512]{1,0:T(8,128)S(1)} collective-permute-done((f32[256,512]{1,0:T(8,128)S(1)}, f32[256,512]{1,0:T(8,128)S(1)}, u32[]{:S(2)}, u32[]{:S(2)}) %collective-permute-start.34) | collective-permute-done | bytes 524320 | tf_op jit(solution)/shard_map/ppermute | solution.py:59
  444.3 14.1 %collective-permute-done.17 = f32[128,2048]{1,0:T(8,128)S(1)} collective-permute-done((f32[128,2048]{1,0:T(8,128)S(1)}, f32[128,2048]{1,0:T(8,128)S(1)}, u32[]{:S(2)}, u32[]{:S(2)}) %collective-permute-start.17) | collective-permute-done | bytes 1048608 | tf_op jit(solution)/shard_map/ppermute | solution.py:59
  500.0 17.0 %collective-permute-done.77 = f32[128,2048]{1,0:T(8,128)S(1)} collective-permute-done((f32[128,2048]{1,0:T(8,128)S(1)}, f32[128,2048]{1,0:T(8,128)S(1)}, u32[]{:S(2)}, u32[]{:S(2)}) %collective-permute-start.77) | collective-permute-done | bytes 1048608 | tf_op jit(solution)/shard_map/ppermute | solution.py:59
  526.8 10.2 %multiply_convert_fusion.1 = bf16[1792,2048]{1,0:T(8,128)(2,1)} fusion(f32[1792,2048]{1,0:T(8,128)} %constant_dynamic-update-slice_fusion.7, f32[]{:T(128)S(6)} %select_n.161), kind=kLoop, calls=%fused_computation.16 | loop fusion | flops 7340032 | bytes 22020100 | tf_op jit(solution)/shard_map/convert_element_type | solution.py:176
  537.3 13.8 %collective-permute-done.82 = f32[128,2048]{1,0:T(8,128)S(1)} collective-permute-done((f32[128,2048]{1,0:T(8,128)}, f32[128,2048]{1,0:T(8,128)S(1)}, u32[]{:S(2)}, u32[]{:S(2)}) %collective-permute-start.82) | collective-permute-done | bytes 1048608 | tf_op jit(solution)/shard_map/ppermute | solution.py:59
  551.1 25.1 %fusion.158 = (f32[1792]{0:T(1024)S(1)}, f32[1792,2048]{1,0:T(8,128)}, f32[1792,2048]{1,0:T(8,128)}) fusion(f32[2048]{0:T(1024)S(1)} %copy-done.97, bf16[1792,2048]{1,0:T(8,128)(2,1)} %multiply_convert_fusion.1, bf16[2048,2048]{1,0:T(8,128)(2,1)} %param.32), kind=kOutput, calls=%fused_computation.419 | convolution fusion | flops 15054403584 | bytes 45104128 | tf_op jit(solution)/shard_map/dot_general | solution.py:23
  579.5 10.4 %multiply_convert_fusion = bf16[1792,2048]{1,0:T(8,128)(2,1)} fusion(f32[1792,2048]{1,0:T(8,128)} %constant_dynamic-update-slice_fusion.21, f32[]{:T(128)S(6)} %select_n.161), kind=kLoop, calls=%fused_computation.13 | loop fusion | flops 7340032 | bytes 22020100 | tf_op jit(solution)/shard_map/convert_element_type | solution.py:176
  589.9 27.8 %multiply_reduce_fusion.2 = (f32[1792]{0:T(1024)S(1)}, f32[1792]{0:T(1024)S(1)}, f32[1792]{0:T(1024)S(1)}, f32[2048]{0:T(1024)S(1)}, f32[1792,2048]{1,0:T(8,128)}) fusion(f32[1792,2048]{1,0:T(8,128)} %get-tuple-element.52, f32[1792]{0:T(1024)S(1)} %broadcast_multiply_fusion, f32[2048]{0:T(1024)S(1)} %copy-done.75, ...), kind=kOutput, calls=%fused_computation.14 | convolution fusion | flops 15061737472 | bytes 45133824 | tf_op jit(solution)/shard_map/dot_general | solution.py:23
  623.5 18.2 %multiply_reduce_fusion = (f32[2048]{0:T(1024)S(1)}, bf16[1792,2048]{1,0:T(8,128)(2,1)S(1)}, bf16[1792,2048]{1,0:T(8,128)(2,1)S(1)}) fusion(f32[1792,2048]{1,0:T(8,128)} %get-tuple-element.195, f32[1792,2048]{1,0:T(8,128)} %get-tuple-element.52, f32[1792]{0:T(1024)S(1)} %get-tuple-element.146, f32[1792]{0:T(1024)S(1)} %get-tuple-element.50, ...), kind=kLoop, calls=%fused_computation.10 | loop fusion | flops 84408320 | bytes 58781696 | tf_op jit(solution)/shard_map/reduce_sum | solution.py:283
  (635 shorter events, 305.3 us)
Async XLA Ops:
  3.3 53.8 %collective-permute-start.4 = (f32[2,2048]{1,0:T(2,128)S(1)}, f32[2,2048]{1,0:T(2,128)}, u32[]{:S(2)}, u32[]{:S(2)}) collective-permute-start(f32[2,2048]{1,0:T(2,128)S(1)} %fusion.113), channel_id=1, source_target_pairs={{0,1},{1,0},{2,3},{3,2},{4,5},{5,4},{6,7},{7,6},{8,9},{9,8},{10,11... | collective-permute-start | bytes 49160 | tf_op jit(solution)/shard_map/ppermute | solution.py:59
  44.7 35.1 %collective-permute-start.23 = (f32[128,512]{1,0:T(8,128)S(1)}, f32[128,512]{1,0:T(8,128)S(1)}, u32[]{:S(2)}, u32[]{:S(2)}) collective-permute-start(f32[128,512]{1,0:T(8,128)S(1)} %pad_maximum_fusion.14), channel_id=1, source_target_pairs={{0,4},{4,0},{8,12},{12,8},{16,20},{20,16},{24,28},{28,24},{1,5},{5... | collective-permute-start | bytes 786440 | tf_op jit(solution)/shard_map/ppermute | solution.py:59
  47.3 32.5 %collective-permute-start.25 = (f32[128,512]{1,0:T(8,128)S(1)}, f32[128,512]{1,0:T(8,128)S(1)}, u32[]{:S(2)}, u32[]{:S(2)}) collective-permute-start(f32[128,512]{1,0:T(8,128)S(1)} %pad_maximum_fusion.12), channel_id=1, source_target_pairs={{0,12},{4,8},{8,4},{12,0},{16,28},{20,24},{24,20},{28,16},{1,13},{... | collective-permute-start | bytes 786440 | tf_op jit(solution)/shard_map/ppermute | solution.py:59
  148.1 46.4 %collective-permute-start.10 = (f32[128,2048]{1,0:T(8,128)S(1)}, f32[128,2048]{1,0:T(8,128)S(1)}, u32[]{:S(2)}, u32[]{:S(2)}) collective-permute-start(f32[128,2048]{1,0:T(8,128)S(1)} %slice_add_fusion.2), channel_id=1, source_target_pairs={{0,2},{1,3},{2,0},{3,1},{4,6},{5,7},{6,4},{7,5},{8,10},{9,11},{10,... | collective-permute-start | bytes 3145736 | tf_op jit(solution)/shard_map/ppermute | solution.py:59
  151.6 50.4 %collective-permute-start.57 = (f32[128,2048]{1,0:T(8,128)S(1)}, f32[128,2048]{1,0:T(8,128)S(1)}, u32[]{:S(2)}, u32[]{:S(2)}) collective-permute-start(f32[128,2048]{1,0:T(8,128)S(1)} %collective-permute-done.53), channel_id=1, source_target_pairs={{8,16},{12,20},{16,24},{20,28},{9,17},{13,21},{17,25},{21,29},{10,... | collective-permute-start | bytes 3145736 | tf_op jit(solution)/shard_map/ppermute | solution.py:59
  170.0 32.0 %collective-permute-start.58 = (f32[128,2048]{1,0:T(8,128)S(1)}, f32[128,2048]{1,0:T(8,128)S(1)}, u32[]{:S(2)}, u32[]{:S(2)}) collective-permute-start(f32[128,2048]{1,0:T(8,128)S(1)} %collective-permute-done.52), channel_id=1, source_target_pairs={{8,0},{12,4},{16,8},{20,12},{9,1},{13,5},{17,9},{21,13},{10,2},{14... | collective-permute-start | bytes 3145736 | tf_op jit(solution)/shard_map/ppermute | solution.py:59
  199.3 33.7 %collective-permute-start.67 = (f32[128,2048]{1,0:T(8,128)}, f32[128,2048]{1,0:T(8,128)}, u32[]{:S(2)}, u32[]{:S(2)}) collective-permute-start(f32[128,2048]{1,0:T(8,128)} %get-tuple-element.88), channel_id=1, source_target_pairs={{0,4},{4,0},{8,12},{12,8},{16,20},{20,16},{24,28},{28,24},{1,5},{5... | collective-permute-start | bytes 3145736 | tf_op jit(solution)/shard_map/ppermute | solution.py:59
  204.0 80.5 %collective-permute-start.60 = (f32[128,2048]{1,0:T(8,128)}, f32[128,2048]{1,0:T(8,128)}, u32[]{:S(2)}, u32[]{:S(2)}) collective-permute-start(f32[128,2048]{1,0:T(8,128)} %get-tuple-element.56), channel_id=1, source_target_pairs={{0,4},{4,0},{8,12},{12,8},{16,20},{20,16},{24,28},{28,24},{1,5},{5... | collective-permute-start | bytes 3145736 | tf_op jit(solution)/shard_map/ppermute | solution.py:59
  204.5 77.2 %collective-permute-start.59 = (f32[128,2048]{1,0:T(8,128)}, f32[128,2048]{1,0:T(8,128)}, u32[]{:S(2)}, u32[]{:S(2)}) collective-permute-start(f32[128,2048]{1,0:T(8,128)} %get-tuple-element.56), channel_id=1, source_target_pairs={{0,1},{1,0},{2,3},{3,2},{4,5},{5,4},{6,7},{7,6},{8,9},{9,8},{10,11... | collective-permute-start | bytes 3145736 | tf_op jit(solution)/shard_map/ppermute | solution.py:59
  214.5 55.3 %collective-permute-start.47 = (f32[128,512]{1,0:T(8,128)}, f32[128,512]{1,0:T(8,128)}, u32[]{:S(2)}, u32[]{:S(2)}) collective-permute-start(f32[128,512]{1,0:T(8,128)} %pad_maximum_fusion.9), channel_id=1, source_target_pairs={{0,12},{4,8},{8,4},{12,0},{16,28},{20,24},{24,20},{28,16},{1,13},{... | collective-permute-start | bytes 786440 | tf_op jit(solution)/shard_map/ppermute | solution.py:59
  223.3 48.0 %collective-permute-start.45 = (f32[128,512]{1,0:T(8,128)}, f32[128,512]{1,0:T(8,128)}, u32[]{:S(2)}, u32[]{:S(2)}) collective-permute-start(f32[128,512]{1,0:T(8,128)} %pad_maximum_fusion.11), channel_id=1, source_target_pairs={{0,4},{4,0},{8,12},{12,8},{16,20},{20,16},{24,28},{28,24},{1,5},{5... | collective-permute-start | bytes 786440 | tf_op jit(solution)/shard_map/ppermute | solution.py:59
  281.7 31.1 %collective-permute-start.43 = (f32[256,512]{1,0:T(8,128)S(1)}, f32[256,512]{1,0:T(8,128)S(1)}, u32[]{:S(2)}, u32[]{:S(2)}) collective-permute-start(f32[256,512]{1,0:T(8,128)S(1)} %copy-done.117), channel_id=1, source_target_pairs={{0,8},{4,12},{8,0},{12,4},{16,24},{20,28},{24,16},{28,20},{1,9},{5... | collective-permute-start | bytes 1572872 | tf_op jit(solution)/shard_map/ppermute | solution.py:59
  304.4 33.4 %collective-permute-start.35 = (f32[256,512]{1,0:T(8,128)S(1)}, f32[256,512]{1,0:T(8,128)S(1)}, u32[]{:S(2)}, u32[]{:S(2)}) collective-permute-start(f32[256,512]{1,0:T(8,128)S(1)} %copy-done.54), channel_id=1, source_target_pairs={{0,4},{4,0},{8,12},{12,8},{16,20},{20,16},{24,28},{28,24},{1,5},{5... | collective-permute-start | bytes 1572872 | tf_op jit(solution)/shard_map/ppermute | solution.py:59
  337.8 103.2 %collective-permute-start.63 = (f32[128,2048]{1,0:T(8,128)S(1)}, f32[128,2048]{1,0:T(8,128)S(1)}, u32[]{:S(2)}, u32[]{:S(2)}) collective-permute-start(f32[128,2048]{1,0:T(8,128)S(1)} %copy-done.34), channel_id=1, source_target_pairs={{16,24},{20,28},{17,25},{21,29},{18,26},{22,30},{19,27},{23,31}} | collective-permute-start | bytes 3145736 | tf_op jit(solution)/shard_map/ppermute | solution.py:59
  346.8 39.4 %collective-permute-start.29 = (f32[256,512]{1,0:T(8,128)S(1)}, f32[256,512]{1,0:T(8,128)S(1)}, u32[]{:S(2)}, u32[]{:S(2)}) collective-permute-start(f32[256,512]{1,0:T(8,128)S(1)} %collective-permute-done.28), channel_id=1, source_target_pairs={{0,4},{4,0},{8,12},{12,8},{16,20},{20,16},{24,28},{28,24},{1,5},{5... | collective-permute-start | bytes 1572872 | tf_op jit(solution)/shard_map/ppermute | solution.py:59
  352.8 90.0 %collective-permute-start.62 = (f32[128,2048]{1,0:T(8,128)S(1)}, f32[128,2048]{1,0:T(8,128)S(1)}, u32[]{:S(2)}, u32[]{:S(2)}) collective-permute-start(f32[128,2048]{1,0:T(8,128)S(1)} %copy-done.32), channel_id=1, source_target_pairs={{8,0},{12,4},{9,1},{13,5},{10,2},{14,6},{11,3},{15,7}} | collective-permute-start | bytes 3145736 | tf_op jit(solution)/shard_map/ppermute | solution.py:59
  375.3 63.1 %collective-permute-start.61 = (f32[128,2048]{1,0:T(8,128)}, f32[128,2048]{1,0:T(8,128)S(1)}, u32[]{:S(2)}, u32[]{:S(2)}) collective-permute-start(f32[128,2048]{1,0:T(8,128)} %collective-permute-done.60), channel_id=1, source_target_pairs={{0,1},{1,0},{2,3},{3,2},{4,5},{5,4},{6,7},{7,6},{8,9},{9,8},{10,11... | collective-permute-start | bytes 3145736 | tf_op jit(solution)/shard_map/ppermute | solution.py:59
  386.1 38.2 %collective-permute-start.49 = (f32[512,256]{1,0:T(8,128)S(1)}, f32[512,256]{1,0:T(8,128)S(1)}, u32[]{:S(2)}, u32[]{:S(2)}) collective-permute-start(f32[512,256]{1,0:T(8,128)S(1)} %fusion.73), channel_id=1, source_target_pairs={{0,16},{4,20},{8,24},{12,28},{16,0},{20,4},{24,8},{28,12},{1,17},{... | collective-permute-start | bytes 1572872 | tf_op jit(solution)/shard_map/ppermute | solution.py:59
  389.9 45.7 %collective-permute-start.34 = (f32[256,512]{1,0:T(8,128)S(1)}, f32[256,512]{1,0:T(8,128)S(1)}, u32[]{:S(2)}, u32[]{:S(2)}) collective-permute-start(f32[256,512]{1,0:T(8,128)S(1)} %fusion.84), channel_id=1, source_target_pairs={{0,16},{4,20},{8,24},{12,28},{16,0},{20,4},{24,8},{28,12},{1,17},{... | collective-permute-start | bytes 1572872 | tf_op jit(solution)/shard_map/ppermute | solution.py:59
  424.3 48.5 %collective-permute-start.75 = (f32[128,2048]{1,0:T(8,128)}, f32[128,2048]{1,0:T(8,128)}, u32[]{:S(2)}, u32[]{:S(2)}) collective-permute-start(f32[128,2048]{1,0:T(8,128)} %collective-permute-done.69), channel_id=1, source_target_pairs={{8,0},{12,4},{16,8},{20,12},{9,1},{13,5},{17,9},{21,13},{10,2},{14... | collective-permute-start | bytes 3145736 | tf_op jit(solution)/shard_map/ppermute | solution.py:59
  440.9 32.5 %collective-permute-start.74 = (f32[128,2048]{1,0:T(8,128)}, f32[128,2048]{1,0:T(8,128)}, u32[]{:S(2)}, u32[]{:S(2)}) collective-permute-start(f32[128,2048]{1,0:T(8,128)} %collective-permute-done.70), channel_id=1, source_target_pairs={{8,16},{12,20},{16,24},{20,28},{9,17},{13,21},{17,25},{21,29},{10,... | collective-permute-start | bytes 3145736 | tf_op jit(solution)/shard_map/ppermute | solution.py:59
  481.7 35.2 %collective-permute-start.77 = (f32[128,2048]{1,0:T(8,128)S(1)}, f32[128,2048]{1,0:T(8,128)S(1)}, u32[]{:S(2)}, u32[]{:S(2)}) collective-permute-start(f32[128,2048]{1,0:T(8,128)S(1)} %get-tuple-element.62), channel_id=1, source_target_pairs={{0,4},{4,0},{8,12},{12,8},{16,20},{20,16},{24,28},{28,24},{1,5},{5... | collective-permute-start | bytes 3145736 | tf_op jit(solution)/shard_map/ppermute | solution.py:59
  490.9 31.6 %collective-permute-start.79 = (f32[128,2048]{1,0:T(8,128)}, f32[128,2048]{1,0:T(8,128)S(1)}, u32[]{:S(2)}, u32[]{:S(2)}) collective-permute-start(f32[128,2048]{1,0:T(8,128)} %collective-permute-done.75), channel_id=1, source_target_pairs={{8,0},{12,4},{9,1},{13,5},{10,2},{14,6},{11,3},{15,7}} | collective-permute-start | bytes 3145736 | tf_op jit(solution)/shard_map/ppermute | solution.py:59
  537.1 39.2 %collective-permute-start.81 = (f32[128,2048]{1,0:T(8,128)}, f32[128,2048]{1,0:T(8,128)S(1)}, u32[]{:S(2)}, u32[]{:S(2)}) collective-permute-start(f32[128,2048]{1,0:T(8,128)} %get-tuple-element.60), channel_id=1, source_target_pairs={{0,1},{1,0},{2,3},{3,2},{4,5},{5,4},{6,7},{7,6},{8,9},{9,8},{10,11... | collective-permute-start | bytes 3145736 | tf_op jit(solution)/shard_map/ppermute | solution.py:59
  (193 other events, 2479.5 us)

commit v2 on v0

v2 whole, which is shorter than its diff:
```python
import functools
import math

import jax
import jax.numpy as jnp
import numpy as np
from jax import lax
from jax.experimental import pallas as pl
from jax.experimental.pallas import tpu as pltpu
from jax.sharding import PartitionSpec as P

HD = 64
QUAD = 4 * HD
PAIR = 2 * HD

norm_eps = 1e-05
rope_base = 10000.0
xpos_base = 512.0
masked_score = -1e30
root_half = 2.0**-0.5
density_scale = 1.0 / math.sqrt(2.0 * math.pi)
f32 = jnp.float32
bf16 = jnp.bfloat16
MIB = 1 << 20


def dot(a, b, dims):
    return lax.dot_general(a, b, (dims, ((), ())), preferred_element_type=f32)


def mm(a, b):
    return dot(a, b, ((1,), (0,)))


def mm_nt(a, b):
    return dot(a, b, ((1,), (1,)))


def mm_tn(a, b):
    return dot(a, b, ((0,), (0,)))


def row_mean(value):
    return jnp.mean(value, axis=-1, keepdims=True)


def row_sum(value):
    return jnp.sum(value, axis=-1, keepdims=True)


def unit_rows(value):
    center = value - row_mean(value)
    inverse = lax.rsqrt(row_mean(center * center) + norm_eps)
    return center * inverse, inverse


def unit_back(grad, unit, inverse, gain):
    scaled = grad * gain
    return inverse * (scaled - row_mean(scaled) - unit * row_mean(scaled * unit))


def turn_tables(count):
    half = HD // 2
    places = np.arange(count, dtype=np.float64)[:, None]
    pair = np.arange(half, dtype=np.float64)[None, :]
    angles = places * rope_base ** (-2.0 * pair / HD)
    zeta = (2.0 * pair + 0.4 * HD) / (1.4 * HD)
    factor = zeta ** ((places - count // 2) / xpos_base)
    tables = []
    for scale in (factor, 1.0 / factor):
        tables.append(np.tile(np.cos(angles) * scale, (1, 4)))
        tables.append(np.tile(np.concatenate([-np.sin(angles), np.sin(angles)], 1), (1, 2))
                      * np.tile(scale, (1, 4)))
    return np.stack(tables).astype(np.float32)


def half_swap(value):
    lane = lax.broadcasted_iota(jnp.int32, value.shape, 1)
    return jnp.where(
        (lane & 32) == 0,
        pltpu.roll(value, value.shape[1] - 32, 1),
        pltpu.roll(value, 32, 1),
    )


def whole(shape):
    return pl.BlockSpec(shape, lambda *_: (0,) * len(shape))


def shape_of(shape, dtype=f32):
    return jax.ShapeDtypeStruct(shape, dtype)


def call(body, grid, ins, outs, shapes, scratch=(), tokens=0, aliases=None):
    count = len(ins)

    def kernel(meta, *refs):
        body(meta, *refs[:count], *refs[count + tokens :])

    return pl.pallas_call(
        kernel,
        grid_spec=pltpu.PrefetchScalarGridSpec(
            num_scalar_prefetch=1,
            grid=grid,
            in_specs=list(ins) + [pl.BlockSpec(memory_space=pl.ANY)] * tokens,
            out_specs=outs,
            scratch_shapes=list(scratch),
        ),
        out_shape=shapes,
        compiler_params=pltpu.CompilerParams(
            dimension_semantics=("arbitrary",) * len(grid), vmem_limit_bytes=64 * MIB
        ),
        input_output_aliases=aliases or {},
    )


class Order:
    def __init__(self, meta):
        self.meta = meta
        self.last = []

    def run(self, body, grid, ins, outs, shapes, args, scratch=(), wait=(), aliases=None):
        extra = list(wait) + self.last
        made = call(body, grid, ins, outs, shapes, scratch, len(extra), aliases)(
            self.meta, *args, *extra
        )
        self.last = [made[0] if isinstance(made, (list, tuple)) else made]
        return made


def half_at(meta, which, half):
    return pl.ds(pl.multiple_of(((meta[0] + which) % 2) * half, half), half)


def spread(ref, count, first=0):
    return jnp.concatenate([ref[pl.ds(first + i, 1), :] for i in range(count)], axis=1)


def mask_kernel(meta, cot_mine, cot_other, mine, other):
    size = mine.shape[0]
    tiles = pl.num_programs(0)
    for which, ref, out in ((0, cot_mine, mine), (1, cot_other, other)):
        first = (((meta[0] + which) % 2) * tiles + pl.program_id(0)) * size
        place = first + lax.broadcasted_iota(jnp.int32, (size, 1), 0)
        out[...] = ref[...].astype(f32) * jnp.where(place < meta[1], 1.0, 0.0)


def send_pieces(meta, first, second, outs, nb, block):
    for s, out in enumerate(outs):
        at = meta[2] ^ (s + 1)
        for part, where in ((0, at), (1, at ^ 4)):
            cols = pl.ds(pl.multiple_of(where * block, block), block)
            out[:, part * block : (part + 1) * block] = first[:, cols].astype(f32)
            out[:, (part + 2) * block : (part + 3) * block] = second[:, cols]


def flip_rows(value, half):
    return jnp.concatenate(
        [
            value[(i ^ 1) * half : ((i ^ 1) + 1) * half]
            for i in range(value.shape[0] // half)
        ],
        axis=0,
    )


def join_two(one, two, count):
    mean = 0.5 * (one[0] + two[0])
    gap = one[0] - two[0]
    joined = [mean, one[1] + two[1] + (0.5 * count) * gap * gap]
    if len(one) > 2:
        joined += [
            one[2] + two[2],
            one[3] + two[3] + one[2] * (one[0] - mean) + two[2] * (two[0] - mean),
        ]
    return joined


def join_all(ref, odd, count):
    cols = []
    for i in range(ref.shape[0]):
        value = ref[i]
        half = value.shape[0] // 2
        value = jnp.where(odd == i % 2, value, flip_rows(value, half))
        cols.append([value[:, c : c + 1] for c in range(4)])
    while len(cols) > 1:
        cols = [join_two(cols[i], cols[i + 1], count) for i in range(0, len(cols), 2)]
        count *= 2
    return cols[0]


def diagonal(count):
    return lax.broadcasted_iota(jnp.int32, (count, count), 0) == lax.broadcasted_iota(
        jnp.int32, (count, count), 1
    )


def as_row(column):
    return jnp.sum(jnp.where(diagonal(column.shape[0]), column, 0.0), axis=0, keepdims=True)


def as_column(row):
    return row_sum(jnp.where(diagonal(row.shape[1]), row, 0.0))


def attend_kernel(meta, tok, gain, shift, weight, bias, sub_gain, sub_shift, out_w, table,
                  a_out, q_out, k_out, v_out, p_out, o_out, y_mine, y_other,
                  a_low, o_all):
    rows, width = o_all.shape
    half = rows // 2
    step = pl.program_id(0)
    places = lax.broadcasted_iota(jnp.int32, (rows, 1), 0) ^ (meta[0] * half)
    keys = lax.broadcasted_iota(jnp.int32, (1, rows), 1) ^ (meta[0] * half)
    allowed = (keys <= places) & (keys < meta[1])

    @pl.when(step == 0)
    def _():
        for which in range(2):
            unit, _ = unit_rows(tok[half_at(meta, which, half), :].astype(f32))
            wide = unit * gain[...] + shift[...]
            a_low[which * half : (which + 1) * half, :] = wide.astype(bf16)
        a_out[...] = a_low[...]

    turned = []
    for j in range(3):
        m = mm(a_low[...], weight[j])
        m = m + jnp.concatenate(
            [bias[j, pl.ds(step * 4 + i, 1), :] for i in range(4)], axis=1
        )
        if j < 2:
            flipped = half_swap(m)
            parts = []
            for which in range(2):
                at = half_at(meta, which, half)
                here = slice(which * half, (which + 1) * half)
                c = jnp.concatenate([table[2 * j, at, :]] * 2, axis=1)
                s = jnp.concatenate([table[2 * j + 1, at, :]] * 2, axis=1)
                parts.append(m[here] * c + flipped[here] * s)
            m = jnp.concatenate(parts, axis=0)
        turned.append(m.astype(bf16))
    q, k, v = turned
    q = q * jnp.asarray(1.0 / math.sqrt(HD), bf16)
    q_out[...] = q
    k_out[...] = k
    v_out[...] = v
    lane = lax.broadcasted_iota(jnp.int32, (1, PAIR), 1)
    for p in range(2):
        here = slice(p * PAIR, (p + 1) * PAIR)
        total = None
        for h in range(2):
            mask = (lane // HD) == h
            scores = mm_nt(jnp.where(mask, q[:, here], jnp.zeros_like(q[:, here])), k[:, here])
            scores = jnp.where(allowed, scores, masked_score)
            weights = jnp.exp(scores - jnp.max(scores, axis=-1, keepdims=True))
            probs = weights / row_sum(weights)
            p_out[p * 2 + h] = probs
            part = mm(
                probs.astype(bf16), jnp.where(mask, v[:, here], jnp.zeros_like(v[:, here]))
            )
            total = part if total is None else total + part
        o_all[:, pl.ds(pl.multiple_of(step * QUAD + p * PAIR, PAIR), PAIR)] = total

    @pl.when(step == pl.num_programs(0) - 1)
    def _():
        o = o_all[...]
        o_out[...] = o
        mean = row_mean(o)
        center = o - mean
        stat_rows = jnp.concatenate([as_row(mean), as_row(row_sum(center * center))], axis=0)
        heads = width // HD
        gain_row, shift_row = spread(sub_gain, heads), spread(sub_shift, heads)
        pieces = []
        for row in (gain_row, shift_row):
            for _ in range(3):
                low = row.astype(bf16)
                pieces.append(low)
                row = row - low.astype(f32)
        vecs = mm(jnp.concatenate(pieces + [jnp.zeros((2, width), bf16)], axis=0), out_w[...])
        gain_out = vecs[0:1] + vecs[1:2] + vecs[2:3]
        shift_out = vecs[3:4] + vecs[4:5] + vecs[5:6]
        extra = jnp.concatenate([gain_out, shift_out, jnp.zeros((6, vecs.shape[1]), f32)], axis=0)
        low = (center * gain_row).astype(bf16)
        for which, out in ((1, y_other), (0, y_mine)):
            here = slice(which * half, (which + 1) * half)
            out[0:half, :] = mm(low[here], out_w[...]) + mean[here] * gain_out
            out[half : half + 8, :] = extra
            out[half + 2 : half + 4, 0:rows] = stat_rows


def stat_rows_of(ref):
    half = ref.shape[1] // 2
    return [ref[i : i + 1, :] for i in (2, 3)], [
        jnp.concatenate([ref[i : i + 1, half:], ref[i : i + 1, 0:half]], axis=1) for i in (2, 3)
    ]


def pair_kernel(width, meta, mine, other, out):
    half = out.shape[0] - 8
    rows = 2 * half
    out[...] = mine[...] + other[...]
    here, _ = stat_rows_of(mine.at[half : half + 8, 0:rows])
    _, there = stat_rows_of(other.at[half : half + 8, 0:rows])
    joined = join_two(here, there, width)
    out[half + 2 : half + 4, 0:rows] = jnp.concatenate(joined, axis=0)


def middle_kernel(attn_width, meta, one, two, one_extra, two_extra, tok, bias, gain, shift,
                   h_out, branch_out, b_out, vec_out, stats):
    size = h_out.shape[0]
    step = pl.program_id(0)

    @pl.when(step == 0)
    def _():
        rows = stats.shape[0]
        here, _ = stat_rows_of(one_extra.at[:, 0:rows])
        there, _ = stat_rows_of(two_extra.at[:, 0:rows])
        mean, m2 = join_two(here, there, attn_width // 2)
        inverse = lax.rsqrt(m2 * (1.0 / attn_width) + norm_eps)
        stats[...] = jnp.concatenate([as_column(mean), as_column(inverse)], axis=1)
        vec_out[...] = one_extra[...] + two_extra[...]

    at = pl.ds(pl.multiple_of(step * size, size), size)
    branch = stats[at, 1:2] * ((one[...] + two[...]) - stats[at, 0:1] * vec_out[0:1, :])
    branch_out[...] = branch
    h1 = tok[...].astype(f32) + (branch + vec_out[1:2, :]) + bias[...]
    h_out[...] = h1
    unit, _ = unit_rows(h1)
    b_out[...] = unit * gain[...] + shift[...]


def unit_kernel(meta, o_all, stats, sub_gain, sub_shift, z_out):
    heads = o_all.shape[1] // HD
    unit = (o_all[...] - stats[:, 0:1]) * stats[:, 1:2]
    z_out[...] = unit * spread(sub_gain, heads) + spread(sub_shift, heads)


def dw_kernel(meta, mine, other, weight, out, low):
    half = mine.shape[0]

    @pl.when(pl.program_id(0) == 0)
    def _():
        low[0:half, :] = mine[...].astype(bf16)
        low[half:, :] = other[...].astype(bf16)

    out[...] = mm_nt(low[...], weight[...]).astype(bf16)


def first_kernel(meta, mine, other, weight, bias, gain, dw, g_out, slope_out, stat_out, low,
                 mean_s, m2_s, s1_s, s2_s):
    half = mine.shape[0]
    step = pl.program_id(0)
    span = weight.shape[1]

    @pl.when(step == 0)
    def _():
        low[0:half, :] = mine[...].astype(bf16)
        low[half:, :] = other[...].astype(bf16)
        for ref in (mean_s, m2_s, s1_s, s2_s):
            ref[...] = jnp.zeros_like(ref)

    done = step.astype(f32)
    share = 1.0 / (done + 1.0)
    u = mm(low[...], weight[...]) + bias[...]
    cdf = 0.5 + 0.5 * lax.erf(u * root_half)
    density = jnp.exp(-0.5 * (u * u)) * density_scale
    g = u * cdf
    slope_out[...] = (cdf + u * density).astype(bf16)
    g_out[...] = g.astype(bf16)
    scaled = dw[...].astype(f32) * gain[...]
    mean_c = row_mean(g)
    center = g - mean_c
    s1_c = row_sum(scaled)
    s2_c = row_sum(scaled * center)
    gap = mean_c - mean_s[...]
    mean_new = mean_s[...] + gap * share
    m2_s[...] += row_sum(center * center) + gap * gap * (span * done * share)
    s2_s[...] += s2_c + s1_s[...] * (mean_s[...] - mean_new) + s1_c * (mean_c - mean_new)
    s1_s[...] += s1_c
    mean_s[...] = mean_new

    @pl.when(step == pl.num_programs(0) - 1)
    def _():
        stat_out[...] = jnp.concatenate([mean_s[...], m2_s[...], s1_s[...], s2_s[...]], axis=1)


def hidden_stats(ref, odd, out, count, ff_width):
    mean, m2, s1, s2 = join_all(ref, odd, count)
    inverse = lax.rsqrt(m2 * (1.0 / ff_width) + norm_eps)
    out[...] = jnp.concatenate(
        [mean, inverse, s1 * (1.0 / ff_width), inverse * s2 * (1.0 / ff_width)], axis=1
    )


def hidden_rows(g, slope, dw, stats, gain, shift):
    inverse = stats[:, 1:2]
    unit = (g.astype(f32) - stats[:, 0:1]) * inverse
    w = (unit * gain + shift).astype(bf16)
    dw = dw.astype(f32)
    dg = inverse * (dw * gain - stats[:, 2:3] - unit * stats[:, 3:4])
    return w, (dg * slope.astype(f32)).astype(bf16), dw * unit, dw


def back_kernel(ff_width, span, meta, g, slope, dw, parts, gain, shift, weight, w_out, du_out, stats,
                sum_out, db_mine, db_other):
    half = db_mine.shape[0]

    @pl.when(pl.program_id(0) == 0)
    def _():
        hidden_stats(parts, meta[0], stats, ff_width // parts.shape[0], ff_width)
        for c in range(g.shape[1] // span):
            at = slice(c * span, (c + 1) * span)
            w, du, gain_part, dw_wide = hidden_rows(
                g[:, at], slope[:, at], dw[:, at], stats[...], gain[:, at], shift[:, at]
            )
            w_out[:, at] = w
            du_out[:, at] = du
            sum_out[:, at] = hidden_sums(du, gain_part, dw_wide)

    part = mm_nt(du_out[...], weight[...])
    db_mine[...] = part[0:half, :]
    db_other[...] = part[half:, :]


def hidden_sums(du, gain_part, dw_wide):
    return jnp.concatenate(
        [
            jnp.sum(du.astype(f32), axis=0, keepdims=True),
            jnp.sum(gain_part, axis=0, keepdims=True),
            jnp.sum(dw_wide, axis=0, keepdims=True),
            jnp.zeros((5, du.shape[1]), f32),
        ],
        axis=0,
    )


def pack_kernel(meta, *refs):
    sources, (out, buffer, sems) = refs[:8], refs[8:]
    where = meta[2] // 2
    inner = (where == 1) | (where == 2)
    half = buffer.shape[1]

    def loads(first):
        return [
            pltpu.make_async_copy(sources[2 * i + first], buffer.at[i], sems.at[i])
            for i in range(4)
        ]

    @pl.when(inner)
    def _():
        for copy in loads(0):
            copy.start()

    @pl.when(jnp.logical_not(inner))
    def _():
        for copy in loads(1):
            copy.start()

    stores = []
    for i, copy in enumerate(loads(0)):
        copy.wait()
        store = pltpu.make_async_copy(
            buffer.at[i], out.at[i * half : (i + 1) * half, :], sems.at[4 + i]
        )
        store.start()
        stores.append(store)
    for store in stores:
        store.wait()


def far_kernel(starts, lower, own, meta, *refs):
    groups = len(starts)
    count = 1 + max(source for pair in starts for source, _ in pair)
    b_src, d_src, refs = refs[:count], refs[count : 2 * count], refs[2 * count :]
    stat_refs, rest = refs[: 2 * groups], refs[2 * groups :]
    up_w, up_b, gain, shift, down_w = rest[:5]
    rest = rest[5:]
    if own:
        w_own, du_own, sum_own, *cols = rest[:7]
        rest = rest[7:]
        ins = ()
    else:
        ins, rest = rest[:3], rest[3:]
    (up_out, down_out, near_out), (b_low, d_low, stats, buffer, sem) = rest[:3], rest[3:]
    half = buffer.shape[1]
    rows = 2 * half
    block = up_out.shape[0]
    where = meta[2] // 2
    inner = (where == 1) | (where == 2)
    mine = pl.ds(pl.multiple_of(meta[2] * block, block), block)
    near = pl.ds(pl.multiple_of((meta[2] ^ 1) * block, block), block)

    @pl.when(pl.program_id(0) == 0)
    def _():
        copies = []
        for n, pair in enumerate(starts):
            for k, (refs_k, low) in enumerate(((b_src, b_low), (d_src, d_low))):
                for i, (source, first) in enumerate(pair):
                    slot = 4 * n + 2 * k + i
                    copy = pltpu.make_async_copy(
                        refs_k[source].at[first + k * lower : first + k * lower + half, :], buffer.at[slot], sem.at[slot]
                    )
                    copy.start()
                    copies.append((copy, low, n * rows + i * half, slot))
        for n in range(groups):
            value = jnp.where(inner, stat_refs[2 * n][...], stat_refs[2 * n + 1][...])
            if lower == 0:
                value = jnp.where(meta[0] == 0, value, flip_rows(value, half))
            stats[n * rows : (n + 1) * rows, :] = value
        for copy, low, at, slot in copies:
            copy.wait()
            low[at : at + half, :] = buffer[slot].astype(bf16)

    for n in range(groups):
        at = slice(n * rows, (n + 1) * rows)
        u = mm(b_low[at, :], up_w[...]) + up_b[...]
        cdf = 0.5 + 0.5 * lax.erf(u * root_half)
        density = jnp.exp(-0.5 * (u * u)) * density_scale
        dw = mm_nt(d_low[at, :], down_w[...])
        w, du, gain_part, dw_wide = hidden_rows(
            u * cdf, cdf + u * density, dw, stats[at, :], gain[...], shift[...]
        )
        terms = [
            mm_tn(b_low[at, mine], du),
            mm_tn(d_low[at, mine], w),
            mm_tn(b_low[at, near], du),
            mm_tn(d_low[at, near], w),
            hidden_sums(du, gain_part, dw_wide),
        ]
        totals = terms if n == 0 else [t + s for t, s in zip(totals, terms)]
    if own:
        terms = [
            mm_tn(cols[0][...], du_own[...]),
            mm_tn(cols[2][...], w_own[...]),
            mm_tn(cols[1][...], du_own[...]),
            mm_tn(cols[3][...], w_own[...]),
            sum_own[...],
        ]
    else:
        low, high = ins[2][0:block, :], ins[2][block : 2 * block, :]
        terms = [ins[0][...], ins[1][...], low, high, ins[2][2 * block :, :]]
    totals = [t + s for t, s in zip(totals, terms)]
    up_out[...] = totals[0]
    down_out[...] = totals[1]
    near_out[0:block, :] = totals[2]
    near_out[block : 2 * block, :] = totals[3]
    near_out[2 * block :, :] = totals[4]


def norm2_kernel(meta, one, two, h1, dy, branch, vecs, gain, dh_out, sum_out):
    size, full = h1.shape
    db = one[...] + two[...]
    unit, inverse = unit_rows(h1[...])
    dh1 = dy[...] + unit_back(db, unit, inverse, gain[...])
    low = dh1.astype(bf16).astype(f32)
    dh_out[:, 0:full] = dh1
    lane = lax.broadcasted_iota(jnp.int32, (size, 128), 1)
    dh_out[:, full : full + 128] = jnp.where(
        lane == 0, row_sum(low * vecs[0:1]), row_sum(low * branch[...])
    )
    sums = jnp.concatenate(
        [
            jnp.sum(db * unit, axis=0, keepdims=True),
            jnp.sum(db, axis=0, keepdims=True),
            jnp.sum(dh1, axis=0, keepdims=True),
            jnp.sum(dy[...], axis=0, keepdims=True),
            jnp.zeros((4, full), f32),
        ],
        axis=0,
    )

    @pl.when(pl.program_id(0) == 0)
    def _():
        sum_out[...] = sums

    @pl.when(pl.program_id(0) > 0)
    def _():
        sum_out[...] += sums


def send_kernel(nb, meta, a_all, dh, *outs):
    send_pieces(meta, a_all, dh, outs, nb, a_all.shape[1] // nb)


def attend_back_kernel(attn_width, meta, dh_mine, dh_other, o_all, stats, sub_gain, out_w, q_all,
                       k_all, v_all, probs_all, table, dm_out, sum_out, dhl_out, do_all):
    rows, width = o_all.shape
    half = rows // 2
    full = out_w.shape[1]
    heads = width // HD
    step = pl.program_id(0)

    @pl.when(step == 0)
    def _():
        gain_row = spread(sub_gain, heads)
        dhl = jnp.concatenate(
            [dh_mine[:, 0:full].astype(bf16), dh_other[:, 0:full].astype(bf16)], axis=0
        )
        dhl_out[...] = dhl
        sums = jnp.concatenate([dh_mine[:, full:], dh_other[:, full:]], axis=0)
        dz = mm_nt(dhl, out_w[...])
        inverse = stats[:, 1:2]
        unit = (o_all[...] - stats[:, 0:1]) * inverse
        do = inverse * (
            dz * gain_row
            - sums[:, 0:1] * (1.0 / attn_width)
            - unit * (sums[:, 1:2] * (1.0 / attn_width))
        )
        do_all[...] = do.astype(bf16)
        sum_out[0:1, :] = jnp.sum(dz * unit, axis=0, keepdims=True)
        sum_out[1:2, :] = jnp.sum(dz, axis=0, keepdims=True)
        sum_out[5:8, :] = jnp.zeros((3, width), f32)

    quad = pl.ds(pl.multiple_of(step * QUAD, QUAD), QUAD)
    do = do_all[:, quad]
    q, k, v = q_all[...], k_all[...], v_all[...]
    lane = lax.broadcasted_iota(jnp.int32, (1, PAIR), 1)
    grads = [[], [], []]
    for p in range(2):
        here = slice(p * PAIR, (p + 1) * PAIR)
        total = [None] * 3
        for h in range(2):
            mask = (lane // HD) == h

            def only(value):
                return jnp.where(mask, value[:, here], jnp.zeros_like(value[:, here]))

            probs = probs_all[p * 2 + h]
            do_h = only(do)
            dprobs = mm_nt(do_h, v[:, here])
            inner = row_sum(probs * dprobs)
            dscores = (probs * (dprobs - inner)).astype(bf16)
            parts = (
                mm(dscores, only(k)),
                mm_tn(dscores, only(q)),
                mm_tn(probs.astype(bf16), do_h),
            )
            total = [part if t is None else t + part for t, part in zip(total, parts)]
        for j in range(3):
            grads[j].append(total[j])
    for j in range(3):
        grad = jnp.concatenate(grads[j], axis=1)
        if j == 0:
            grad = grad * (1.0 / math.sqrt(HD))
        if j < 2:
            flipped = half_swap(grad)
            parts = []
            for which in range(2):
                at = half_at(meta, which, half)
                here = slice(which * half, (which + 1) * half)
                c = jnp.concatenate([table[2 * j, at, :]] * 2, axis=1)
                s = jnp.concatenate([table[2 * j + 1, at, :]] * 2, axis=1)
                parts.append(grad[here] * c - flipped[here] * s)
            grad = jnp.concatenate(parts, axis=0)
        dm_out[:, pl.ds(pl.multiple_of(j * width + step * QUAD, QUAD), QUAD)] = grad
        sum_out[2 + j : 3 + j, quad] = jnp.sum(
            grad.astype(bf16).astype(f32), axis=0, keepdims=True
        )


def tail_kernel(meta, dm, weight, w, down_w, mine, other, low):
    half = mine.shape[0] // 2
    width = weight.shape[2]

    @pl.when(pl.program_id(0) == 0)
    def _():
        low[...] = dm[...].astype(bf16)

    total = mm_nt(low[:, 0:width], weight[0])
    for j in (1, 2):
        total = total + mm_nt(low[:, j * width : (j + 1) * width], weight[j])
    part = mm(w[...], down_w[...])
    mine[0:half, :] = total[0:half, :]
    mine[half:, :] = part[0:half, :]
    other[0:half, :] = total[half:, :]
    other[half:, :] = part[half:, :]


def norm1_kernel(meta, one, two, res_one, res_two, h1, tok, dh, gain, bias, sum_in, out, res_out,
                 sum_out):
    full = out.shape[1]
    da = one[...] + two[...]
    unit, inverse = unit_rows(tok[...].astype(f32))
    out[...] = dh[:, 0:full] + unit_back(da, unit, inverse, gain[...])
    res_out[...] = h1[...] + (res_one[...] + res_two[...]) + bias[...]
    sums = jnp.concatenate(
        [
            jnp.zeros((4, full), f32),
            jnp.sum(da * unit, axis=0, keepdims=True),
            jnp.sum(da, axis=0, keepdims=True),
            jnp.zeros((2, full), f32),
        ],
        axis=0,
    )

    @pl.when(pl.program_id(0) == 0)
    def _():
        sum_out[...] = sum_in[...] + sums

    @pl.when(pl.program_id(0) > 0)
    def _():
        sum_out[...] += sums


def place_kernel(meta, mine, other, out):
    tiles = pl.num_programs(0) // 2
    local = (pl.program_id(0) // tiles) == meta[0]
    out[...] = jnp.where(local, mine[...], other[...]).astype(bf16)


def add_kernel(count, meta, *refs):
    total = refs[0][...]
    for ref in refs[1:count]:
        total = total + ref[...]
    refs[count][...] = total


def square_kernel(nb, meta, a_all, dhl, *refs):
    pieces, sides, (own_out, mirror_out, a_low, d_low, right) = refs[:3], refs[3:11], refs[11:]
    rows, full = a_all.shape
    half, block = rows // 2, full // nb
    split = sides[0].shape[1]
    for part, at in ((0, meta[2]), (1, meta[2] ^ 4)):
        cols = pl.ds(pl.multiple_of(at * block, block), block)
        a_low[0:rows, part * block : (part + 1) * block] = a_all[:, cols]
        d_low[0:rows, part * block : (part + 1) * block] = dhl[:, cols]
    for s in range(4):
        at = rows * s
        if s > 0:
            for which in range(2):
                here = at + which * half
                rows_here = half_at(meta, which, half)
                a_low[here : here + half, :] = pieces[s - 1][rows_here, 0 : 2 * block].astype(bf16)
                d_low[here : here + half, :] = pieces[s - 1][rows_here, 2 * block :].astype(bf16)
        right[at : at + rows, 0:split] = sides[s][...].astype(bf16)
        right[at : at + rows, split:] = sides[4 + s][...].astype(bf16)
    for out, part in ((mirror_out, block), (own_out, 0)):
        out[:, 0:split] = mm_tn(a_low[:, part : part + block], right[:, 0:split])
        out[:, split:] = mm_tn(d_low[:, part : part + block], right[:, split:])


def final_square_kernel(meta, own, got, m_out, o_out):
    width = m_out.shape[2]
    for j in range(3):
        cols = slice(j * width, (j + 1) * width)
        m_out[j] = own[:, cols] + got[:, cols]
    o_out[...] = (own[:, 3 * width :] + got[:, 3 * width :]).T


def final_hidden_kernel(meta, up_own, up_got, down_own, down_got, up_out, down_out):
    up_out[...] = up_own[...] + up_got[...]
    down_out[...] = (down_own[...] + down_got[...]).T


def make_local(nb, nm):
    pair = [(i, i ^ 1) for i in range(nm)]
    cross = [(i, i ^ 2) for i in range(nm)]
    pairs = [[i, i + 1] for i in range(0, nm, 2)]
    full = nb == 8
    middle_link = [(2, 4), (3, 5), (4, 2), (5, 3)]
    outward_link = [(2, 0), (3, 1), (4, 6), (5, 7)]

    def to_core(value):
        return lax.ppermute(value, "mp", pair)

    def to_y(value):
        return lax.ppermute(value, "mp", cross)

    def to_batch(value, s):
        return lax.ppermute(value, "batch", [(i, i ^ s) for i in range(nb)])

    def to_middle(value):
        return lax.ppermute(value, "batch", middle_link)

    def outward(value):
        return lax.ppermute(value, "batch", outward_link)

    def local(
        tokens,
        lengths,
        cotangent,
        norm1_gain,
        norm1_shift,
        qkv_weight,
        qkv_bias,
        sub1_gain,
        sub1_shift,
        out_weight,
        out_bias,
        norm2_gain,
        norm2_shift,
        up_weight,
        up_bias,
        sub2_gain,
        sub2_shift,
        down_weight,
        down_bias,
    ):
        rows, D = tokens.shape
        half = rows // 2
        width = out_weight.shape[0]
        heads = width // HD
        hidden = up_weight.shape[1]
        attn_width = width * nm
        ff_width = hidden * nm
        block = D // nb
        span = 512
        chunks = hidden // span
        parts = D // span
        quads = heads // 4
        tiles = 4
        index = lax.axis_index("batch")
        meta = jnp.stack([lax.axis_index("mp") % 2, lengths[0], index]).astype(jnp.int32)
        always = lengths[0] >= 0
        table = jnp.asarray(turn_tables(rows))
        weight = jnp.transpose(qkv_weight, (1, 0, 2))

        def segment(stage):
            def skip():
                return jax.tree.map(
                    lambda s: jnp.zeros(s.shape, s.dtype), jax.eval_shape(stage)
                )

            return lax.cond(always, stage, skip)

        def meet(*values):
            return lax.optimization_barrier(values)

        def line(vec):
            return vec.reshape(1, -1)

        def rolled(step):
            return lambda i, *_: (0, i) if step == 1 else (i, 0)

        half_shape = shape_of((half, D))
        half_tile = pl.BlockSpec((half // tiles, D), rolled(0))
        tok_mine = pl.BlockSpec((half // tiles, D), lambda i, m: (m[0] * tiles + i, 0))
        tok_other = pl.BlockSpec((half // tiles, D), lambda i, m: ((1 - m[0]) * tiles + i, 0))
        ext_spec, ext_shape = whole((half + 8, D)), shape_of((half + 8, D))
        dh_spec, dh_shape = whole((half, D + 128)), shape_of((half, D + 128))
        dh_tile = pl.BlockSpec((half // tiles, D + 128), rolled(0))
        row_spec = whole((1, D))
        wide_spec, wide_shape = whole((rows, width)), shape_of((rows, width))
        quad = pl.BlockSpec((rows, QUAD), rolled(1))
        quad_weight = pl.BlockSpec((3, D, QUAD), lambda i, *_: (0, 0, i))
        probs_spec = pl.BlockSpec((4, rows, rows), lambda i, *_: (i, 0, 0))
        table_spec = whole((4, rows, PAIR))
        wide = pl.BlockSpec((1, span), rolled(1))
        tall = pl.BlockSpec((D, span), rolled(1))
        flat = pl.BlockSpec((span, D), rolled(0))
        half_part = pl.BlockSpec((half, span), rolled(1))
        many = pl.BlockSpec((rows, span), rolled(1))
        low_hidden = shape_of((rows, hidden), bf16)
        low_rows = shape_of((rows, D), bf16)
        tiny2, tiny4 = shape_of((rows, 2)), shape_of((rows, 4))
        tile = pl.BlockSpec((block, span), rolled(1))
        sum_tile = pl.BlockSpec((8, span), rolled(1))
        gain2, shift2, bias2 = line(sub2_gain), line(sub2_shift), line(up_bias)

        def add(order, *terms):
            shape = terms[0].shape
            tall_tile = pl.BlockSpec((shape[0] // tiles, shape[1]), rolled(0))
            return order.run(
                functools.partial(add_kernel, len(terms)),
                (tiles,),
                [tall_tile] * len(terms),
                tall_tile,
                shape_of(shape),
                terms,
            )

        def pair_join(value):
            return lax.all_gather(value, "mp", axis_index_groups=pairs, axis=0, tiled=True)

        dy, dy_other = Order(meta).run(
            mask_kernel, (tiles,), [tok_mine, tok_other], [half_tile] * 2, [half_shape] * 2,
            (cotangent, cotangent),
        )
        if full:
            dy_e1, dy_m1 = to_batch(dy, 2), to_middle(dy)

        def attention():
            order = Order(meta)
            low_shape = shape_of((rows, width), bf16)
            a, q, k, v, probs, o, y_mine, y_other = order.run(
                attend_kernel,
                (quads,),
                [whole((rows, D)), row_spec, row_spec, quad_weight, whole((3, heads, HD)),
                 whole((heads, HD)), whole((heads, HD)), whole((width, D)), table_spec],
                [whole((rows, D)), quad, quad, quad, probs_spec, wide_spec, ext_spec, ext_spec],
                [low_rows, low_shape, low_shape, low_shape,
                 shape_of((heads, rows, rows)), wide_shape, ext_shape, ext_shape],
                (tokens, line(norm1_gain), line(norm1_shift), weight, qkv_bias, sub1_gain,
                 sub1_shift, out_weight, table),
                [pltpu.VMEM((rows, D), bf16), pltpu.VMEM((rows, width), f32)],
            )
            y_pair = order.run(
                functools.partial(pair_kernel, width),
                (1,),
                [ext_spec] * 2,
                ext_spec,
                ext_shape,
                (y_mine, to_core(y_other)),
            )
            return a, q, k, v, probs, o, y_pair

        a, q, k, v, probs, o, y_pair = segment(attention)
        if full:
            dy_e1, dy_m1, y_pair = meet(dy_e1, dy_m1, y_pair)
            dy_f1, dy_m2 = outward(dy_m1), to_middle(dy_e1)

        def after_attention():
            order = Order(meta)
            y_cross = to_y(y_pair)
            dw, dyl = order.run(
                dw_kernel,
                (chunks,),
                [whole((half, D))] * 2 + [flat],
                [many, whole((rows, D))],
                [low_hidden, low_rows],
                (dy, dy_other, down_weight),
            )
            return dw, dyl, order.run(
                functools.partial(middle_kernel, attn_width),
                (tiles,),
                [half_tile, half_tile] + [pl.BlockSpec((8, D), lambda i, *_: (half // 8, 0))] * 2
                + [tok_mine] + [row_spec] * 3,
                [half_tile] * 3 + [whole((8, D)), whole((rows, 2))],
                [half_shape] * 3 + [shape_of((8, D)), tiny2],
                (y_pair, y_cross, y_pair, y_cross, tokens, line(out_bias), line(norm2_gain),
                 line(norm2_shift)),
            )

        dw, dyl, (h1, branch, b_mine, vecs, stats) = segment(after_attention)
        if full:
            dy_f1, dy_m2, b_mine = meet(dy_f1, dy_m2, b_mine)
            b_e1, b_m1 = to_batch(b_mine, 2), to_middle(b_mine)

        def hidden_first():
            order = Order(meta)
            dy_near = pair_join(dy_e1) if full else ()
            g, slope, stats_g, b = order.run(
                first_kernel,
                (chunks,),
                [whole((half, D))] * 2 + [tall, wide, wide, many],
                [many, many, whole((rows, 4)), whole((rows, D))],
                [low_hidden, low_hidden, tiny4, low_rows],
                (b_mine, to_core(b_mine), up_weight, bias2, gain2, dw),
                [pltpu.VMEM((rows, 1), f32)] * 4,
            )
            return g, slope, lax.all_gather(stats_g, "mp"), b, dy_near

        g, slope, g_stats, b, dy_near = segment(hidden_first)
        if full:
            b_e1, b_m1, g, dy_near = meet(b_e1, b_m1, g, dy_near)
            b_f1, b_m2 = outward(b_m1), to_middle(b_e1)

        def hidden_back():
            order = Order(meta)
            b_near = pair_join(b_e1) if full else ()
            w, du, st, h_sum, db_mine, db_other = order.run(
                functools.partial(back_kernel, ff_width, span),
                (parts,),
                [whole((rows, hidden))] * 3 + [whole((nm, rows, 4))]
                + [whole((1, hidden))] * 2 + [pl.BlockSpec((span, hidden), rolled(0))],
                [whole((rows, hidden))] * 2 + [whole((rows, 4)), whole((8, hidden))]
                + [half_part] * 2,
                [low_hidden, low_hidden, tiny4, shape_of((8, hidden)), half_shape, half_shape],
                (g, slope, dw, g_stats, gain2, shift2, up_weight),
            )
            return w, du, st, h_sum, add(order, db_mine, to_core(db_other)), b_near

        w, du, st, h_sum, db_pair, b_near = segment(hidden_back)
        if full:
            b_f1, b_m2, db_pair, b_near = meet(b_f1, b_m2, db_pair, b_near)
            st_near, st_far = to_batch(st, 2), (to_batch(st, 6), to_batch(st, 4))
            st_near, b_m2 = meet(st_near, b_m2)
            b_f2, dy_f2 = outward(b_m2), outward(dy_m2)

        def far_pass(order, b_src, d_src, starts, lower, stats_in, own, wait=()):
            size = len(starts) * rows
            cols = [
                pl.BlockSpec((rows, block), lambda i, m: (0, m[2])),
                pl.BlockSpec((rows, block), lambda i, m: (0, m[2] ^ 1)),
            ] * 2
            near_tile = pl.BlockSpec((2 * block + 8, span), rolled(1))
            fresh = own[0].dtype == bf16
            if fresh:
                w_own, du_own, sum_own, b_own, d_own = own
                tail = (w_own, du_own, sum_own, b_own, b_own, d_own, d_own)
                specs = [many, many, sum_tile] + cols
            else:
                tail, specs = tuple(own), [tile, tile, near_tile]
            count = 4 * len(starts)
            sources = (*b_src, *d_src)
            return order.run(
                functools.partial(far_kernel, starts, lower, fresh),
                (chunks,),
                [pl.BlockSpec(memory_space=pl.ANY)] * len(sources)
                + [whole((rows, 4))] * len(stats_in)
                + [tall, wide, wide, wide, flat]
                + specs,
                [tile, tile, near_tile],
                [shape_of((block, hidden))] * 2 + [shape_of((2 * block + 8, hidden))],
                (*sources, *stats_in, up_weight, bias2, gain2, shift2, down_weight, *tail),
                [pltpu.VMEM((size, D), bf16)] * 2
                + [pltpu.VMEM((size, 4), f32), pltpu.VMEM((count, half, D), f32),
                   pltpu.SemaphoreType.DMA((count,))],
                wait=wait,
                aliases={} if fresh else {
                    1 + len(sources) + len(stats_in) + 5 + i: i for i in range(3)},
            )

        def middle_norm_back():
            order = Order(meta)
            db_cross = to_y(db_pair)
            sums = ()
            if full:
                sums = far_pass(
                    order, [b_near], [dy_near], (((0, 0), (0, half)),), 0, (st_near, st_near),
                    (w, du, h_sum, b, dyl),
                )
            z = order.run(
                unit_kernel,
                (1,),
                [wide_spec, whole((rows, 2)), whole((heads, HD)), whole((heads, HD))],
                wide_spec,
                wide_shape,
                (o, stats, sub1_gain, sub1_shift),
            )
            dh_mine, d_sums = order.run(
                norm2_kernel,
                (tiles,),
                [half_tile] * 5 + [whole((8, D)), row_spec],
                [dh_tile, whole((8, D))],
                [dh_shape, shape_of((8, D))],
                (db_pair, db_cross, h1, dy, branch, vecs, line(norm2_gain)),
            )
            return dh_mine, d_sums, z, sums

        dh_mine, d_sums, z, sums = segment(middle_norm_back)
        if full:
            b_f2, dy_f2, st_far, dh_mine, z = meet(b_f2, dy_f2, st_far, dh_mine, z)
            z_x, z_z, z_d = to_batch(z, 1), to_batch(z, 2), to_batch(z, 3)

        def attention_back():
            order = Order(meta)
            dh_other = to_core(dh_mine)
            packed = ()
            if full:
                far = order.run(
                    pack_kernel,
                    (1,),
                    [pl.BlockSpec(memory_space=pl.ANY)] * 8,
                    pl.BlockSpec(memory_space=pl.ANY),
                    shape_of((2 * rows, D)),
                    (b_m1, b_f1, b_m2, b_f2, dy_m1, dy_f1, dy_m2, dy_f2),
                    [pltpu.VMEM((4, half, D), f32), pltpu.SemaphoreType.DMA((8,))],
                )
                packed = [far, to_core(far)]
            dm, h_sums, dhl = order.run(
                functools.partial(attend_back_kernel, attn_width),
                (quads,),
                [dh_spec, dh_spec, wide_spec, whole((rows, 2)), whole((heads, HD)),
                 whole((width, D)), quad, quad, quad, probs_spec, table_spec],
                [whole((rows, 3 * width)), whole((8, width)), whole((rows, D))],
                [shape_of((rows, 3 * width)), shape_of((8, width)), low_rows],
                (dh_mine, dh_other, o, stats, sub1_gain, out_weight, q, k, v, probs, table),
                [pltpu.VMEM((rows, width), bf16)],
            )
            sends = ()
            if full:
                sends = order.run(
                    functools.partial(send_kernel, nb),
                    (tiles,),
                    [half_tile, dh_tile],
                    [pl.BlockSpec((half // tiles, 4 * block), rolled(0))] * 3,
                    [shape_of((half, 4 * block))] * 3,
                    (a, dh_mine),
                )
            return packed, dm, h_sums, dhl, sends

        packed, dm, h_sums, dhl, sends = segment(attention_back)
        main = Order(meta)
        if full:
            z_x, z_z, z_d, dm, sends = meet(z_x, z_z, z_d, dm, sends)
            dm_x, dm_z = to_batch(dm, 1), to_batch(dm, 2)
            pieces = [to_batch(sends[s - 1], s) for s in (1, 2, 3)]
            sums = far_pass(
                main, packed, packed, (((0, 0), (1, 0)), ((0, half), (1, half))), rows,
                (st_far[0], st_far[1], st_far[1], st_far[0]), sums,
            )

        both = pl.BlockSpec((rows, span), rolled(1))
        tail_mine, tail_other = main.run(
            tail_kernel,
            (parts,),
            [whole((rows, 3 * width)), pl.BlockSpec((3, span, width), lambda i, *_: (0, i, 0)),
             whole((rows, hidden)), pl.BlockSpec((hidden, span), rolled(1))],
            [both] * 2,
            [shape_of((rows, D))] * 2,
            (dm, weight, w, down_weight),
            [pltpu.VMEM((rows, 3 * width), bf16)],
        )
        if full:
            dm_x, dm_z, pieces, sums, tail_other = meet(dm_x, dm_z, pieces, sums, tail_other)
            near_got, dm_d = to_batch(sums[2], 1), to_batch(dm_x, 2)

        def input_back():
            joined = [pair_join(piece) for piece in pieces] if full else ()
            return add(Order(meta), tail_mine, to_core(tail_other)), joined

        da_pair, pieces = segment(input_back)
        da_cross = to_y(da_pair)
        if full:
            da_pair, pieces = meet(da_pair, pieces)

            sides = [dm, dm_x, dm_z, dm_d, z, z_x, z_z, z_d]
            s_own, s_mirror = main.run(
                functools.partial(square_kernel, nb),
                (1,),
                [whole((rows, D))] * 2 + [whole((rows, 4 * block))] * 3
                + [whole((rows, 3 * width))] * 4 + [wide_spec] * 4,
                [whole((block, 4 * width))] * 2,
                [shape_of((block, 4 * width))] * 2,
                (a, dhl, *pieces, *sides),
                [pltpu.VMEM((4 * rows, 2 * block), bf16)] * 2
                + [pltpu.VMEM((4 * rows, 4 * width), bf16)],
            )
            s_got = to_batch(s_mirror, 4)

        main.last = [s_own] if full else []
        low_tile = pl.BlockSpec((half // tiles, D), lambda i, *_: (tiles + i, 0))
        t_mine, r_mine, d_sums = main.run(
            norm1_kernel,
            (tiles,),
            [half_tile, half_tile, low_tile, low_tile, half_tile, tok_mine, dh_tile, row_spec,
             row_spec, whole((8, D))],
            [half_tile, half_tile, whole((8, D))],
            [half_shape, half_shape, shape_of((8, D))],
            (da_pair, da_cross, da_pair, da_cross, h1, tokens, dh_mine, line(norm1_gain),
             line(down_bias), d_sums),
        )

        def place():
            order = Order(meta)
            sums = d_sums + to_core(d_sums)
            outs = [
                order.run(
                    place_kernel,
                    (2 * tiles,),
                    [pl.BlockSpec((half // tiles, D), lambda i, *_: (i % tiles, 0))] * 2,
                    pl.BlockSpec((half // tiles, D), rolled(0)),
                    low_rows,
                    (mine, to_core(mine)),
                )
                for mine in (r_mine, t_mine)
            ]
            return (*outs, sums)

        result, tokens_grad, d_sums = segment(place)

        def small_sums():
            comb = jnp.concatenate([d_sums, h_sums], axis=1)
            for s in (1, 2, 4):
                comb = comb + to_batch(comb, s)
            return comb

        lanes = hidden // 128
        per = 128 // nb
        if not full:

            def scatter(value, axis):
                return lax.psum_scatter(value, "batch", scatter_dimension=axis, tiled=True)

            d_sums = scatter(d_sums, 1)
            h_sums = lax.psum(h_sums, "batch")
            h_parts = scatter(h_sum[:3].reshape(3, lanes, 128), 2)
            dm_low = dm.astype(bf16)
            grad_qkv = scatter(
                jnp.stack([mm_tn(a, dm_low[:, j * width : (j + 1) * width]) for j in range(3)], 1), 0
            )
            grad_out = scatter(mm_tn(z.astype(bf16), dhl), 1)
            grad_up = scatter(mm_tn(b, du), 0)
            grad_down = scatter(mm_tn(w, dyl), 1)
        else:
            comb = segment(small_sums)
            d_sums = lax.dynamic_slice_in_dim(comb, index * block, block, 1)
            h_sums = comb[:, D:]
            h_parts = (sums[2][2 * block :] + near_got[2 * block :])[:3]
            h_parts = lax.dynamic_slice_in_dim(
                h_parts.reshape(3, lanes, 128), index * per, per, 2
            )
            main.last = [comb]
            cut = hidden // 4
            grad_up, grad_down = main.run(
                final_hidden_kernel,
                (4,),
                [pl.BlockSpec((block, cut), rolled(1))] * 3
                + [pl.BlockSpec((block, cut), lambda i, *_: (1, i))],
                [pl.BlockSpec((block, cut), rolled(1)), pl.BlockSpec((cut, block), rolled(0))],
                [shape_of((block, hidden)), shape_of((hidden, block))],
                (sums[0], near_got, sums[1], near_got),
            )
            grad_qkv, grad_out = main.run(
                final_square_kernel,
                (1,),
                [whole((block, 4 * width))] * 2,
                [whole((3, block, width)), whole((width, block))],
                [shape_of((3, block, width)), shape_of((width, block))],
                (s_own, s_got),
            )
            grad_qkv = jnp.transpose(grad_qkv, (1, 0, 2))
        per = HD // nb

        def own_part(value, shape):
            return lax.dynamic_slice_in_dim(value.reshape(shape), index * per, per, len(shape) - 1)

        return (
            result,
            tokens_grad,
            d_sums[4],
            d_sums[5],
            grad_qkv,
            own_part(h_sums[2:5], (3, heads, HD)),
            own_part(h_sums[0], (heads, HD)),
            own_part(h_sums[1], (heads, HD)),
            grad_out,
            d_sums[2],
            d_sums[0],
            d_sums[1],
            grad_up,
            h_parts[0],
            h_parts[1],
            h_parts[2],
            grad_down,
            d_sums[3],
        )

    return local


def solution(mesh):
    in_specs = (
        P("batch", None),
        P("batch"),
        P("batch", None),
        P(),
        P(),
        P(None, None, "mp"),
        P(None, "mp", None),
        P("mp", None),
        P("mp", None),
        P("mp", None),
        P(),
        P(),
        P(),
        P(None, "mp"),
        P("mp"),
        P("mp"),
        P("mp"),
        P("mp", None),
        P(),
    )
    out_specs = (
        P("batch", None),
        P("batch", None),
        P("batch"),
        P("batch"),
        P("batch", None, "mp"),
        P(None, "mp", "batch"),
        P("mp", "batch"),
        P("mp", "batch"),
        P("mp", "batch"),
        P("batch"),
        P("batch"),
        P("batch"),
        P("batch", "mp"),
        P("mp", "batch"),
        P("mp", "batch"),
        P("mp", "batch"),
        P("mp", "batch"),
        P("batch"),
    )
    local = make_local(mesh.shape["batch"], mesh.shape["mp"])
    return jax.shard_map(local, mesh=mesh, in_specs=in_specs, out_specs=out_specs, check_vma=False)
```

time: 1390 us -> 453 us (0.33)
  waiting for transfers between devices: 1130 us -> 179 us
  Pallas kernels: 0 us -> 183 us
  matrix products: 86 us -> 0 us
  blocking collectives: 78.7 us -> 8.84 us
  starting transfers between devices: 0.67 us -> 54 us
  local copies, waits for them, and re-layouts: 40.3 us -> 8.5 us
  other arithmetic: 30.7 us -> 2.95 us
    reduce_scatter x4 -> x0, waiting for transfers between devices: 822 us -> none  [the longest x1 286 us: local(): lax.psum_scatter(grad_down_weight, 'batch', scatter_dimension=1, tiled=True)]
    pallas_call x0 -> x23, Pallas kernels: none -> 183 us  [run(): call(body, grid, ins, outs, shapes, scratch, len(extra), aliases)]
    psum x3 -> x0, waiting for transfers between devices: 179 us -> none  [the longest x2 137 us: branch_total(): return lax.psum(partial_rows, 'mp')]
    ppermute x0 -> x39, waiting for transfers between devices: none -> 153 us  [the longest x19 61.1 us: to_batch(): return lax.ppermute(value, 'batch', [(i, i ^ s) for i in range(nb)])]
    unnamed x13 -> x0, waiting for transfers between devices: 125 us -> none
    dot_general x18 -> x0, matrix products: 86 us -> none  [the longest x1 10.9 us: local(): jnp.dot(normed2, up_weight, preferred_element_type=jnp.float32) + up_bias]
    ppermute x0 -> x39, starting transfers between devices: none -> 53.9 us  [the longest x19 36.4 us: to_batch(): return lax.ppermute(value, 'batch', [(i, i ^ s) for i in range(nb)])]
    unnamed x1 -> x0, blocking collectives: 40.7 us -> none
  transfers between devices with their start and end apart: 10 -> 44, of which waited for: 10 -> 21; matrix products, arithmetic and copies ran while one was open for 6% -> 2% of each run, Pallas kernels for 0% -> 39%
where the time goes in v2:
time: 453 us; the launch traced here: 451 us
  Pallas kernels  183 us (40%)
  waiting for transfers between devices  179 us (40%)
  starting transfers between devices  54 us (12%)
  between operations  14.6 us (3%)
  blocking collectives  8.84 us (2%)
  local copies, waits for them, and re-layouts  8.5 us (2%)
    pallas_call x23, Pallas kernels, run(): call(body, grid, ins, outs, shapes, scratch, len(extra), aliases)  183 us
    ppermute x19, waiting for transfers between devices, to_batch(): return lax.ppermute(value, 'batch', [(i, i ^ s) for i in range(nb)])  61.1 us
    ppermute x3, waiting for transfers between devices, to_y(): return lax.ppermute(value, 'mp', cross)  52.8 us
    ppermute x19, starting transfers between devices, to_batch(): return lax.ppermute(value, 'batch', [(i, i ^ s) for i in range(nb)])  36.4 us
    ppermute x9, waiting for transfers between devices, to_core(): return lax.ppermute(value, 'mp', pair)  24.3 us
    all_gather x5, waiting for transfers between devices, pair_join(): lax.all_gather(value, 'mp', axis_index_groups=pairs, axis=0, tiled=True)  22.7 us
    ppermute x4, waiting for transfers between devices, outward(): return lax.ppermute(value, 'batch', outward_link)  14.6 us
  transfers between devices with their start and end apart: 44, of which 21 were waited for; matrix products, arithmetic and copies ran while one was open for 2% of the time, Pallas kernels for 39%

profile of v2, /device:TPU:0, one launch (start us, length us, event | category | flops | bytes accessed | tf_op | source)
XLA Modules:
  0.0 450.7 jit_solution(12206710137795081437)
XLA Ops:
  17.4 18.9 %conditional.9 = (bf16[256,2048]{1,0:T(8,128)(2,1)}, bf16[256,512]{1,0:T(8,128)(2,1)}, bf16[256,512]{1,0:T(8,128)(2,1)}, bf16[256,512]{1,0:T(8,128)(2,1)}, f32[8...) conditional(s32[]{:T(128)} %bitcast.7, () %tuple.89, (f32[2048]{0:T(1024)}, f32[2048]{0:T(1024)}, ...), branch_computations={%region_0.1_spmd, %region_1.2_spmd} | conditional | bytes 5570636 | solution.py:823
  17.4 12.4 %branch_1_fun.16 = (bf16[256,2048]{1,0:T(8,128)(2,1)}, bf16[256,512]{1,0:T(8,128)(2,1)}, bf16[256,512]{1,0:T(8,128)(2,1)}, bf16[256,512]{1,0:T(8,128)(2,1)}, f32...) custom-call(s32[3]{0:T(128)} %get-tuple-element.182.meta, ...), custom_call_target="tpu_custom_call" | custom-call | tf_op jit(solution)/shard_map/cond/branch_1_fun/pallas_call | solution.py:124
  42.2 31.3 %conditional.10 = (bf16[256,2048]{1,0:T(8,128)(2,1)}, bf16[256,2048]{1,0:T(8,128)(2,1)}, f32[128,2048]{1,0:T(8,128)}, f32[128,2048]{1,0:T(8,128)}, f32[128,2048]...) conditional(s32[]{:T(128)} %bitcast.7, () %tuple.92, (s32[3]{0:T(128)}, f32[128,2048]{1,0:T(8,128)}, ...), branch_computations={%region_2.3_spmd, %region_3.4_spmd} | conditional | bytes 5310544 | solution.py:823
  51.6 16.6 %collective-permute-done.1.refs_1_.refs_3_ = f32[136,2048]{1,0:T(8,128)} collective-permute-done((f32[136,2048]{1,0:T(8,128)}, f32[136,2048]{1,0:T(8,128)}, u32[]{:S(2)}, u32[]{:S(2)}) %collective-permute-start.1) | collective-permute-done | bytes 1114144 | tf_op jit(solution)/shard_map/cond/branch_1_fun/ppermute | solution.py:766
  82.0 22.9 %conditional.11 = (bf16[256,2048]{1,0:T(8,128)(2,1)}, bf16[256,2048]{1,0:T(8,128)(2,1)}, f32[4,256,4]{2,1,0:T(8,128)}, bf16[256,2048]{1,0:T(8,128)(2,1)}, f32[256,2048]{1,0:T(8,128)}) conditional(s32[]{:T(128)} %bitcast.7, () %tuple.95, (f32[128,2048]{1,0:T(8,128)}, s32[3]{0:T(128)}, bf16[2048,2048]{1,0:T(8,128)(2,1)}, f32[1,2048]{1,0:T(1,128)}, ...), branch_computations={%region_4.5_spmd, %region_5.6_spmd} | conditional | bytes 13652088 | solution.py:823
  85.8 10.3 %branch_1_fun.20 = (bf16[256,2048]{1,0:T(8,128)(2,1)}, bf16[256,2048]{1,0:T(8,128)(2,1)}, f32[256,4]{1,0:T(8,128)}, bf16[256,2048]{1,0:T(8,128)(2,1)}) custom-call(s32[3]{0:T(128)} %get-tuple-element.219.meta, f32[128,2048]{1,0:T(8,128)} %get-tuple-element.220.refs_0_, f32[128,2048]{1,0:T(8,128)} %collective-permute-done.2.refs_1_, ...), custom_call_target="tpu_custom_call" | custom-call | tf_op jit(solution)/shard_map/cond/branch_1_fun/pallas_call | solution.py:124
  108.0 20.1 %conditional.12 = (bf16[256,2048]{1,0:T(8,128)(2,1)}, bf16[256,2048]{1,0:T(8,128)(2,1)}, f32[256,4]{1,0:T(8,128)}, f32[8,2048]{1,0:T(8,128)}, f32[128,2048]{1,0:T(8,128)}, /*index=5*/f32[256,2048]{1,0:T(8,128)}) conditional(s32[]{:T(128)} %bitcast.7, () %tuple.88, (s32[3]{0:T(128)}, bf16[256,2048]{1,0:T(8,128)(2,1)}, bf16[256,2048]{1,0:T(8,128)(2,1)}, ...), branch_computations={%region_6.7_spmd, %region_7.8_spmd} | conditional | bytes 13631616 | solution.py:823
  108.7 11.1 %branch_1_fun.21 = (bf16[256,2048]{1,0:T(8,128)(2,1)}, bf16[256,2048]{1,0:T(8,128)(2,1)}, f32[256,4]{1,0:T(8,128)}, f32[8,2048]{1,0:T(8,128)}, f32[128,2048]{1,0:T(8,128)}, /*index=5*/f32[128,2048]{1,0:T(8,128)}) custom-call(s32[3]{0:T(128)} %get-tuple-element.230.meta, bf16[256,2048]{1,0:T(8,128)(2,1)} %get-tuple-element.231.refs_0_, ...), custom_call_target="tpu_custom_call" | custom-call | tf_op jit(solution)/shard_map/cond/branch_1_fun/pallas_call | solution.py:124
  142.5 30.1 %conditional.13 = (f32[128,2176]{1,0:T(8,128)}, f32[8,2048]{1,0:T(8,128)}, f32[256,512]{1,0:T(8,128)}, f32[256,2048]{1,0:T(8,128)}, f32[256,2048]{1,0:T(8,128)}, /*index=5*/f32[520,2048]{1,0:T(8,128)}) conditional(s32[]{:T(128)} %bitcast.7, () %tuple.101, (f32[128,2048]{1,0:T(8,128)}, f32[2048]{0:T(1024)}, s32[3]{0:T(128)}, f32[256,2048]{1,0:T(8,128)}, ...), branch_computations={%region_8.9_spmd, %region_9.10_spmd} | conditional | bytes 10158152 | solution.py:823
  143.0 17.7 %branch_1_fun.23 = (f32[256,2048]{1,0:T(8,128)}, f32[256,2048]{1,0:T(8,128)}, f32[520,2048]{1,0:T(8,128)}) custom-call(s32[3]{0:T(128)} %get-tuple-element.245.meta, f32[256,2048]{1,0:T(8,128)} %get-tuple-element.256.refs_0_, f32[256,2048]{1,0:T(8,128)} %get-tuple-element.257.refs_1_, f32[256,4]{1,0:T(8,128)} %get-tuple-element.258.refs_2_.refs_3_, ...), custom_call_target="tpu_custom_call" | custom-call | tf_op jit(solution)/shard_map/cond/branch_1_fun/pallas_call | solution.py:124
  172.6 14.5 %collective-permute-done.23 = f32[128,2048]{1,0:T(8,128)} collective-permute-done((f32[128,2048]{1,0:T(8,128)}, f32[128,2048]{1,0:T(8,128)}, u32[]{:S(2)}, u32[]{:S(2)}) %collective-permute-start.23) | collective-permute-done | bytes 1048608 | tf_op jit(solution)/shard_map/ppermute | solution.py:775
  190.7 26.9 %conditional.14 = (f32[512,2048]{1,0:T(8,128)}, f32[512,2048]{1,0:T(8,128)}, f32[256,1536]{1,0:T(8,128)}, f32[8,512]{1,0:T(8,128)}, bf16[256,2048]{1,0:T(8,128)(...) conditional(s32[]{:T(128)} %bitcast.7, () %tuple.104, (s32[3]{0:T(128)}, ...), branch_computations={%region_10.11_spmd, %region_11.12_spmd} | conditional | bytes 21233808 | solution.py:823
  203.8 9.2 %branch_1_fun.27 = (f32[256,1536]{1,0:T(8,128)}, f32[8,512]{1,0:T(8,128)}, bf16[256,2048]{1,0:T(8,128)(2,1)}) custom-call(s32[3]{0:T(128)} %get-tuple-element.274.meta, f32[128,2176]{1,0:T(8,128)} %get-tuple-element.283.refs_0_.refs_1_, f32[128,2176]{1,0:T(8,128)} %collective-permute-done.6.refs_1_, f32[256,512]{1,0:T(8,128)} %get-tuple-element.284.refs_2_, ...), custom_call_target="tpu_custom_call" | custom-call | tf_op jit(solution)/shard_map/cond/branch_1_fun/pallas_call | solution.py:124
  222.7 24.6 %shard_map.336 = (f32[256,2048]{1,0:T(8,128)}, f32[256,2048]{1,0:T(8,128)}, f32[520,2048]{1,0:T(8,128)}) custom-call(s32[3]{0:T(128)} %pad_add_fusion.meta, f32[512,2048]{1,0:T(8,128)} %get-tuple-element.488.refs_0_.refs_2_, f32[512,2048]{1,0:T(8,128)} %get-tuple-element.489.refs_1_.refs_3_, ...), custom_call_target="tpu_custom_call", output_to_operand_aliasing={{0}: (14, {}), {1}: (15, {}), {2}: (16, {})} | custom-call | tf_op jit(solution)/shard_map/pallas_call | solution.py:124
  247.3 10.8 %shard_map.337 = (f32[256,2048]{1,0:T(8,128)}, f32[256,2048]{1,0:T(8,128)}) custom-call(s32[3]{0:T(128)} %pad_add_fusion.meta, f32[256,1536]{1,0:T(8,128)} %get-tuple-element.484.refs_0_.refs_5_, bf16[3,2048,512]{2,1,0:T(8,128)(2,1)} %bitcast.35, bf16[256,2048]{1,0:T(8,128)(2,1)} %get-tuple-element.457.refs_2_, bf16[2048,2048]{1,0:T(8,128)(2,1)} %refs_3_.1, ...), custom_call_target="tpu_custom_call" | custom-call | tf_op jit(solution)/shard_map/pallas_call | solution.py:124
  268.0 10.1 %collective-permute-done.34 = f32[128,1024]{1,0:T(8,128)} collective-permute-done((f32[128,1024]{1,0:T(8,128)}, f32[128,1024]{1,0:T(8,128)}, u32[]{:S(2)}, u32[]{:S(2)}) %collective-permute-start.34) | collective-permute-done | bytes 524320 | tf_op jit(solution)/shard_map/ppermute | solution.py:769
  279.9 33.0 %conditional.15 = (f32[256,2048]{1,0:T(8,128)}, f32[256,1024]{1,0:T(8,128)}, f32[256,1024]{1,0:T(8,128)}, f32[256,1024]{1,0:T(8,128)}) conditional(s32[]{:T(128)} %bitcast.7, () %tuple.87, (f32[256,2048]{1,0:T(8,128)}, s32[3]{0:T(128)}, f32[256,2048]{1,0:T(8,128)}, f32[128,1024]{1,0:T(8,128)}, f32[128,1024]{1,0:T(8,128)}, ...), branch_computations={%region_12.13_spmd, %region_13.14_spmd} | conditional | bytes 22544576 | solution.py:823
  290.2 11.1 %all-gather.13.cloned.1.call-done = f32[256,1024]{1,0:T(8,128)} async-done(((f32[128,1024]{1,0:T(8,128)}), f32[256,1024]{1,0:T(8,128)}) %all-gather.13.cloned.1.call-update) | async-done | bytes 1048592 | tf_op jit(solution)/shard_map/cond/branch_1_fun/all_gather | solution.py:872
  301.3 11.6 %all-gather.15.cloned.1.call-done = f32[256,1024]{1,0:T(8,128)} async-done(((f32[128,1024]{1,0:T(8,128)}), f32[256,1024]{1,0:T(8,128)}) %all-gather.15.cloned.1.call-update) | async-done | bytes 1048592 | tf_op jit(solution)/shard_map/cond/branch_1_fun/all_gather | solution.py:872
  314.9 9.6 %shard_map.338 = (f32[256,2048]{1,0:T(8,128)}, f32[256,2048]{1,0:T(8,128)}) custom-call(s32[3]{0:T(128)} %pad_add_fusion.meta, bf16[256,2048]{1,0:T(8,128)(2,1)} %get-tuple-element.479.refs_0_, bf16[256,2048]{1,0:T(8,128)(2,1)} %get-tuple-element.507.refs_1_, f32[256,1024]{1,0:T(8,128)} %get-tuple-element.508.refs_2_, ...), custom_call_target="tpu_custom_call" | custom-call | tf_op jit(solution)/shard_map/pallas_call | solution.py:124
  328.1 33.0 %collective-permute-done.35.refs_1_.refs_3_ = f32[256,2048]{1,0:T(8,128)} collective-permute-done((f32[256,2048]{1,0:T(8,128)}, f32[256,2048]{1,0:T(8,128)}, u32[]{:S(2)}, u32[]{:S(2)}) %collective-permute-start.35) | collective-permute-done | bytes 2097184 | tf_op jit(solution)/shard_map/ppermute | solution.py:766
  367.4 17.6 %conditional.16 = (bf16[256,2048]{1,0:T(8,128)(2,1)}, bf16[256,2048]{1,0:T(8,128)(2,1)}, f32[8,2048]{1,0:T(8,128)}) conditional(s32[]{:T(128)} %bitcast.7, () %tuple.86, (f32[128,2048]{1,0:T(8,128)}, s32[3]{0:T(128)}, f32[128,2048]{1,0:T(8,128)}, f32[8,2048]{1,0:T(8,128)}) %tuple.109), branch_computations={%region_14.15_spmd, %region_15.16_spmd} | conditional | flops 16384 | bytes 8847504 | solution.py:823
  385.0 41.7 %conditional.17 = (f32[8,2560]{1,0:T(8,128)S(1)}) conditional(s32[]{:T(128)} %bitcast.7, () %tuple.110, (f32[8,2048]{1,0:T(8,128)}, f32[8,512]{1,0:T(8,128)}) %tuple.111), branch_computations={%region_16.17_spmd, %region_17.18_spmd} | conditional | flops 61440 | bytes 1884288 | solution.py:823
  392.9 26.7 %collective-permute-done.12 = f32[8,2560]{1,0:T(8,128)S(1)} collective-permute-done((f32[8,2560]{1,0:T(8,128)S(1)}, f32[8,2560]{1,0:T(8,128)S(1)}, u32[]{:S(2)}, u32[]{:S(2)}) %collective-permute-start.12) | collective-permute-done | bytes 81952 | tf_op jit(solution)/shard_map/cond/branch_1_fun/ppermute | solution.py:769
  (124 shorter events, 206.4 us)
Async XLA Ops:
  12.7 26.5 %collective-permute-start.14 = (f32[128,2048]{1,0:T(8,128)}, f32[128,2048]{1,0:T(8,128)}, u32[]{:S(2)}, u32[]{:S(2)}) collective-permute-start(f32[128,2048]{1,0:T(8,128)} %get-tuple-element.431), channel_id=1, source_target_pairs={{0,8},{4,12},{8,0},{12,4},{16,24},{20,28},{24,16},{28,20},{1,9},{5... | collective-permute-start | bytes 3145736 | tf_op jit(solution)/shard_map/ppermute | solution.py:769
  39.2 34.2 %collective-permute-start.16 = (f32[128,2048]{1,0:T(8,128)}, f32[128,2048]{1,0:T(8,128)}, u32[]{:S(2)}, u32[]{:S(2)}) collective-permute-start(f32[128,2048]{1,0:T(8,128)} %collective-permute-done.15), channel_id=1, source_target_pairs={{8,0},{12,4},{16,24},{20,28},{9,1},{13,5},{17,25},{21,29},{10,2},{... | collective-permute-start | bytes 3145736 | tf_op jit(solution)/shard_map/ppermute | solution.py:775
  40.5 33.0 %collective-permute-start.17 = (f32[128,2048]{1,0:T(8,128)}, f32[128,2048]{1,0:T(8,128)}, u32[]{:S(2)}, u32[]{:S(2)}) collective-permute-start(f32[128,2048]{1,0:T(8,128)} %collective-permute-done.14), channel_id=1, source_target_pairs={{8,16},{12,20},{16,8},{20,12},{9,17},{13,21},{17,9},{21,13},{10,18... | collective-permute-start | bytes 3145736 | tf_op jit(solution)/shard_map/ppermute | solution.py:772
  73.5 31.5 %collective-permute-start.18 = (f32[128,2048]{1,0:T(8,128)}, f32[128,2048]{1,0:T(8,128)}, u32[]{:S(2)}, u32[]{:S(2)}) collective-permute-start(f32[128,2048]{1,0:T(8,128)} %get-tuple-element.438), channel_id=1, source_target_pairs={{0,8},{4,12},{8,0},{12,4},{16,24},{20,28},{24,16},{28,20},{1,9},{5... | collective-permute-start | bytes 3145736 | tf_op jit(solution)/shard_map/ppermute | solution.py:769
  105.0 28.3 %collective-permute-start.21 = (f32[128,2048]{1,0:T(8,128)}, f32[128,2048]{1,0:T(8,128)}, u32[]{:S(2)}, u32[]{:S(2)}) collective-permute-start(f32[128,2048]{1,0:T(8,128)} %collective-permute-done.19), channel_id=1, source_target_pairs={{8,0},{12,4},{16,24},{20,28},{9,1},{13,5},{17,25},{21,29},{10,2},{... | collective-permute-start | bytes 3145736 | tf_op jit(solution)/shard_map/ppermute | solution.py:775
  106.3 27.0 %collective-permute-start.22 = (f32[128,2048]{1,0:T(8,128)}, f32[128,2048]{1,0:T(8,128)}, u32[]{:S(2)}, u32[]{:S(2)}) collective-permute-start(f32[128,2048]{1,0:T(8,128)} %collective-permute-done.18), channel_id=1, source_target_pairs={{8,16},{12,20},{16,8},{20,12},{9,17},{13,21},{17,9},{21,13},{10,18... | collective-permute-start | bytes 3145736 | tf_op jit(solution)/shard_map/ppermute | solution.py:772
  132.0 40.6 %collective-permute-start.24 = (f32[128,2048]{1,0:T(8,128)}, f32[128,2048]{1,0:T(8,128)}, u32[]{:S(2)}, u32[]{:S(2)}) collective-permute-start(f32[128,2048]{1,0:T(8,128)} %collective-permute-done.17), channel_id=1, source_target_pairs={{8,0},{12,4},{16,24},{20,28},{9,1},{13,5},{17,25},{21,29},{10,2},{... | collective-permute-start | bytes 3145736 | tf_op jit(solution)/shard_map/ppermute | solution.py:775
  136.1 51.1 %collective-permute-start.23 = (f32[128,2048]{1,0:T(8,128)}, f32[128,2048]{1,0:T(8,128)}, u32[]{:S(2)}, u32[]{:S(2)}) collective-permute-start(f32[128,2048]{1,0:T(8,128)} %collective-permute-done.22), channel_id=1, source_target_pairs={{8,0},{12,4},{16,24},{20,28},{9,1},{13,5},{17,25},{21,29},{10,2},{... | collective-permute-start | bytes 3145736 | tf_op jit(solution)/shard_map/ppermute | solution.py:775
  137.4 35.2 %collective-permute-start.25 = (f32[256,4]{1,0:T(8,128)}, f32[256,4]{1,0:T(8,128)}, u32[]{:S(2)}, u32[]{:S(2)}) collective-permute-start(f32[256,4]{1,0:T(8,128)} %get-tuple-element.446), channel_id=1, source_target_pairs={{0,24},{4,28},{8,16},{12,20},{16,8},{20,12},{24,0},{28,4},{1,25},{... | collective-permute-start | bytes 12296 | tf_op jit(solution)/shard_map/ppermute | solution.py:769
  139.7 32.9 %collective-permute-start.26 = (f32[256,4]{1,0:T(8,128)}, f32[256,4]{1,0:T(8,128)}, u32[]{:S(2)}, u32[]{:S(2)}) collective-permute-start(f32[256,4]{1,0:T(8,128)} %get-tuple-element.446), channel_id=1, source_target_pairs={{0,16},{4,20},{8,24},{12,28},{16,0},{20,4},{24,8},{28,12},{1,17},{... | collective-permute-start | bytes 12296 | tf_op jit(solution)/shard_map/ppermute | solution.py:769
  187.2 30.4 %collective-permute-start.27 = (f32[256,512]{1,0:T(8,128)}, f32[256,512]{1,0:T(8,128)}, u32[]{:S(2)}, u32[]{:S(2)}) collective-permute-start(f32[256,512]{1,0:T(8,128)} %get-tuple-element.469.refs_9_), channel_id=1, source_target_pairs={{0,4},{4,0},{8,12},{12,8},{16,20},{20,16},{24,28},{28,24},{1,5},{5... | collective-permute-start | bytes 1572872 | tf_op jit(solution)/shard_map/ppermute | solution.py:769
  188.7 29.0 %collective-permute-start.28 = (f32[256,512]{1,0:T(8,128)}, f32[256,512]{1,0:T(8,128)}, u32[]{:S(2)}, u32[]{:S(2)}) collective-permute-start(f32[256,512]{1,0:T(8,128)} %get-tuple-element.469.refs_9_), channel_id=1, source_target_pairs={{0,8},{4,12},{8,0},{12,4},{16,24},{20,28},{24,16},{28,20},{1,9},{5... | collective-permute-start | bytes 1572872 | tf_op jit(solution)/shard_map/ppermute | solution.py:769
  188.7 29.0 %collective-permute-start.29 = (f32[256,512]{1,0:T(8,128)}, f32[256,512]{1,0:T(8,128)}, u32[]{:S(2)}, u32[]{:S(2)}) collective-permute-start(f32[256,512]{1,0:T(8,128)} %get-tuple-element.469.refs_9_), channel_id=1, source_target_pairs={{0,12},{4,8},{8,4},{12,0},{16,28},{20,24},{24,20},{28,16},{1,13},{... | collective-permute-start | bytes 1572872 | tf_op jit(solution)/shard_map/ppermute | solution.py:769
  217.6 60.5 %collective-permute-start.30 = (f32[256,1536]{1,0:T(8,128)}, f32[256,1536]{1,0:T(8,128)}, u32[]{:S(2)}, u32[]{:S(2)}) collective-permute-start(f32[256,1536]{1,0:T(8,128)} %get-tuple-element.484.refs_0_.refs_5_), channel_id=1, source_target_pairs={{0,4},{4,0},{8,12},{12,8},{16,20},{20,16},{24,28},{28,24},{1,5},{5... | collective-permute-start | bytes 4718600 | tf_op jit(solution)/shard_map/ppermute | solution.py:769
  219.2 58.9 %collective-permute-start.31 = (f32[256,1536]{1,0:T(8,128)}, f32[256,1536]{1,0:T(8,128)}, u32[]{:S(2)}, u32[]{:S(2)}) collective-permute-start(f32[256,1536]{1,0:T(8,128)} %get-tuple-element.484.refs_0_.refs_5_), channel_id=1, source_target_pairs={{0,8},{4,12},{8,0},{12,4},{16,24},{20,28},{24,16},{28,20},{1,9},{5... | collective-permute-start | bytes 4718600 | tf_op jit(solution)/shard_map/ppermute | solution.py:769
  219.2 46.5 %collective-permute-start.32 = (f32[128,1024]{1,0:T(8,128)}, f32[128,1024]{1,0:T(8,128)}, u32[]{:S(2)}, u32[]{:S(2)}) collective-permute-start(f32[128,1024]{1,0:T(8,128)} %get-tuple-element.485), channel_id=1, source_target_pairs={{0,4},{4,0},{8,12},{12,8},{16,20},{20,16},{24,28},{28,24},{1,5},{5... | collective-permute-start | bytes 1572872 | tf_op jit(solution)/shard_map/ppermute | solution.py:769
  219.8 48.3 %collective-permute-start.33 = (f32[128,1024]{1,0:T(8,128)}, f32[128,1024]{1,0:T(8,128)}, u32[]{:S(2)}, u32[]{:S(2)}) collective-permute-start(f32[128,1024]{1,0:T(8,128)} %get-tuple-element.486), channel_id=1, source_target_pairs={{0,8},{4,12},{8,0},{12,4},{16,24},{20,28},{24,16},{28,20},{1,9},{5... | collective-permute-start | bytes 1572872 | tf_op jit(solution)/shard_map/ppermute | solution.py:769
  221.8 56.4 %collective-permute-start.34 = (f32[128,1024]{1,0:T(8,128)}, f32[128,1024]{1,0:T(8,128)}, u32[]{:S(2)}, u32[]{:S(2)}) collective-permute-start(f32[128,1024]{1,0:T(8,128)} %get-tuple-element.487), channel_id=1, source_target_pairs={{0,12},{4,8},{8,4},{12,0},{16,28},{20,24},{24,20},{28,16},{1,13},{... | collective-permute-start | bytes 1572872 | tf_op jit(solution)/shard_map/ppermute | solution.py:769
  278.1 151.2 %collective-permute-start.38 = (f32[520,2048]{1,0:T(8,128)}, f32[520,2048]{1,0:T(8,128)}, u32[]{:S(2)}, u32[]{:S(2)}) collective-permute-start(f32[520,2048]{1,0:T(8,128)} %get-tuple-element.526), channel_id=1, source_target_pairs={{0,4},{4,0},{8,12},{12,8},{16,20},{20,16},{24,28},{28,24},{1,5},{5... | collective-permute-start | bytes 12779528 | tf_op jit(solution)/shard_map/ppermute | solution.py:769
  279.6 35.3 %collective-permute-start.36 = (f32[256,1536]{1,0:T(8,128)}, f32[256,1536]{1,0:T(8,128)}, u32[]{:S(2)}, u32[]{:S(2)}) collective-permute-start(f32[256,1536]{1,0:T(8,128)} %collective-permute-done.30.refs_6_), channel_id=1, source_target_pairs={{0,8},{4,12},{8,0},{12,4},{16,24},{20,28},{24,16},{28,20},{1,9},{5... | collective-permute-start | bytes 4718600 | tf_op jit(solution)/shard_map/ppermute | solution.py:769
  281.2 31.7 %all-gather.15.cloned.1.call-start = ((), (), s32[]{:S(2)}) async-start(), calls=%async_computation.4 | async-start | bytes 1572864 | tf_op jit(solution)/shard_map/cond/branch_1_fun/all_gather | solution.py:872
  312.9 48.1 %collective-permute-start.35 = (f32[256,2048]{1,0:T(8,128)}, f32[256,2048]{1,0:T(8,128)}, u32[]{:S(2)}, u32[]{:S(2)}) collective-permute-start(f32[256,2048]{1,0:T(8,128)} %get-tuple-element.505), channel_id=1, source_target_pairs={{0,2},{1,3},{2,0},{3,1},{4,6},{5,7},{6,4},{7,5},{8,10},{9,11},{10,... | collective-permute-start | bytes 6291464 | tf_op jit(solution)/shard_map/ppermute | solution.py:766
  324.5 115.2 %collective-permute-start.37 = (f32[256,2048]{1,0:T(8,128)}, f32[256,2048]{1,0:T(8,128)}, u32[]{:S(2)}, u32[]{:S(2)}) collective-permute-start(f32[256,2048]{1,0:T(8,128)} %get-tuple-element.524), channel_id=1, source_target_pairs={{0,16},{4,20},{8,24},{12,28},{16,0},{20,4},{24,8},{28,12},{1,17},{... | collective-permute-start | bytes 6291464 | tf_op jit(solution)/shard_map/ppermute | solution.py:769
  391.0 28.6 %collective-permute-start.12 = (f32[8,2560]{1,0:T(8,128)S(1)}, f32[8,2560]{1,0:T(8,128)S(1)}, u32[]{:S(2)}, u32[]{:S(2)}) collective-permute-start(f32[8,2560]{1,0:T(8,128)S(1)} %add.22), channel_id=1, source_target_pairs={{0,8},{4,12},{8,0},{12,4},{16,24},{20,28},{24,16},{28,20},{1,9},{5... | collective-permute-start | bytes 245768 | tf_op jit(solution)/shard_map/cond/branch_1_fun/ppermute | solution.py:769
  (21 other events, 257.3 us)
Sparse Core Ops, SparseCore 0:
  84.4 10.0 all-gather.6
  110.3 13.7 all-gather.8
  282.3 7.3 all-gather.10
  291.1 10.1 all-gather.12
  302.7 10.1 all-gather.14

commit v3 on v2

--- a/solution.py
+++ b/solution.py
@@ -91,7 +91,7 @@
     return jax.ShapeDtypeStruct(shape, dtype)
 
 
-def call(body, grid, ins, outs, shapes, scratch=(), tokens=0, aliases=None):
+def call(body, grid, ins, outs, shapes, scratch=(), tokens=0, aliases=None, cover=0):
     count = len(ins)
 
     def kernel(meta, *refs):
@@ -111,17 +111,21 @@
             dimension_semantics=("arbitrary",) * len(grid), vmem_limit_bytes=64 * MIB
         ),
         input_output_aliases=aliases or {},
+        cost_estimate=pl.CostEstimate(flops=cover, bytes_accessed=0, transcendentals=0)
+        if cover
+        else None,
     )
 
 
 class Order:
-    def __init__(self, meta):
+    def __init__(self, meta, cover=0):
         self.meta = meta
         self.last = []
+        self.cover = cover
 
     def run(self, body, grid, ins, outs, shapes, args, scratch=(), wait=(), aliases=None):
         extra = list(wait) + self.last
-        made = call(body, grid, ins, outs, shapes, scratch, len(extra), aliases)(
+        made = call(body, grid, ins, outs, shapes, scratch, len(extra), aliases, self.cover)(
             self.meta, *args, *extra
         )
         self.last = [made[0] if isinstance(made, (list, tuple)) else made]
@@ -136,22 +140,19 @@
     return jnp.concatenate([ref[pl.ds(first + i, 1), :] for i in range(count)], axis=1)
 
 
-def mask_kernel(meta, cot_mine, cot_other, mine, other):
+def mask_kernel(meta, cot, mine):
     size = mine.shape[0]
-    tiles = pl.num_programs(0)
-    for which, ref, out in ((0, cot_mine, mine), (1, cot_other, other)):
-        first = (((meta[0] + which) % 2) * tiles + pl.program_id(0)) * size
-        place = first + lax.broadcasted_iota(jnp.int32, (size, 1), 0)
-        out[...] = ref[...].astype(f32) * jnp.where(place < meta[1], 1.0, 0.0)
-
-
-def send_pieces(meta, first, second, outs, nb, block):
+    first = (meta[0] * pl.num_programs(0) + pl.program_id(0)) * size
+    place = first + lax.broadcasted_iota(jnp.int32, (size, 1), 0)
+    mine[...] = cot[...].astype(f32) * jnp.where(place < meta[1], 1.0, 0.0)
+
+
+def send_pieces(meta, value, outs, block):
     for s, out in enumerate(outs):
         at = meta[2] ^ (s + 1)
         for part, where in ((0, at), (1, at ^ 4)):
             cols = pl.ds(pl.multiple_of(where * block, block), block)
-            out[:, part * block : (part + 1) * block] = first[:, cols].astype(f32)
-            out[:, (part + 2) * block : (part + 3) * block] = second[:, cols]
+            out[:, part * block : (part + 1) * block] = value[:, cols].astype(f32)
 
 
 def flip_rows(value, half):
@@ -203,9 +204,10 @@
     return row_sum(jnp.where(diagonal(row.shape[1]), row, 0.0))
 
 
-def attend_kernel(meta, tok, gain, shift, weight, bias, sub_gain, sub_shift, out_w, table,
+def attend_kernel(nb, meta, tok, gain, shift, weight, bias, sub_gain, sub_shift, out_w, table,
                   a_out, q_out, k_out, v_out, p_out, o_out, y_mine, y_other,
-                  a_low, o_all):
+                  *rest):
+    sends, (a_low, o_all) = rest[:-2], rest[-2:]
     rows, width = o_all.shape
     half = rows // 2
     step = pl.program_id(0)
@@ -220,6 +222,8 @@
             wide = unit * gain[...] + shift[...]
             a_low[which * half : (which + 1) * half, :] = wide.astype(bf16)
         a_out[...] = a_low[...]
+        if sends:
+            send_pieces(meta, a_low.at[0:half, :], sends, tok.shape[1] // nb)
 
     turned = []
     for j in range(3):
@@ -284,24 +288,24 @@
             here = slice(which * half, (which + 1) * half)
             out[0:half, :] = mm(low[here], out_w[...]) + mean[here] * gain_out
             out[half : half + 8, :] = extra
-            out[half + 2 : half + 4, 0:rows] = stat_rows
-
-
-def stat_rows_of(ref):
-    half = ref.shape[1] // 2
-    return [ref[i : i + 1, :] for i in (2, 3)], [
-        jnp.concatenate([ref[i : i + 1, half:], ref[i : i + 1, 0:half]], axis=1) for i in (2, 3)
-    ]
-
-
-def pair_kernel(width, meta, mine, other, out):
-    half = out.shape[0] - 8
-    rows = 2 * half
-    out[...] = mine[...] + other[...]
-    here, _ = stat_rows_of(mine.at[half : half + 8, 0:rows])
-    _, there = stat_rows_of(other.at[half : half + 8, 0:rows])
-    joined = join_two(here, there, width)
-    out[half + 2 : half + 4, 0:rows] = jnp.concatenate(joined, axis=0)
+            for p in range(2):
+                out[half + 2 + 2 * p : half + 4 + 2 * p, 0:rows] = jnp.where(
+                    meta[0] == p, stat_rows, jnp.zeros_like(stat_rows)
+                )
+
+
+def join_rows(refs, odd, count):
+    cols = []
+    for ref in refs:
+        half = ref.shape[1] // 2
+        for p in range(2):
+            rows = ref[2 + 2 * p : 4 + 2 * p, :]
+            swapped = jnp.concatenate([rows[:, half:], rows[:, :half]], axis=1)
+            rows = jnp.where(odd == p, rows, swapped)
+            cols.append([rows[0:1], rows[1:2]])
+    near = join_two(cols[0], cols[1], count)
+    far = join_two(cols[2], cols[3], count)
+    return join_two(near, far, 2 * count)
 
 
 def middle_kernel(attn_width, meta, one, two, one_extra, two_extra, tok, bias, gain, shift,
@@ -312,9 +316,8 @@
     @pl.when(step == 0)
     def _():
         rows = stats.shape[0]
-        here, _ = stat_rows_of(one_extra.at[:, 0:rows])
-        there, _ = stat_rows_of(two_extra.at[:, 0:rows])
-        mean, m2 = join_two(here, there, attn_width // 2)
+        extras = (one_extra.at[:, 0:rows], two_extra.at[:, 0:rows])
+        mean, m2 = join_rows(extras, meta[0], attn_width // 4)
         inverse = lax.rsqrt(m2 * (1.0 / attn_width) + norm_eps)
         stats[...] = jnp.concatenate([as_column(mean), as_column(inverse)], axis=1)
         vec_out[...] = one_extra[...] + two_extra[...]
@@ -328,19 +331,18 @@
     b_out[...] = unit * gain[...] + shift[...]
 
 
-def unit_kernel(meta, o_all, stats, sub_gain, sub_shift, z_out):
-    heads = o_all.shape[1] // HD
-    unit = (o_all[...] - stats[:, 0:1]) * stats[:, 1:2]
-    z_out[...] = unit * spread(sub_gain, heads) + spread(sub_shift, heads)
-
-
-def dw_kernel(meta, mine, other, weight, out, low):
-    half = mine.shape[0]
+def dw_kernel(meta, cot, weight, out, low):
+    half = cot.shape[0] // 2
 
     @pl.when(pl.program_id(0) == 0)
     def _():
-        low[0:half, :] = mine[...].astype(bf16)
-        low[half:, :] = other[...].astype(bf16)
+        for which in range(2):
+            first = ((meta[0] + which) % 2) * half
+            place = first + lax.broadcasted_iota(jnp.int32, (half, 1), 0)
+            rows = cot[half_at(meta, which, half), :]
+            low[which * half : (which + 1) * half, :] = jnp.where(
+                place < meta[1], rows, jnp.zeros_like(rows)
+            )
 
     out[...] = mm_nt(low[...], weight[...]).astype(bf16)
 
@@ -546,7 +548,7 @@
     near_out[2 * block :, :] = totals[4]
 
 
-def norm2_kernel(meta, one, two, h1, dy, branch, vecs, gain, dh_out, sum_out):
+def norm2_kernel(nb, meta, one, two, h1, dy, branch, vecs, gain, dh_out, sum_out, *sends):
     size, full = h1.shape
     db = one[...] + two[...]
     unit, inverse = unit_rows(h1[...])
@@ -575,14 +577,12 @@
     @pl.when(pl.program_id(0) > 0)
     def _():
         sum_out[...] += sums
-
-
-def send_kernel(nb, meta, a_all, dh, *outs):
-    send_pieces(meta, a_all, dh, outs, nb, a_all.shape[1] // nb)
-
-
-def attend_back_kernel(attn_width, meta, dh_mine, dh_other, o_all, stats, sub_gain, out_w, q_all,
-                       k_all, v_all, probs_all, table, dm_out, sum_out, dhl_out, do_all):
+    if sends:
+        send_pieces(meta, dh_out, sends, full // nb)
+
+
+def attend_back_kernel(attn_width, meta, dh_mine, dh_other, o_all, stats, sub_gain, sub_shift, out_w, q_all,
+                       k_all, v_all, probs_all, table, dm_out, dv_out, sum_out, dhl_out, do_all):
     rows, width = o_all.shape
     half = rows // 2
     full = out_w.shape[1]
@@ -606,6 +606,7 @@
             - unit * (sums[:, 1:2] * (1.0 / attn_width))
         )
         do_all[...] = do.astype(bf16)
+        dv_out[:, width:] = unit * gain_row + spread(sub_shift, heads)
         sum_out[0:1, :] = jnp.sum(dz * unit, axis=0, keepdims=True)
         sum_out[1:2, :] = jnp.sum(dz, axis=0, keepdims=True)
         sum_out[5:8, :] = jnp.zeros((3, width), f32)
@@ -651,19 +652,23 @@
                 s = jnp.concatenate([table[2 * j + 1, at, :]] * 2, axis=1)
                 parts.append(grad[here] * c - flipped[here] * s)
             grad = jnp.concatenate(parts, axis=0)
-        dm_out[:, pl.ds(pl.multiple_of(j * width + step * QUAD, QUAD), QUAD)] = grad
+        if j < 2:
+            dm_out[:, pl.ds(pl.multiple_of(j * width + step * QUAD, QUAD), QUAD)] = grad
+        else:
+            dv_out[:, quad] = grad
         sum_out[2 + j : 3 + j, quad] = jnp.sum(
             grad.astype(bf16).astype(f32), axis=0, keepdims=True
         )
 
 
-def tail_kernel(meta, dm, weight, w, down_w, mine, other, low):
+def tail_kernel(meta, dm, dv, weight, w, down_w, mine, other, low):
     half = mine.shape[0] // 2
     width = weight.shape[2]
 
     @pl.when(pl.program_id(0) == 0)
     def _():
-        low[...] = dm[...].astype(bf16)
+        low[:, 0 : 2 * width] = dm[...].astype(bf16)
+        low[:, 2 * width :] = dv[...].astype(bf16)
 
     total = mm_nt(low[:, 0:width], weight[0])
     for j in (1, 2):
@@ -675,30 +680,25 @@
     other[half:, :] = part[half:, :]
 
 
-def norm1_kernel(meta, one, two, res_one, res_two, h1, tok, dh, gain, bias, sum_in, out, res_out,
-                 sum_out):
+def norm1_kernel(meta, one, two, h1, tok, dh, gain, bias, sum_in, out, sum_out):
     full = out.shape[1]
-    da = one[...] + two[...]
-    unit, inverse = unit_rows(tok[...].astype(f32))
-    out[...] = dh[:, 0:full] + unit_back(da, unit, inverse, gain[...])
-    res_out[...] = h1[...] + (res_one[...] + res_two[...]) + bias[...]
-    sums = jnp.concatenate(
-        [
-            jnp.zeros((4, full), f32),
-            jnp.sum(da * unit, axis=0, keepdims=True),
-            jnp.sum(da, axis=0, keepdims=True),
-            jnp.zeros((2, full), f32),
-        ],
-        axis=0,
-    )
-
-    @pl.when(pl.program_id(0) == 0)
-    def _():
-        sum_out[...] = sum_in[...] + sums
-
-    @pl.when(pl.program_id(0) > 0)
-    def _():
-        sum_out[...] += sums
+    step = pl.program_id(0)
+    total = one[...] + two[...]
+
+    @pl.when(step == 0)
+    def _():
+        sum_out[...] = sum_in[...]
+
+    @pl.when(step < pl.num_programs(0) // 2)
+    def _():
+        unit, inverse = unit_rows(tok[...].astype(f32))
+        out[...] = dh[:, 0:full] + unit_back(total, unit, inverse, gain[...])
+        sum_out[4:5, :] += jnp.sum(total * unit, axis=0, keepdims=True)
+        sum_out[5:6, :] += jnp.sum(total, axis=0, keepdims=True)
+
+    @pl.when(step >= pl.num_programs(0) // 2)
+    def _():
+        out[...] = h1[...] + total + bias[...]
 
 
 def place_kernel(meta, mine, other, out):
@@ -714,36 +714,58 @@
     refs[count][...] = total
 
 
-def square_kernel(nb, meta, a_all, dhl, *refs):
-    pieces, sides, (own_out, mirror_out, a_low, d_low, right) = refs[:3], refs[3:11], refs[11:]
-    rows, full = a_all.shape
+def join_kernel(meta, *refs):
+    pieces, (out, buffer, sems) = refs[:3], refs[3:]
+    half = buffer.shape[1]
+    loads = [pltpu.make_async_copy(pieces[i], buffer.at[i], sems.at[i]) for i in range(3)]
+    for copy in loads:
+        copy.start()
+    stores = []
+    for i, copy in enumerate(loads):
+        copy.wait()
+        store = pltpu.make_async_copy(
+            buffer.at[i], out.at[i * half : (i + 1) * half, :], sems.at[3 + i]
+        )
+        store.start()
+        stores.append(store)
+    for store in stores:
+        store.wait()
+
+
+def square_kernel(nb, part, meta, *refs):
+    lists, rest = refs[: 7 * (part + 1)], refs[7 * (part + 1) :]
+    sides, (own_out, mirror_out), lows = rest[:4], rest[4:6], rest[6:]
+    right = lows[-1]
+    rows, full = lists[0].shape
     half, block = rows // 2, full // nb
-    split = sides[0].shape[1]
-    for part, at in ((0, meta[2]), (1, meta[2] ^ 4)):
-        cols = pl.ds(pl.multiple_of(at * block, block), block)
-        a_low[0:rows, part * block : (part + 1) * block] = a_all[:, cols]
-        d_low[0:rows, part * block : (part + 1) * block] = dhl[:, cols]
+    width = own_out.shape[1] // 2
+    for n, low in enumerate(lows[:-1]):
+        own, mine, other = lists[7 * n], lists[7 * n + 1 : 7 * n + 4], lists[7 * n + 4 : 7 * n + 7]
+        for which, at in ((0, meta[2]), (1, meta[2] ^ 4)):
+            cols = pl.ds(pl.multiple_of(at * block, block), block)
+            low[0:rows, which * block : (which + 1) * block] = own[:, cols]
+        for s in range(3):
+            here = rows * (s + 1)
+            low[here : here + half, :] = mine[s][...].astype(bf16)
+            low[here + half : here + rows, :] = other[s][...].astype(bf16)
     for s in range(4):
-        at = rows * s
-        if s > 0:
-            for which in range(2):
-                here = at + which * half
-                rows_here = half_at(meta, which, half)
-                a_low[here : here + half, :] = pieces[s - 1][rows_here, 0 : 2 * block].astype(bf16)
-                d_low[here : here + half, :] = pieces[s - 1][rows_here, 2 * block :].astype(bf16)
-        right[at : at + rows, 0:split] = sides[s][...].astype(bf16)
-        right[at : at + rows, split:] = sides[4 + s][...].astype(bf16)
-    for out, part in ((mirror_out, block), (own_out, 0)):
-        out[:, 0:split] = mm_tn(a_low[:, part : part + block], right[:, 0:split])
-        out[:, split:] = mm_tn(d_low[:, part : part + block], right[:, split:])
-
-
-def final_square_kernel(meta, own, got, m_out, o_out):
+        right[rows * s : rows * (s + 1), :] = sides[s][...].astype(bf16)
+    for out, first in ((mirror_out, block), (own_out, 0)):
+        left = lows[0][:, first : first + block]
+        if part == 0:
+            out[...] = mm_tn(left, right[...])
+        else:
+            out[:, 0:width] = mm_tn(left, right[:, 0:width])
+            out[:, width:] = mm_tn(lows[1][:, first : first + block], right[:, width:])
+
+
+def final_square_kernel(meta, one_own, one_got, two_own, two_got, m_out, o_out):
     width = m_out.shape[2]
-    for j in range(3):
+    for j in range(2):
         cols = slice(j * width, (j + 1) * width)
-        m_out[j] = own[:, cols] + got[:, cols]
-    o_out[...] = (own[:, 3 * width :] + got[:, 3 * width :]).T
+        m_out[j] = one_own[:, cols] + one_got[:, cols]
+    m_out[2] = two_own[:, 0:width] + two_got[:, 0:width]
+    o_out[...] = (two_own[:, width:] + two_got[:, width:]).T
 
 
 def final_hidden_kernel(meta, up_own, up_got, down_own, down_got, up_out, down_out):
@@ -807,6 +829,7 @@
         chunks = hidden // span
         parts = D // span
         quads = heads // 4
+        sends = 3 if full else 0
         tiles = 4
         index = lax.axis_index("batch")
         meta = jnp.stack([lax.axis_index("mp") % 2, lengths[0], index]).astype(jnp.int32)
@@ -834,7 +857,6 @@
         half_shape = shape_of((half, D))
         half_tile = pl.BlockSpec((half // tiles, D), rolled(0))
         tok_mine = pl.BlockSpec((half // tiles, D), lambda i, m: (m[0] * tiles + i, 0))
-        tok_other = pl.BlockSpec((half // tiles, D), lambda i, m: ((1 - m[0]) * tiles + i, 0))
         ext_spec, ext_shape = whole((half + 8, D)), shape_of((half + 8, D))
         dh_spec, dh_shape = whole((half, D + 128)), shape_of((half, D + 128))
         dh_tile = pl.BlockSpec((half // tiles, D + 128), rolled(0))
@@ -856,24 +878,11 @@
         sum_tile = pl.BlockSpec((8, span), rolled(1))
         gain2, shift2, bias2 = line(sub2_gain), line(sub2_shift), line(up_bias)
 
-        def add(order, *terms):
-            shape = terms[0].shape
-            tall_tile = pl.BlockSpec((shape[0] // tiles, shape[1]), rolled(0))
-            return order.run(
-                functools.partial(add_kernel, len(terms)),
-                (tiles,),
-                [tall_tile] * len(terms),
-                tall_tile,
-                shape_of(shape),
-                terms,
-            )
-
         def pair_join(value):
             return lax.all_gather(value, "mp", axis_index_groups=pairs, axis=0, tiled=True)
 
-        dy, dy_other = Order(meta).run(
-            mask_kernel, (tiles,), [tok_mine, tok_other], [half_tile] * 2, [half_shape] * 2,
-            (cotangent, cotangent),
+        dy = Order(meta).run(
+            mask_kernel, (tiles,), [tok_mine], half_tile, half_shape, (cotangent,)
         )
         if full:
             dy_e1, dy_m1 = to_batch(dy, 2), to_middle(dy)
@@ -881,31 +890,27 @@
         def attention():
             order = Order(meta)
             low_shape = shape_of((rows, width), bf16)
-            a, q, k, v, probs, o, y_mine, y_other = order.run(
-                attend_kernel,
+            a, q, k, v, probs, o, y_mine, y_other, *a_sent = order.run(
+                functools.partial(attend_kernel, nb),
                 (quads,),
                 [whole((rows, D)), row_spec, row_spec, quad_weight, whole((3, heads, HD)),
                  whole((heads, HD)), whole((heads, HD)), whole((width, D)), table_spec],
-                [whole((rows, D)), quad, quad, quad, probs_spec, wide_spec, ext_spec, ext_spec],
+                    [whole((rows, D)), quad, quad, quad, probs_spec, wide_spec, ext_spec, ext_spec]
+                + [whole((half, 2 * block))] * sends,
                 [low_rows, low_shape, low_shape, low_shape,
-                 shape_of((heads, rows, rows)), wide_shape, ext_shape, ext_shape],
+                 shape_of((heads, rows, rows)), wide_shape, ext_shape, ext_shape]
+                + [shape_of((half, 2 * block))] * sends,
                 (tokens, line(norm1_gain), line(norm1_shift), weight, qkv_bias, sub1_gain,
                  sub1_shift, out_weight, table),
                 [pltpu.VMEM((rows, D), bf16), pltpu.VMEM((rows, width), f32)],
             )
-            y_pair = order.run(
-                functools.partial(pair_kernel, width),
-                (1,),
-                [ext_spec] * 2,
-                ext_spec,
-                ext_shape,
-                (y_mine, to_core(y_other)),
-            )
-            return a, q, k, v, probs, o, y_pair
-
-        a, q, k, v, probs, o, y_pair = segment(attention)
+            y_pair = y_mine + to_core(y_other)
+            return a, q, k, v, probs, o, y_pair, a_sent
+
+        a, q, k, v, probs, o, y_pair, a_sent = segment(attention)
         if full:
-            dy_e1, dy_m1, y_pair = meet(dy_e1, dy_m1, y_pair)
+            dy_e1, dy_m1, y_pair, a_sent = meet(dy_e1, dy_m1, y_pair, a_sent)
+            a_got = [None, to_batch(a_sent[1], 2), to_batch(a_sent[2], 3)]
             dy_f1, dy_m2 = outward(dy_m1), to_middle(dy_e1)
 
         def after_attention():
@@ -914,10 +919,10 @@
             dw, dyl = order.run(
                 dw_kernel,
                 (chunks,),
-                [whole((half, D))] * 2 + [flat],
+                [whole((rows, D)), flat],
                 [many, whole((rows, D))],
                 [low_hidden, low_rows],
-                (dy, dy_other, down_weight),
+                (cotangent, down_weight),
             )
             return dw, dyl, order.run(
                 functools.partial(middle_kernel, attn_width),
@@ -932,7 +937,10 @@
 
         dw, dyl, (h1, branch, b_mine, vecs, stats) = segment(after_attention)
         if full:
-            dy_f1, dy_m2, b_mine = meet(dy_f1, dy_m2, b_mine)
+            dy_f1, dy_m2, b_mine, a_sent, a_got[1], a_got[2] = meet(
+                dy_f1, dy_m2, b_mine, a_sent, a_got[1], a_got[2]
+            )
+            a_got[0] = to_batch(a_sent[0], 1)
             b_e1, b_m1 = to_batch(b_mine, 2), to_middle(b_mine)
 
         def hidden_first():
@@ -951,12 +959,13 @@
 
         g, slope, g_stats, b, dy_near = segment(hidden_first)
         if full:
-            b_e1, b_m1, g, dy_near = meet(b_e1, b_m1, g, dy_near)
+            b_e1, b_m1, a_got, g, dy_near = meet(b_e1, b_m1, a_got, g, dy_near)
             b_f1, b_m2 = outward(b_m1), to_middle(b_e1)
 
         def hidden_back():
             order = Order(meta)
             b_near = pair_join(b_e1) if full else ()
+            a_core = [to_core(piece) for piece in a_got[1:]] if full else ()
             w, du, st, h_sum, db_mine, db_other = order.run(
                 functools.partial(back_kernel, ff_width, span),
                 (parts,),
@@ -967,14 +976,14 @@
                 [low_hidden, low_hidden, tiny4, shape_of((8, hidden)), half_shape, half_shape],
                 (g, slope, dw, g_stats, gain2, shift2, up_weight),
             )
-            return w, du, st, h_sum, add(order, db_mine, to_core(db_other)), b_near
-
-        w, du, st, h_sum, db_pair, b_near = segment(hidden_back)
+            return w, du, st, h_sum, db_mine + to_core(db_other), b_near, a_core
+
+        w, du, st, h_sum, db_pair, b_near, a_core = segment(hidden_back)
         if full:
             b_f1, b_m2, db_pair, b_near = meet(b_f1, b_m2, db_pair, b_near)
             st_near, st_far = to_batch(st, 2), (to_batch(st, 6), to_batch(st, 4))
-            st_near, b_m2 = meet(st_near, b_m2)
-            b_f2, dy_f2 = outward(b_m2), outward(dy_m2)
+            st_near, dy_m2 = meet(st_near, dy_m2)
+            dy_f2, b_f2 = outward(dy_m2), outward(b_m2)
 
         def far_pass(order, b_src, d_src, starts, lower, stats_in, own, wait=()):
             size = len(starts) * rows
@@ -1019,32 +1028,50 @@
                     order, [b_near], [dy_near], (((0, 0), (0, half)),), 0, (st_near, st_near),
                     (w, du, h_sum, b, dyl),
                 )
-            z = order.run(
-                unit_kernel,
-                (1,),
-                [wide_spec, whole((rows, 2)), whole((heads, HD)), whole((heads, HD))],
-                wide_spec,
-                wide_shape,
-                (o, stats, sub1_gain, sub1_shift),
-            )
-            dh_mine, d_sums = order.run(
-                norm2_kernel,
+            outs = order.run(
+                functools.partial(norm2_kernel, nb),
                 (tiles,),
                 [half_tile] * 5 + [whole((8, D)), row_spec],
-                [dh_tile, whole((8, D))],
-                [dh_shape, shape_of((8, D))],
+                [dh_tile, whole((8, D))]
+                + [pl.BlockSpec((half // tiles, 2 * block), rolled(0))] * sends,
+                [dh_shape, shape_of((8, D))] + [shape_of((half, 2 * block))] * sends,
                 (db_pair, db_cross, h1, dy, branch, vecs, line(norm2_gain)),
             )
-            return dh_mine, d_sums, z, sums
-
-        dh_mine, d_sums, z, sums = segment(middle_norm_back)
+            return outs, sums
+
+        (dh_mine, d_sums, *dh_sent), sums = segment(middle_norm_back)
         if full:
-            b_f2, dy_f2, st_far, dh_mine, z = meet(b_f2, dy_f2, st_far, dh_mine, z)
-            z_x, z_z, z_d = to_batch(z, 1), to_batch(z, 2), to_batch(z, 3)
+            st_far, dy_f2, dh_mine, dh_sent = meet(st_far, dy_f2, dh_mine, dh_sent)
+            dh_got = [to_batch(dh_sent[0], 1), None, None]
 
         def attention_back():
             order = Order(meta)
             dh_other = to_core(dh_mine)
+            a_first = to_core(a_got[0]) if full else ()
+            dm, dv, h_sums, dhl = order.run(
+                functools.partial(attend_back_kernel, attn_width),
+                (quads,),
+                [dh_spec, dh_spec, wide_spec, whole((rows, 2)), whole((heads, HD)),
+                 whole((heads, HD)), whole((width, D)), quad, quad, quad, probs_spec, table_spec],
+                [whole((rows, 2 * width))] * 2 + [whole((8, width)), whole((rows, D))],
+                [shape_of((rows, 2 * width))] * 2 + [shape_of((8, width)), low_rows],
+                (dh_mine, dh_other, o, stats, sub1_gain, sub1_shift, out_weight, q, k, v, probs,
+                 table),
+                [pltpu.VMEM((rows, width), bf16)],
+            )
+            return dm, dv, h_sums, dhl, a_first
+
+        dm, dv, h_sums, dhl, a_first = segment(attention_back)
+        main = Order(meta, 10**11)
+        if full:
+            b_f2, dh_got[0], dm, dv, dh_sent = meet(b_f2, dh_got[0], dm, dv, dh_sent)
+            dm_x, dm_z = to_batch(dm, 1), to_batch(dm, 2)
+            dh_got[1] = to_batch(dh_sent[1], 2)
+
+        both = pl.BlockSpec((rows, span), rolled(1))
+
+        def prepare():
+            order = Order(meta)
             packed = ()
             if full:
                 far = order.run(
@@ -1057,103 +1084,119 @@
                     [pltpu.VMEM((4, half, D), f32), pltpu.SemaphoreType.DMA((8,))],
                 )
                 packed = [far, to_core(far)]
-            dm, h_sums, dhl = order.run(
-                functools.partial(attend_back_kernel, attn_width),
-                (quads,),
-                [dh_spec, dh_spec, wide_spec, whole((rows, 2)), whole((heads, HD)),
-                 whole((width, D)), quad, quad, quad, probs_spec, table_spec],
-                [whole((rows, 3 * width)), whole((8, width)), whole((rows, D))],
-                [shape_of((rows, 3 * width)), shape_of((8, width)), low_rows],
-                (dh_mine, dh_other, o, stats, sub1_gain, out_weight, q, k, v, probs, table),
-                [pltpu.VMEM((rows, width), bf16)],
-            )
-            sends = ()
-            if full:
-                sends = order.run(
-                    functools.partial(send_kernel, nb),
-                    (tiles,),
-                    [half_tile, dh_tile],
-                    [pl.BlockSpec((half // tiles, 4 * block), rolled(0))] * 3,
-                    [shape_of((half, 4 * block))] * 3,
-                    (a, dh_mine),
-                )
-            return packed, dm, h_sums, dhl, sends
-
-        packed, dm, h_sums, dhl, sends = segment(attention_back)
-        main = Order(meta)
+            tail_mine, tail_other = order.run(
+                tail_kernel,
+                (parts,),
+                [whole((rows, 2 * width)), pl.BlockSpec((rows, width), lambda i, *_: (0, 0)),
+                 pl.BlockSpec((3, span, width), lambda i, *_: (0, i, 0)),
+                 whole((rows, hidden)), pl.BlockSpec((hidden, span), rolled(1))],
+                [both] * 2,
+                [shape_of((rows, D))] * 2,
+                (dm, dv, weight, w, down_weight),
+                [pltpu.VMEM((rows, 3 * width), bf16)],
+            )
+            return packed, tail_mine + to_core(tail_other)
+
+        packed, da_pair = segment(prepare)
         if full:
-            z_x, z_z, z_d, dm, sends = meet(z_x, z_z, z_d, dm, sends)
-            dm_x, dm_z = to_batch(dm, 1), to_batch(dm, 2)
-            pieces = [to_batch(sends[s - 1], s) for s in (1, 2, 3)]
+            dm_x, dm_z, dh_got[1], packed, dv, dh_sent, da_pair = meet(
+                dm_x, dm_z, dh_got[1], packed, dv, dh_sent, da_pair
+            )
+            dv_x = to_batch(dv, 1)
+            dm_d = to_batch(dm_x, 2)
+            dh_got[2] = to_batch(dh_sent[2], 3)
+            da_cross = to_y(da_pair)
             sums = far_pass(
                 main, packed, packed, (((0, 0), (1, 0)), ((0, half), (1, half))), rows,
                 (st_far[0], st_far[1], st_far[1], st_far[0]), sums,
             )
 
-        both = pl.BlockSpec((rows, span), rolled(1))
-        tail_mine, tail_other = main.run(
-            tail_kernel,
-            (parts,),
-            [whole((rows, 3 * width)), pl.BlockSpec((3, span, width), lambda i, *_: (0, i, 0)),
-             whole((rows, hidden)), pl.BlockSpec((hidden, span), rolled(1))],
-            [both] * 2,
-            [shape_of((rows, D))] * 2,
-            (dm, weight, w, down_weight),
-            [pltpu.VMEM((rows, 3 * width), bf16)],
-        )
         if full:
-            dm_x, dm_z, pieces, sums, tail_other = meet(dm_x, dm_z, pieces, sums, tail_other)
-            near_got, dm_d = to_batch(sums[2], 1), to_batch(dm_x, 2)
-
-        def input_back():
-            joined = [pair_join(piece) for piece in pieces] if full else ()
-            return add(Order(meta), tail_mine, to_core(tail_other)), joined
-
-        da_pair, pieces = segment(input_back)
-        da_cross = to_y(da_pair)
+            dv_x, dm_d, dh_got[2], sums, dm, dv = meet(dv_x, dm_d, dh_got[2], sums, dm, dv)
+            near_got, dv_z, dv_d = to_batch(sums[2], 1), to_batch(dv, 2), to_batch(dv_x, 2)
+            cut = 2 * width
+            a_join = [*a_got, a_first, *a_core]
+
+            def square(part, lefts, sides):
+                def piece(array, s):
+                    at = s if array.shape[0] > half else 0
+                    return pl.BlockSpec((half, 2 * block), lambda i, *_: (at, 0))
+
+                specs = []
+                for _, got in lefts:
+                    specs += [whole((rows, D))] + [piece(got[i], i % 3) for i in range(6)]
+                lists = [array for own, got in lefts for array in (own, *got)]
+                return main.run(
+                    functools.partial(square_kernel, nb, part),
+                    (1,),
+                    specs + [whole((rows, cut))] * 4,
+                    [whole((block, cut))] * 2,
+                    [shape_of((block, cut))] * 2,
+                    (*lists, *sides),
+                    [pltpu.VMEM((4 * rows, 2 * block), bf16)] * len(lefts)
+                    + [pltpu.VMEM((4 * rows, cut), bf16)],
+                )
+
+            one_own, one_mirror = square(0, [(a, a_join)], [dm, dm_x, dm_z, dm_d])
+            one_got = to_batch(one_mirror, 4)
+        else:
+            da_cross = to_y(da_pair)
+        row_tile = pl.BlockSpec((half // tiles, D), rolled(0))
+        row_mod = pl.BlockSpec((half // tiles, D), lambda i, *_: (i % tiles, 0))
+        last = main.last
+
+        def input_norm_back():
+            order = Order(meta)
+            order.last = last
+            joined = ()
+            if full:
+                dh_all = Order(meta).run(
+                    join_kernel,
+                    (1,),
+                    [pl.BlockSpec(memory_space=pl.ANY)] * 3,
+                    pl.BlockSpec(memory_space=pl.ANY),
+                    shape_of((3 * half, 2 * block)),
+                    dh_got,
+                    [pltpu.VMEM((3, half, 2 * block), f32), pltpu.SemaphoreType.DMA((6,))],
+                )
+                joined = [dh_all] * 3 + [to_core(dh_all)] * 3
+            outs = order.run(
+                norm1_kernel,
+                (2 * tiles,),
+                [row_tile, row_tile, row_mod,
+                 pl.BlockSpec((half // tiles, D), lambda i, m: (m[0] * tiles + i % tiles, 0)),
+                 pl.BlockSpec((half // tiles, D + 128), lambda i, *_: (i % tiles, 0)), row_spec,
+                 row_spec, whole((8, D))],
+                [row_tile, whole((8, D))],
+                [shape_of((rows, D)), shape_of((8, D))],
+                (da_pair, da_cross, h1, tokens, dh_mine, line(norm1_gain),
+                 line(down_bias), d_sums),
+            )
+            return outs, joined
+
+        (mine, d_sums), dh_join = segment(input_norm_back)
         if full:
-            da_pair, pieces = meet(da_pair, pieces)
-
-            sides = [dm, dm_x, dm_z, dm_d, z, z_x, z_z, z_d]
-            s_own, s_mirror = main.run(
-                functools.partial(square_kernel, nb),
-                (1,),
-                [whole((rows, D))] * 2 + [whole((rows, 4 * block))] * 3
-                + [whole((rows, 3 * width))] * 4 + [wide_spec] * 4,
-                [whole((block, 4 * width))] * 2,
-                [shape_of((block, 4 * width))] * 2,
-                (a, dhl, *pieces, *sides),
-                [pltpu.VMEM((4 * rows, 2 * block), bf16)] * 2
-                + [pltpu.VMEM((4 * rows, 4 * width), bf16)],
-            )
-            s_got = to_batch(s_mirror, 4)
-
-        main.last = [s_own] if full else []
-        low_tile = pl.BlockSpec((half // tiles, D), lambda i, *_: (tiles + i, 0))
-        t_mine, r_mine, d_sums = main.run(
-            norm1_kernel,
-            (tiles,),
-            [half_tile, half_tile, low_tile, low_tile, half_tile, tok_mine, dh_tile, row_spec,
-             row_spec, whole((8, D))],
-            [half_tile, half_tile, whole((8, D))],
-            [half_shape, half_shape, shape_of((8, D))],
-            (da_pair, da_cross, da_pair, da_cross, h1, tokens, dh_mine, line(norm1_gain),
-             line(down_bias), d_sums),
-        )
+            dv_z, dv_d, dh_join = meet(dv_z, dv_d, dh_join)
+            two_own, two_mirror = square(
+                1, [(a, a_join), (dhl, dh_join)], [dv, dv_x, dv_z, dv_d]
+            )
+            two_got = to_batch(two_mirror, 4)
 
         def place():
             order = Order(meta)
             sums = d_sums + to_core(d_sums)
+            other = to_core(mine)
             outs = [
                 order.run(
                     place_kernel,
                     (2 * tiles,),
-                    [pl.BlockSpec((half // tiles, D), lambda i, *_: (i % tiles, 0))] * 2,
-                    pl.BlockSpec((half // tiles, D), rolled(0)),
+                    [pl.BlockSpec((half // tiles, D), functools.partial(
+                        lambda first, i, *_: (first + i % tiles, 0), first))] * 2,
+                    row_tile,
                     low_rows,
-                    (mine, to_core(mine)),
+                    (mine, other),
                 )
-                for mine in (r_mine, t_mine)
+                for first in (tiles, 0)
             ]
             return (*outs, sums)
 
@@ -1175,7 +1218,8 @@
             d_sums = scatter(d_sums, 1)
             h_sums = lax.psum(h_sums, "batch")
             h_parts = scatter(h_sum[:3].reshape(3, lanes, 128), 2)
-            dm_low = dm.astype(bf16)
+            dm_low = jnp.concatenate([dm, dv[:, :width]], axis=1).astype(bf16)
+            z = dv[:, width:]
             grad_qkv = scatter(
                 jnp.stack([mm_tn(a, dm_low[:, j * width : (j + 1) * width]) for j in range(3)], 1), 0
             )
@@ -1183,31 +1227,32 @@
             grad_up = scatter(mm_tn(b, du), 0)
             grad_down = scatter(mm_tn(w, dyl), 1)
         else:
+            near_got, sums, d_sums = meet(near_got, sums, d_sums)
+            h_parts = (sums[2][2 * block :] + near_got[2 * block :])[:3]
+            h_parts = lax.dynamic_slice_in_dim(
+                h_parts.reshape(3, lanes, 128), index * per, per, 2
+            )
+            strip = hidden // 4
+            grad_up, grad_down = main.run(
+                final_hidden_kernel,
+                (4,),
+                [pl.BlockSpec((block, strip), rolled(1))] * 3
+                + [pl.BlockSpec((block, strip), lambda i, *_: (1, i))],
+                [pl.BlockSpec((block, strip), rolled(1)), pl.BlockSpec((strip, block), rolled(0))],
+                [shape_of((block, hidden)), shape_of((hidden, block))],
+                (sums[0], near_got, sums[1], near_got),
+            )
+            d_sums, grad_up = meet(d_sums, grad_up)
             comb = segment(small_sums)
             d_sums = lax.dynamic_slice_in_dim(comb, index * block, block, 1)
             h_sums = comb[:, D:]
-            h_parts = (sums[2][2 * block :] + near_got[2 * block :])[:3]
-            h_parts = lax.dynamic_slice_in_dim(
-                h_parts.reshape(3, lanes, 128), index * per, per, 2
-            )
-            main.last = [comb]
-            cut = hidden // 4
-            grad_up, grad_down = main.run(
-                final_hidden_kernel,
-                (4,),
-                [pl.BlockSpec((block, cut), rolled(1))] * 3
-                + [pl.BlockSpec((block, cut), lambda i, *_: (1, i))],
-                [pl.BlockSpec((block, cut), rolled(1)), pl.BlockSpec((cut, block), rolled(0))],
-                [shape_of((block, hidden)), shape_of((hidden, block))],
-                (sums[0], near_got, sums[1], near_got),
-            )
             grad_qkv, grad_out = main.run(
                 final_square_kernel,
                 (1,),
-                [whole((block, 4 * width))] * 2,
+                [whole((block, cut))] * 4,
                 [whole((3, block, width)), whole((width, block))],
                 [shape_of((3, block, width)), shape_of((width, block))],
-                (s_own, s_got),
+                (one_own, one_got, two_own, two_got),
             )
             grad_qkv = jnp.transpose(grad_qkv, (1, 0, 2))
         per = HD // nb

time: 453 us -> 395 us (0.87)
  waiting for transfers between devices: 179 us -> 117 us
  Pallas kernels: 183 us -> 171 us
  other arithmetic: 2.95 us -> 10 us
  local copies, waits for them, and re-layouts: 8.5 us -> 14.6 us
    all_gather x5 -> x2, waiting for transfers between devices: 22.7 us -> 0.01 us  [pair_join(): lax.all_gather(value, 'mp', axis_index_groups=pairs, axis=0, tiled=True)]
    ppermute x3, waiting for transfers between devices: 52.8 us -> 31.2 us  [to_y(): return lax.ppermute(value, 'mp', cross)]
    ppermute x4, waiting for transfers between devices: 14.6 us -> 1.82 us  [outward(): return lax.ppermute(value, 'batch', outward_link)]
    pallas_call x23 -> x20, Pallas kernels: 183 us -> 171 us  [run(): call(body, grid, ins, outs, shapes, scratch, len(extra), aliases, self.co...]
    cond x1 -> x5, local copies, waits for them, and re-layouts: 0.84 us -> 9.31 us
    add x0 -> x3, other arithmetic: none -> 7.94 us  [the longest x1 3.2 us: prepare(): return (packed, tail_mine + to_core(tail_other))]
    ppermute x9 -> x12, waiting for transfers between devices: 24.3 us -> 20.3 us  [to_core(): return lax.ppermute(value, 'mp', pair)]
    ppermute x19 -> x23, starting transfers between devices: 36.4 us -> 39.1 us  [to_batch(): return lax.ppermute(value, 'batch', [(i, i ^ s) for i in range(nb)])]
  transfers between devices with their start and end apart: 44 -> 48, of which waited for: 21 -> 19; matrix products, arithmetic and copies ran while one was open for 2% -> 6% of each run, Pallas kernels for 39% -> 41%
where the time goes in v3:
time: 395 us; the launch traced here: 393 us
  Pallas kernels  171 us (43%)
  waiting for transfers between devices  117 us (30%)
  starting transfers between devices  56 us (14%)
  between operations  14.9 us (4%)
  local copies, waits for them, and re-layouts  14.6 us (4%)
  other arithmetic  10 us (3%)
  blocking collectives  9.09 us (2%)
    pallas_call x20, Pallas kernels, run(): call(body, grid, ins, outs, shapes, scratch, len(extra), aliases, self.co...  171 us
    ppermute x23, waiting for transfers between devices, to_batch(): return lax.ppermute(value, 'batch', [(i, i ^ s) for i in range(nb)])  62.3 us
    ppermute x23, starting transfers between devices, to_batch(): return lax.ppermute(value, 'batch', [(i, i ^ s) for i in range(nb)])  39.1 us
    ppermute x3, waiting for transfers between devices, to_y(): return lax.ppermute(value, 'mp', cross)  31.2 us
    ppermute x12, waiting for transfers between devices, to_core(): return lax.ppermute(value, 'mp', pair)  20.3 us
    cond x5, local copies, waits for them, and re-layouts  9.31 us
    all_gather x1, blocking collectives, hidden_first(): return (g, slope, lax.all_gather(stats_g, 'mp'), b, dy_near)  9.09 us
  transfers between devices with their start and end apart: 48, of which 19 were waited for; matrix products, arithmetic and copies ran while one was open for 6% of the time, Pallas kernels for 41%

profile of v3, /device:TPU:0, one launch (start us, length us, event | category | flops | bytes accessed | tf_op | source)
XLA Modules:
  0.0 392.9 jit_solution(9727280877967173622)
XLA Ops:
  17.0 18.1 %conditional.10 = (bf16[256,2048]{1,0:T(8,128)(2,1)}, bf16[256,512]{1,0:T(8,128)(2,1)}, bf16[256,512]{1,0:T(8,128)(2,1)}, bf16[256,512]{1,0:T(8,128)(2,1)}, f32[...) conditional(s32[]{:T(128)} %bitcast.9, () %tuple.101, ...), branch_computations={%region_0.1_spmd, %region_1.2_spmd} | conditional | flops 278528 | bytes 7798904 | solution.py:846
  17.0 12.7 %branch_1_fun.14 = (bf16[256,2048]{1,0:T(8,128)(2,1)}, bf16[256,512]{1,0:T(8,128)(2,1)}, bf16[256,512]{1,0:T(8,128)(2,1)}, bf16[256,512]{1,0:T(8,128)(2,1)}, f32...) custom-call(s32[3]{0:T(128)} %get-tuple-element.202.meta, ...), custom_call_target="tpu_custom_call" | custom-call | tf_op jit(solution)/shard_map/cond/branch_1_fun/pallas_call | solution.py:128
  50.7 30.2 %conditional.11 = (bf16[256,2048]{1,0:T(8,128)(2,1)}, bf16[256,2048]{1,0:T(8,128)(2,1)}, f32[128,2048]{1,0:T(8,128)}, f32[128,2048]{1,0:T(8,128)}, f32[128,2048]...) conditional(s32[]{:T(128)} %bitcast.9, () %tuple.104, (s32[3]{0:T(128)}, bf16[256,2048]{1,0:T(8,128)(2,1)}, ...), branch_computations={%region_2.3_spmd, %region_3.4_spmd} | conditional | bytes 5310544 | solution.py:846
  59.7 15.8 %collective-permute-done.1.refs_1_.refs_3_ = f32[136,2048]{1,0:T(8,128)} collective-permute-done((f32[136,2048]{1,0:T(8,128)}, f32[136,2048]{1,0:T(8,128)}, u32[]{:S(2)}, u32[]{:S(2)}) %collective-permute-start.1) | collective-permute-done | bytes 1114144 | tf_op jit(solution)/shard_map/cond/branch_1_fun/ppermute | solution.py:788
  84.8 23.0 %conditional.12 = (bf16[256,2048]{1,0:T(8,128)(2,1)}, bf16[256,2048]{1,0:T(8,128)(2,1)}, f32[4,256,4]{2,1,0:T(8,128)}, bf16[256,2048]{1,0:T(8,128)(2,1)}, f32[256,2048]{1,0:T(8,128)}) conditional(s32[]{:T(128)} %bitcast.9, () %tuple.107, (f32[128,2048]{1,0:T(8,128)}, s32[3]{0:T(128)}, bf16[2048,2048]{1,0:T(8,128)(2,1)}, f32[1,2048]{1,0:T(1,128)}, ...), branch_computations={%region_4.5_spmd, %region_5.6_spmd} | conditional | bytes 13652088 | solution.py:846
  88.6 10.1 %branch_1_fun.17 = (bf16[256,2048]{1,0:T(8,128)(2,1)}, bf16[256,2048]{1,0:T(8,128)(2,1)}, f32[256,4]{1,0:T(8,128)}, bf16[256,2048]{1,0:T(8,128)(2,1)}) custom-call(s32[3]{0:T(128)} %get-tuple-element.241.meta, f32[128,2048]{1,0:T(8,128)} %get-tuple-element.242.refs_0_, f32[128,2048]{1,0:T(8,128)} %collective-permute-done.2.refs_1_, ...), custom_call_target="tpu_custom_call" | custom-call | tf_op jit(solution)/shard_map/cond/branch_1_fun/pallas_call | solution.py:128
  98.7 9.1 %all-gather = f32[1024,4]{1,0:T(8,128)} all-gather(f32[256,4]{1,0:T(8,128)} %get-tuple-element.249), channel_id=2, replica_groups=mesh['batch'=8,'mp'=4] {'mp'}, dimensions={0}, use_global_device_ids=true | all-gather | bytes 20480 | tf_op jit(solution)/shard_map/cond/branch_1_fun/all_gather | solution.py:958
  110.7 19.4 %conditional.13 = (bf16[256,2048]{1,0:T(8,128)(2,1)}, bf16[256,2048]{1,0:T(8,128)(2,1)}, f32[256,4]{1,0:T(8,128)}, f32[8,2048]{1,0:T(8,128)}, f32[128,2048]{1,0:...) conditional(s32[]{:T(128)} %bitcast.9, () %tuple.110, (s32[3]{0:T(128)}, ...), branch_computations={%region_6.7_spmd, %region_7.8_spmd} | conditional | flops 262144 | bytes 18874592 | solution.py:846
  111.5 11.1 %branch_1_fun.18 = (bf16[256,2048]{1,0:T(8,128)(2,1)}, bf16[256,2048]{1,0:T(8,128)(2,1)}, f32[256,4]{1,0:T(8,128)}, f32[8,2048]{1,0:T(8,128)}, f32[128,2048]{1,0:T(8,128)}, /*index=5*/f32[128,2048]{1,0:T(8,128)}) custom-call(s32[3]{0:T(128)} %get-tuple-element.252.meta, bf16[256,2048]{1,0:T(8,128)(2,1)} %get-tuple-element.253.refs_0_, ...), custom_call_target="tpu_custom_call" | custom-call | tf_op jit(solution)/shard_map/cond/branch_1_fun/pallas_call | solution.py:128
  147.1 30.4 %conditional.14 = (f32[128,2176]{1,0:T(8,128)}, f32[8,2048]{1,0:T(8,128)}, f32[128,512]{1,0:T(8,128)}, f32[128,512]{1,0:T(8,128)}, f32[128,512]{1,0:T(8,128)}, /...) conditional(s32[]{:T(128)} %bitcast.9, () %tuple.114, (f32[128,2048]{1,0:T(8,128)}, ...), branch_computations={%region_8.9_spmd, %region_9.10_spmd} | conditional | bytes 10420320 | solution.py:846
  147.5 17.7 %branch_1_fun.19 = (f32[256,2048]{1,0:T(8,128)}, f32[256,2048]{1,0:T(8,128)}, f32[520,2048]{1,0:T(8,128)}) custom-call(s32[3]{0:T(128)} %get-tuple-element.269.meta, f32[256,2048]{1,0:T(8,128)} %get-tuple-element.276.refs_0_, f32[256,2048]{1,0:T(8,128)} %get-tuple-element.277.refs_1_, f32[256,4]{1,0:T(8,128)} %get-tuple-element.278.refs_2_.refs_3_, ...), custom_call_target="tpu_custom_call" | custom-call | tf_op jit(solution)/shard_map/cond/branch_1_fun/pallas_call | solution.py:128
  179.1 12.5 %conditional.15 = (f32[256,1024]{1,0:T(8,128)}, f32[256,1024]{1,0:T(8,128)}, f32[8,512]{1,0:T(8,128)}, bf16[256,2048]{1,0:T(8,128)(2,1)}, f32[128,512]{1,0:T(8,128)}) conditional(s32[]{:T(128)} %bitcast.9, () %tuple.117, (f32[128,2176]{1,0:T(8,128)}, s32[3]{0:T(128)}, f32[256,512]{1,0:T(8,128)}, f32[256,2]{1,0:T(8,128)}, f32[8,64]{1,0:T(8,128)}, ...), branch_computations={%region_10.11_spmd, %region_11.12_spmd} | conditional | bytes 5505144 | solution.py:846
  182.2 9.4 %branch_1_fun.21 = (f32[256,1024]{1,0:T(8,128)}, f32[256,1024]{1,0:T(8,128)}, f32[8,512]{1,0:T(8,128)}, bf16[256,2048]{1,0:T(8,128)(2,1)}) custom-call(s32[3]{0:T(128)} %get-tuple-element.297.meta, f32[128,2176]{1,0:T(8,128)} %get-tuple-element.298.refs_0_, f32[128,2176]{1,0:T(8,128)} %collective-permute-done.7.refs_1_, ...), custom_call_target="tpu_custom_call" | custom-call | tf_op jit(solution)/shard_map/cond/branch_1_fun/pallas_call | solution.py:128
  196.9 22.6 %conditional.16 = (f32[512,2048]{1,0:T(8,128)}, f32[512,2048]{1,0:T(8,128)}, f32[256,2048]{1,0:T(8,128)}) conditional(s32[]{:T(128)} %bitcast.9, () %tuple.120, (s32[3]{0:T(128)}, f32[128,2048]{1,0:T(8,128)}, f32[128,2048]{1,0:T(8,128)}, f32[128,2048]{1,0:T(8,128)}, f32[128,2048]{1,0:T(8,128)}, /*index=5*/f32[128,2048]{1,0:T(8,128)}, ...), branch_computations={%region_12.13_spmd, %region_13.14_spmd} | conditional | flops 524288 | bytes 31457384 | solution.py:846
  201.0 10.9 %branch_1_fun.23 = (f32[256,2048]{1,0:T(8,128)}, f32[256,2048]{1,0:T(8,128)}) custom-call(s32[3]{0:T(128)} %get-tuple-element.314.meta, f32[256,1024]{1,0:T(8,128)} %get-tuple-element.323.refs_0_, f32[256,1024]{1,0:T(8,128)} %get-tuple-element.324.refs_1_, bf16[3,2048,512]{2,1,0:T(8,128)(2,1)} %get-tuple-element.325.refs_2_, ...), custom_call_target="tpu_custom_call" | custom-call | tf_op jit(solution)/shard_map/cond/branch_1_fun/pallas_call | solution.py:128
  228.4 24.6 %shard_map.337 = (f32[256,2048]{1,0:T(8,128)}, f32[256,2048]{1,0:T(8,128)}, f32[520,2048]{1,0:T(8,128)}) custom-call(s32[3]{0:T(128)} %pad_add_fusion.meta, f32[512,2048]{1,0:T(8,128)} %get-tuple-element.585.refs_0_.refs_2_, f32[512,2048]{1,0:T(8,128)} %get-tuple-element.586.refs_1_.refs_3_, ...), custom_call_target="tpu_custom_call", output_to_operand_aliasing={{0}: (14, {}), {1}: (15, {}), {2}: (16, {})} | custom-call | flops 99999997952 | tf_op jit(solution)/shard_map/pallas_call | solution.py:128
  263.5 9.2 %collective-permute-done.37 = f32[256,2048]{1,0:T(8,128)} collective-permute-done((f32[256,2048]{1,0:T(8,128)}, f32[256,2048]{1,0:T(8,128)}, u32[]{:S(2)}, u32[]{:S(2)}) %collective-permute-start.37) | collective-permute-done | bytes 2097184 | tf_op jit(solution)/shard_map/ppermute | solution.py:788
  272.7 19.7 %conditional.17 = (f32[256,2048]{1,0:T(8,128)}, f32[8,2048]{1,0:T(8,128)}, f32[384,512]{1,0:T(8,128)}, f32[384,512]{1,0:T(8,128)}, f32[384,512]{1,0:T(8,128)}, /...) conditional(s32[]{:T(128)} %bitcast.9, () %tuple.100, (f32[2048]{0:T(1024)}, f32[2048]{0:T(1024)}, ...), branch_computations={%region_14.15_spmd, %region_15.16_spmd} | conditional | bytes 9437288 | solution.py:846
  279.5 8.6 %branch_1_fun.24 = (f32[256,2048]{1,0:T(8,128)}, f32[8,2048]{1,0:T(8,128)}) custom-call(s32[3]{0:T(128)} %get-tuple-element.330.meta, f32[256,2048]{1,0:T(8,128)} %get-tuple-element.331.refs_0_, f32[256,2048]{1,0:T(8,128)} %get-tuple-element.332.refs_1_, f32[128,2048]{1,0:T(8,128)} %get-tuple-element.333.refs_2_, ...), custom_call_target="tpu_custom_call" | custom-call | tf_op jit(solution)/shard_map/cond/branch_1_fun/pallas_call | solution.py:128
  292.4 11.5 %collective-permute-done.42.refs_16_ = f32[256,1024]{1,0:T(8,128)} collective-permute-done((f32[256,1024]{1,0:T(8,128)}, f32[256,1024]{1,0:T(8,128)}, u32[]{:S(2)}, u32[]{:S(2)}) %collective-permute-start.42) | collective-permute-done | bytes 1048608 | tf_op jit(solution)/shard_map/ppermute | solution.py:791
  303.9 17.3 %collective-permute-done.43.refs_17_ = f32[256,1024]{1,0:T(8,128)} collective-permute-done((f32[256,1024]{1,0:T(8,128)}, f32[256,1024]{1,0:T(8,128)}, u32[]{:S(2)}, u32[]{:S(2)}) %collective-permute-start.43) | collective-permute-done | bytes 1048608 | tf_op jit(solution)/shard_map/ppermute | solution.py:791
  327.9 18.7 %conditional.18 = (bf16[256,2048]{1,0:T(8,128)(2,1)}, bf16[256,2048]{1,0:T(8,128)(2,1)}, f32[8,2048]{1,0:T(8,128)}) conditional(s32[]{:T(128)} %bitcast.9, () %tuple.99, (f32[256,2048]{1,0:T(8,128)}, s32[3]{0:T(128)}, f32[8,2048]{1,0:T(8,128)}) %tuple.125), branch_computations={%region_16.17_spmd, %region_17.18_spmd} | conditional | flops 16384 | bytes 8847464 | solution.py:846
  354.8 23.9 %conditional.19 = (f32[8,2560]{1,0:T(8,128)S(1)}) conditional(s32[]{:T(128)} %bitcast.9, () %tuple.126, (f32[8,2048]{1,0:T(8,128)}, f32[8,512]{1,0:T(8,128)}) %tuple.130), branch_computations={%region_18.19_spmd, %region_19.20_spmd} | conditional | flops 61440 | bytes 1884288 | solution.py:846
  362.9 9.2 %collective-permute-done.15 = f32[8,2560]{1,0:T(8,128)S(1)} collective-permute-done((f32[8,2560]{1,0:T(8,128)S(1)}, f32[8,2560]{1,0:T(8,128)S(1)}, u32[]{:S(2)}, u32[]{:S(2)}) %collective-permute-start.15) | collective-permute-done | bytes 81952 | tf_op jit(solution)/shard_map/cond/branch_1_fun/ppermute | solution.py:791
  (132 shorter events, 200.6 us)
Async XLA Ops:
  12.4 26.5 %collective-permute-start.17 = (f32[128,2048]{1,0:T(8,128)}, f32[128,2048]{1,0:T(8,128)}, u32[]{:S(2)}, u32[]{:S(2)}) collective-permute-start(f32[128,2048]{1,0:T(8,128)} %shard_map.336), channel_id=1, source_target_pairs={{0,8},{4,12},{8,0},{12,4},{16,24},{20,28},{24,16},{28,20},{1,9},{5... | collective-permute-start | bytes 3145736 | tf_op jit(solution)/shard_map/ppermute | solution.py:791
  38.9 42.0 %collective-permute-start.19 = (f32[128,2048]{1,0:T(8,128)}, f32[128,2048]{1,0:T(8,128)}, u32[]{:S(2)}, u32[]{:S(2)}) collective-permute-start(f32[128,2048]{1,0:T(8,128)} %collective-permute-done.18), channel_id=1, source_target_pairs={{8,0},{12,4},{16,24},{20,28},{9,1},{13,5},{17,25},{21,29},{10,2},{... | collective-permute-start | bytes 3145736 | tf_op jit(solution)/shard_map/ppermute | solution.py:797
  40.2 40.7 %collective-permute-start.20 = (f32[128,2048]{1,0:T(8,128)}, f32[128,2048]{1,0:T(8,128)}, u32[]{:S(2)}, u32[]{:S(2)}) collective-permute-start(f32[128,2048]{1,0:T(8,128)} %collective-permute-done.17), channel_id=1, source_target_pairs={{8,16},{12,20},{16,8},{20,12},{9,17},{13,21},{17,9},{21,13},{10,18... | collective-permute-start | bytes 3145736 | tf_op jit(solution)/shard_map/ppermute | solution.py:794
  41.8 39.0 %collective-permute-start.21 = (f32[128,512]{1,0:T(8,128)}, f32[128,512]{1,0:T(8,128)}, u32[]{:S(2)}, u32[]{:S(2)}) collective-permute-start(f32[128,512]{1,0:T(8,128)} %get-tuple-element.514), channel_id=1, source_target_pairs={{0,8},{4,12},{8,0},{12,4},{16,24},{20,28},{24,16},{28,20},{1,9},{5... | collective-permute-start | bytes 786440 | tf_op jit(solution)/shard_map/ppermute | solution.py:791
  49.6 31.2 %collective-permute-start.22 = (f32[128,512]{1,0:T(8,128)}, f32[128,512]{1,0:T(8,128)}, u32[]{:S(2)}, u32[]{:S(2)}) collective-permute-start(f32[128,512]{1,0:T(8,128)} %get-tuple-element.515), channel_id=1, source_target_pairs={{0,12},{4,8},{8,4},{12,0},{16,28},{20,24},{24,20},{28,16},{1,13},{... | collective-permute-start | bytes 786440 | tf_op jit(solution)/shard_map/ppermute | solution.py:791
  80.9 26.9 %collective-permute-start.23 = (f32[128,2048]{1,0:T(8,128)}, f32[128,2048]{1,0:T(8,128)}, u32[]{:S(2)}, u32[]{:S(2)}) collective-permute-start(f32[128,2048]{1,0:T(8,128)} %get-tuple-element.516), channel_id=1, source_target_pairs={{0,8},{4,12},{8,0},{12,4},{16,24},{20,28},{24,16},{28,20},{1,9},{5... | collective-permute-start | bytes 3145736 | tf_op jit(solution)/shard_map/ppermute | solution.py:791
  107.8 31.7 %collective-permute-start.26 = (f32[128,2048]{1,0:T(8,128)}, f32[128,2048]{1,0:T(8,128)}, u32[]{:S(2)}, u32[]{:S(2)}) collective-permute-start(f32[128,2048]{1,0:T(8,128)} %collective-permute-done.24), channel_id=1, source_target_pairs={{8,0},{12,4},{16,24},{20,28},{9,1},{13,5},{17,25},{21,29},{10,2},{... | collective-permute-start | bytes 3145736 | tf_op jit(solution)/shard_map/ppermute | solution.py:797
  109.1 30.4 %collective-permute-start.27 = (f32[128,2048]{1,0:T(8,128)}, f32[128,2048]{1,0:T(8,128)}, u32[]{:S(2)}, u32[]{:S(2)}) collective-permute-start(f32[128,2048]{1,0:T(8,128)} %collective-permute-done.23), channel_id=1, source_target_pairs={{8,16},{12,20},{16,8},{20,12},{9,17},{13,21},{17,9},{21,13},{10,18... | collective-permute-start | bytes 3145736 | tf_op jit(solution)/shard_map/ppermute | solution.py:794
  138.2 39.3 %collective-permute-start.32 = (f32[128,2048]{1,0:T(8,128)}, f32[128,2048]{1,0:T(8,128)}, u32[]{:S(2)}, u32[]{:S(2)}) collective-permute-start(f32[128,2048]{1,0:T(8,128)} %collective-permute-done.20), channel_id=1, source_target_pairs={{8,0},{12,4},{16,24},{20,28},{9,1},{13,5},{17,25},{21,29},{10,2},{... | collective-permute-start | bytes 3145736 | tf_op jit(solution)/shard_map/ppermute | solution.py:797
  139.6 53.8 %collective-permute-start.28 = (f32[128,2048]{1,0:T(8,128)}, f32[128,2048]{1,0:T(8,128)}, u32[]{:S(2)}, u32[]{:S(2)}) collective-permute-start(f32[128,2048]{1,0:T(8,128)} %collective-permute-done.27), channel_id=1, source_target_pairs={{8,0},{12,4},{16,24},{20,28},{9,1},{13,5},{17,25},{21,29},{10,2},{... | collective-permute-start | bytes 3145736 | tf_op jit(solution)/shard_map/ppermute | solution.py:797
  140.9 36.6 %collective-permute-start.29 = (f32[256,4]{1,0:T(8,128)}, f32[256,4]{1,0:T(8,128)}, u32[]{:S(2)}, u32[]{:S(2)}) collective-permute-start(f32[256,4]{1,0:T(8,128)} %get-tuple-element.533), channel_id=1, source_target_pairs={{0,24},{4,28},{8,16},{12,20},{16,8},{20,12},{24,0},{28,4},{1,25},{... | collective-permute-start | bytes 12296 | tf_op jit(solution)/shard_map/ppermute | solution.py:791
  142.9 34.6 %collective-permute-start.30 = (f32[256,4]{1,0:T(8,128)}, f32[256,4]{1,0:T(8,128)}, u32[]{:S(2)}, u32[]{:S(2)}) collective-permute-start(f32[256,4]{1,0:T(8,128)} %get-tuple-element.533), channel_id=1, source_target_pairs={{0,16},{4,20},{8,24},{12,28},{16,0},{20,4},{24,8},{28,12},{1,17},{... | collective-permute-start | bytes 12296 | tf_op jit(solution)/shard_map/ppermute | solution.py:791
  193.4 31.1 %collective-permute-start.34 = (f32[256,1024]{1,0:T(8,128)}, f32[256,1024]{1,0:T(8,128)}, u32[]{:S(2)}, u32[]{:S(2)}) collective-permute-start(f32[256,1024]{1,0:T(8,128)} %get-tuple-element.595.refs_7_), channel_id=1, source_target_pairs={{0,4},{4,0},{8,12},{12,8},{16,20},{20,16},{24,28},{28,24},{1,5},{5... | collective-permute-start | bytes 3145736 | tf_op jit(solution)/shard_map/ppermute | solution.py:791
  194.9 29.6 %collective-permute-start.35 = (f32[256,1024]{1,0:T(8,128)}, f32[256,1024]{1,0:T(8,128)}, u32[]{:S(2)}, u32[]{:S(2)}) collective-permute-start(f32[256,1024]{1,0:T(8,128)} %get-tuple-element.595.refs_7_), channel_id=1, source_target_pairs={{0,8},{4,12},{8,0},{12,4},{16,24},{20,28},{24,16},{28,20},{1,9},{5... | collective-permute-start | bytes 3145736 | tf_op jit(solution)/shard_map/ppermute | solution.py:791
  194.9 29.6 %collective-permute-start.36 = (f32[128,512]{1,0:T(8,128)}, f32[128,512]{1,0:T(8,128)}, u32[]{:S(2)}, u32[]{:S(2)}) collective-permute-start(f32[128,512]{1,0:T(8,128)} %get-tuple-element.566), channel_id=1, source_target_pairs={{0,8},{4,12},{8,0},{12,4},{16,24},{20,28},{24,16},{28,20},{1,9},{5... | collective-permute-start | bytes 786440 | tf_op jit(solution)/shard_map/ppermute | solution.py:791
  224.5 30.0 %collective-permute-start.38 = (f32[256,1024]{1,0:T(8,128)}, f32[256,1024]{1,0:T(8,128)}, u32[]{:S(2)}, u32[]{:S(2)}) collective-permute-start(f32[256,1024]{1,0:T(8,128)} %get-tuple-element.615.refs_14_), channel_id=1, source_target_pairs={{0,4},{4,0},{8,12},{12,8},{16,20},{20,16},{24,28},{28,24},{1,5},{5... | collective-permute-start | bytes 3145736 | tf_op jit(solution)/shard_map/ppermute | solution.py:791
  225.0 29.5 %collective-permute-start.39 = (f32[256,1024]{1,0:T(8,128)}, f32[256,1024]{1,0:T(8,128)}, u32[]{:S(2)}, u32[]{:S(2)}) collective-permute-start(f32[256,1024]{1,0:T(8,128)} %collective-permute-done.34.refs_8_), channel_id=1, source_target_pairs={{0,8},{4,12},{8,0},{12,4},{16,24},{20,28},{24,16},{28,20},{1,9},{5... | collective-permute-start | bytes 3145736 | tf_op jit(solution)/shard_map/ppermute | solution.py:791
  225.4 29.1 %collective-permute-start.40 = (f32[128,512]{1,0:T(8,128)}, f32[128,512]{1,0:T(8,128)}, u32[]{:S(2)}, u32[]{:S(2)}) collective-permute-start(f32[128,512]{1,0:T(8,128)} %get-tuple-element.584), channel_id=1, source_target_pairs={{0,12},{4,8},{8,4},{12,0},{16,28},{20,24},{24,20},{28,16},{1,13},{... | collective-permute-start | bytes 786440 | tf_op jit(solution)/shard_map/ppermute | solution.py:791
  228.0 44.7 %collective-permute-start.37 = (f32[256,2048]{1,0:T(8,128)}, f32[256,2048]{1,0:T(8,128)}, u32[]{:S(2)}, u32[]{:S(2)}) collective-permute-start(f32[256,2048]{1,0:T(8,128)} %get-tuple-element.576), channel_id=1, source_target_pairs={{0,2},{1,3},{2,0},{3,1},{4,6},{5,7},{6,4},{7,5},{8,10},{9,11},{10,... | collective-permute-start | bytes 6291464 | tf_op jit(solution)/shard_map/ppermute | solution.py:788
  254.5 92.0 %collective-permute-start.41 = (f32[520,2048]{1,0:T(8,128)}, f32[520,2048]{1,0:T(8,128)}, u32[]{:S(2)}, u32[]{:S(2)}) collective-permute-start(f32[520,2048]{1,0:T(8,128)} %get-tuple-element.640), channel_id=1, source_target_pairs={{0,4},{4,0},{8,12},{12,8},{16,20},{20,16},{24,28},{28,24},{1,5},{5... | collective-permute-start | bytes 12779528 | tf_op jit(solution)/shard_map/ppermute | solution.py:791
  255.0 48.9 %collective-permute-start.42 = (f32[256,1024]{1,0:T(8,128)}, f32[256,1024]{1,0:T(8,128)}, u32[]{:S(2)}, u32[]{:S(2)}) collective-permute-start(f32[256,1024]{1,0:T(8,128)} %get-tuple-element.615.refs_14_), channel_id=1, source_target_pairs={{0,8},{4,12},{8,0},{12,4},{16,24},{20,28},{24,16},{28,20},{1,9},{5... | collective-permute-start | bytes 3145736 | tf_op jit(solution)/shard_map/ppermute | solution.py:791
  255.6 65.6 %collective-permute-start.43 = (f32[256,1024]{1,0:T(8,128)}, f32[256,1024]{1,0:T(8,128)}, u32[]{:S(2)}, u32[]{:S(2)}) collective-permute-start(f32[256,1024]{1,0:T(8,128)} %collective-permute-done.38.refs_15_), channel_id=1, source_target_pairs={{0,8},{4,12},{8,0},{12,4},{16,24},{20,28},{24,16},{28,20},{1,9},{5... | collective-permute-start | bytes 3145736 | tf_op jit(solution)/shard_map/ppermute | solution.py:791
  263.0 118.7 %collective-permute-start.44 = (f32[256,1024]{1,0:T(8,128)}, f32[256,1024]{1,0:T(8,128)}, u32[]{:S(2)}, u32[]{:S(2)}) collective-permute-start(f32[256,1024]{1,0:T(8,128)} %get-tuple-element.635), channel_id=1, source_target_pairs={{0,16},{4,20},{8,24},{12,28},{16,0},{20,4},{24,8},{28,12},{1,17},{... | collective-permute-start | bytes 3145736 | tf_op jit(solution)/shard_map/ppermute | solution.py:791
  327.9 53.8 %collective-permute-start.45 = (f32[256,1024]{1,0:T(8,128)}, f32[256,1024]{1,0:T(8,128)}, u32[]{:S(2)}, u32[]{:S(2)}) collective-permute-start(f32[256,1024]{1,0:T(8,128)} %get-tuple-element.636), channel_id=1, source_target_pairs={{0,16},{4,20},{8,24},{12,28},{16,0},{20,4},{24,8},{28,12},{1,17},{... | collective-permute-start | bytes 3145736 | tf_op jit(solution)/shard_map/ppermute | solution.py:791
  (24 other events, 294.1 us)
Sparse Core Ops, SparseCore 0:
  87.2 10.3 all-gather.3
  113.1 14.5 all-gather.5

commit v4 on v3

--- a/solution.py
+++ b/solution.py
@@ -22,6 +22,7 @@
 f32 = jnp.float32
 bf16 = jnp.bfloat16
 MIB = 1 << 20
+COVER = 10**11
 
 
 def dot(a, b, dims):
@@ -91,7 +92,7 @@
     return jax.ShapeDtypeStruct(shape, dtype)
 
 
-def call(body, grid, ins, outs, shapes, scratch=(), tokens=0, aliases=None, cover=0):
+def call(body, grid, ins, outs, shapes, scratch=(), tokens=0, cover=0):
     count = len(ins)
 
     def kernel(meta, *refs):
@@ -110,7 +111,6 @@
         compiler_params=pltpu.CompilerParams(
             dimension_semantics=("arbitrary",) * len(grid), vmem_limit_bytes=64 * MIB
         ),
-        input_output_aliases=aliases or {},
         cost_estimate=pl.CostEstimate(flops=cover, bytes_accessed=0, transcendentals=0)
         if cover
         else None,
@@ -123,9 +123,9 @@
         self.last = []
         self.cover = cover
 
-    def run(self, body, grid, ins, outs, shapes, args, scratch=(), wait=(), aliases=None):
+    def run(self, body, grid, ins, outs, shapes, args, scratch=(), wait=()):
         extra = list(wait) + self.last
-        made = call(body, grid, ins, outs, shapes, scratch, len(extra), aliases, self.cover)(
+        made = call(body, grid, ins, outs, shapes, scratch, len(extra), self.cover)(
             self.meta, *args, *extra
         )
         self.last = [made[0] if isinstance(made, (list, tuple)) else made]
@@ -256,7 +256,7 @@
             scores = mm_nt(jnp.where(mask, q[:, here], jnp.zeros_like(q[:, here])), k[:, here])
             scores = jnp.where(allowed, scores, masked_score)
             weights = jnp.exp(scores - jnp.max(scores, axis=-1, keepdims=True))
-            probs = weights / row_sum(weights)
+            probs = weights * (1.0 / row_sum(weights))
             p_out[p * 2 + h] = probs
             part = mm(
                 probs.astype(bf16), jnp.where(mask, v[:, here], jnp.zeros_like(v[:, here]))
@@ -504,10 +504,9 @@
                     copy.start()
                     copies.append((copy, low, n * rows + i * half, slot))
         for n in range(groups):
-            value = jnp.where(inner, stat_refs[2 * n][...], stat_refs[2 * n + 1][...])
-            if lower == 0:
-                value = jnp.where(meta[0] == 0, value, flip_rows(value, half))
-            stats[n * rows : (n + 1) * rows, :] = value
+            stats[n * rows : (n + 1) * rows, :] = jnp.where(
+                inner, stat_refs[2 * n][...], stat_refs[2 * n + 1][...]
+            )
         for copy, low, at, slot in copies:
             copy.wait()
             low[at : at + half, :] = buffer[slot].astype(bf16)
@@ -776,7 +775,6 @@
 def make_local(nb, nm):
     pair = [(i, i ^ 1) for i in range(nm)]
     cross = [(i, i ^ 2) for i in range(nm)]
-    pairs = [[i, i + 1] for i in range(0, nm, 2)]
     full = nb == 8
     middle_link = [(2, 4), (3, 5), (4, 2), (5, 3)]
     outward_link = [(2, 0), (3, 1), (4, 6), (5, 7)]
@@ -878,11 +876,13 @@
         sum_tile = pl.BlockSpec((8, span), rolled(1))
         gain2, shift2, bias2 = line(sub2_gain), line(sub2_shift), line(up_bias)
 
-        def pair_join(value):
-            return lax.all_gather(value, "mp", axis_index_groups=pairs, axis=0, tiled=True)
-
         dy = Order(meta).run(
-            mask_kernel, (tiles,), [tok_mine], half_tile, half_shape, (cotangent,)
+            mask_kernel,
+            (2,),
+            [pl.BlockSpec((half // 2, D), lambda i, m: (m[0] * 2 + i, 0))],
+            pl.BlockSpec((half // 2, D), rolled(0)),
+            half_shape,
+            (cotangent,),
         )
         if full:
             dy_e1, dy_m1 = to_batch(dy, 2), to_middle(dy)
@@ -945,7 +945,7 @@
 
         def hidden_first():
             order = Order(meta)
-            dy_near = pair_join(dy_e1) if full else ()
+            dy_core = to_core(dy_e1) if full else ()
             g, slope, stats_g, b = order.run(
                 first_kernel,
                 (chunks,),
@@ -955,17 +955,16 @@
                 (b_mine, to_core(b_mine), up_weight, bias2, gain2, dw),
                 [pltpu.VMEM((rows, 1), f32)] * 4,
             )
-            return g, slope, lax.all_gather(stats_g, "mp"), b, dy_near
-
-        g, slope, g_stats, b, dy_near = segment(hidden_first)
+            return g, slope, lax.all_gather(stats_g, "mp"), b, dy_core
+
+        g, slope, g_stats, b, dy_core = segment(hidden_first)
         if full:
-            b_e1, b_m1, a_got, g, dy_near = meet(b_e1, b_m1, a_got, g, dy_near)
+            b_e1, b_m1, a_got, g, dy_core = meet(b_e1, b_m1, a_got, g, dy_core)
             b_f1, b_m2 = outward(b_m1), to_middle(b_e1)
 
         def hidden_back():
             order = Order(meta)
-            b_near = pair_join(b_e1) if full else ()
-            a_core = [to_core(piece) for piece in a_got[1:]] if full else ()
+            b_core, a_core = (to_core(b_e1), [to_core(a_got[1])]) if full else ((), [])
             w, du, st, h_sum, db_mine, db_other = order.run(
                 functools.partial(back_kernel, ff_width, span),
                 (parts,),
@@ -976,14 +975,15 @@
                 [low_hidden, low_hidden, tiny4, shape_of((8, hidden)), half_shape, half_shape],
                 (g, slope, dw, g_stats, gain2, shift2, up_weight),
             )
-            return w, du, st, h_sum, db_mine + to_core(db_other), b_near, a_core
-
-        w, du, st, h_sum, db_pair, b_near, a_core = segment(hidden_back)
+            return w, du, st, h_sum, db_mine + to_core(db_other), b_core, a_core
+
+        w, du, st, h_sum, db_pair, b_core, a_core = segment(hidden_back)
         if full:
-            b_f1, b_m2, db_pair, b_near = meet(b_f1, b_m2, db_pair, b_near)
-            st_near, st_far = to_batch(st, 2), (to_batch(st, 6), to_batch(st, 4))
-            st_near, dy_m2 = meet(st_near, dy_m2)
-            dy_f2, b_f2 = outward(dy_m2), outward(b_m2)
+            b_f1, b_m2, db_pair, b_core = meet(b_f1, b_m2, db_pair, b_core)
+            st_near = to_batch(st, 2)
+            st_near, dy_m2, b_m2, st = meet(st_near, dy_m2, b_m2, st)
+            dy_f2, b_f2, st_six = outward(dy_m2), outward(b_m2), to_batch(st, 6)
+        db_cross = to_y(db_pair)
 
         def far_pass(order, b_src, d_src, starts, lower, stats_in, own, wait=()):
             size = len(starts) * rows
@@ -1015,39 +1015,31 @@
                 + [pltpu.VMEM((size, 4), f32), pltpu.VMEM((count, half, D), f32),
                    pltpu.SemaphoreType.DMA((count,))],
                 wait=wait,
-                aliases={} if fresh else {
-                    1 + len(sources) + len(stats_in) + 5 + i: i for i in range(3)},
-            )
-
-        def middle_norm_back():
-            order = Order(meta)
-            db_cross = to_y(db_pair)
-            sums = ()
-            if full:
-                sums = far_pass(
-                    order, [b_near], [dy_near], (((0, 0), (0, half)),), 0, (st_near, st_near),
-                    (w, du, h_sum, b, dyl),
-                )
-            outs = order.run(
-                functools.partial(norm2_kernel, nb),
-                (tiles,),
-                [half_tile] * 5 + [whole((8, D)), row_spec],
-                [dh_tile, whole((8, D))]
-                + [pl.BlockSpec((half // tiles, 2 * block), rolled(0))] * sends,
-                [dh_shape, shape_of((8, D))] + [shape_of((half, 2 * block))] * sends,
-                (db_pair, db_cross, h1, dy, branch, vecs, line(norm2_gain)),
-            )
-            return outs, sums
-
-        (dh_mine, d_sums, *dh_sent), sums = segment(middle_norm_back)
+            )
+
+        early = Order(meta, COVER)
         if full:
-            st_far, dy_f2, dh_mine, dh_sent = meet(st_far, dy_f2, dh_mine, dh_sent)
-            dh_got = [to_batch(dh_sent[0], 1), None, None]
+            sums = far_pass(
+                early, [b_e1, b_core], [dy_e1, dy_core], (((0, 0), (1, 0)),), 0,
+                (st_near, st_near), (w, du, h_sum, b, dyl),
+            )
+        dh_mine, d_sums, *dh_sent = early.run(
+            functools.partial(norm2_kernel, nb),
+            (tiles,),
+            [half_tile] * 5 + [whole((8, D)), row_spec],
+            [dh_tile, whole((8, D))]
+            + [pl.BlockSpec((half // tiles, 2 * block), rolled(0))] * sends,
+            [dh_shape, shape_of((8, D))] + [shape_of((half, 2 * block))] * sends,
+            (db_pair, db_cross, h1, dy, branch, vecs, line(norm2_gain)),
+        )
+        if full:
+            st_six, dy_f2, dh_mine, dh_sent, st = meet(st_six, dy_f2, dh_mine, dh_sent, st)
+            st_far = (st_six, to_batch(st, 4))
 
         def attention_back():
             order = Order(meta)
             dh_other = to_core(dh_mine)
-            a_first = to_core(a_got[0]) if full else ()
+            a_late = [to_core(a_got[0]), to_core(a_got[2])] if full else ()
             dm, dv, h_sums, dhl = order.run(
                 functools.partial(attend_back_kernel, attn_width),
                 (quads,),
@@ -1059,14 +1051,14 @@
                  table),
                 [pltpu.VMEM((rows, width), bf16)],
             )
-            return dm, dv, h_sums, dhl, a_first
-
-        dm, dv, h_sums, dhl, a_first = segment(attention_back)
-        main = Order(meta, 10**11)
+            return dm, dv, h_sums, dhl, a_late
+
+        dm, dv, h_sums, dhl, a_late = segment(attention_back)
+        main = Order(meta, COVER)
         if full:
-            b_f2, dh_got[0], dm, dv, dh_sent = meet(b_f2, dh_got[0], dm, dv, dh_sent)
+            b_f2, st_far, dm, dv, dh_sent = meet(b_f2, st_far, dm, dv, dh_sent)
             dm_x, dm_z = to_batch(dm, 1), to_batch(dm, 2)
-            dh_got[1] = to_batch(dh_sent[1], 2)
+            dh_got = [None, to_batch(dh_sent[1], 2), None]
 
         both = pl.BlockSpec((rows, span), rolled(1))
 
@@ -1104,7 +1096,7 @@
             )
             dv_x = to_batch(dv, 1)
             dm_d = to_batch(dm_x, 2)
-            dh_got[2] = to_batch(dh_sent[2], 3)
+            dh_got[0], dh_got[2] = to_batch(dh_sent[0], 1), to_batch(dh_sent[2], 3)
             da_cross = to_y(da_pair)
             sums = far_pass(
                 main, packed, packed, (((0, 0), (1, 0)), ((0, half), (1, half))), rows,
@@ -1112,10 +1104,10 @@
             )
 
         if full:
-            dv_x, dm_d, dh_got[2], sums, dm, dv = meet(dv_x, dm_d, dh_got[2], sums, dm, dv)
+            dv_x, dm_d, dh_got, sums, dm, dv = meet(dv_x, dm_d, dh_got, sums, dm, dv)
             near_got, dv_z, dv_d = to_batch(sums[2], 1), to_batch(dv, 2), to_batch(dv_x, 2)
             cut = 2 * width
-            a_join = [*a_got, a_first, *a_core]
+            a_join = [*a_got, a_late[0], *a_core, a_late[1]]
 
             def square(part, lefts, sides):
                 def piece(array, s):
@@ -1204,7 +1196,7 @@
 
         def small_sums():
             comb = jnp.concatenate([d_sums, h_sums], axis=1)
-            for s in (1, 2, 4):
+            for s in (1, 2):
                 comb = comb + to_batch(comb, s)
             return comb
 
@@ -1244,8 +1236,8 @@
             )
             d_sums, grad_up = meet(d_sums, grad_up)
             comb = segment(small_sums)
-            d_sums = lax.dynamic_slice_in_dim(comb, index * block, block, 1)
-            h_sums = comb[:, D:]
+            comb_far = to_batch(comb, 4)
+            main.last = [comb]
             grad_qkv, grad_out = main.run(
                 final_square_kernel,
                 (1,),
@@ -1254,6 +1246,9 @@
                 [shape_of((3, block, width)), shape_of((width, block))],
                 (one_own, one_got, two_own, two_got),
             )
+            comb = comb + comb_far
+            d_sums = lax.dynamic_slice_in_dim(comb, index * block, block, 1)
+            h_sums = comb[:, D:]
             grad_qkv = jnp.transpose(grad_qkv, (1, 0, 2))
         per = HD // nb
 

time: 395 us -> 380 us (0.962)
  between operations: 14.9 us -> 1.47 us
    ppermute x4, waiting for transfers between devices: 1.82 us -> 13.3 us  [outward(): return lax.ppermute(value, 'batch', outward_link)]
    ppermute x3, waiting for transfers between devices: 31.2 us -> 23.4 us  [to_y(): return lax.ppermute(value, 'mp', cross)]
    ppermute x12 -> x14, waiting for transfers between devices: 20.3 us -> 17.6 us  [to_core(): return lax.ppermute(value, 'mp', pair)]
  transfers between devices with their start and end apart: 48 -> 48, of which waited for: 19 -> 21; matrix products, arithmetic and copies ran while one was open for 6% -> 6% of each run, Pallas kernels for 41% -> 44%
where the time goes in v4:
time: 380 us; the launch traced here: 378 us
  Pallas kernels  169 us (44%)
  waiting for transfers between devices  115 us (30%)
  starting transfers between devices  55.8 us (15%)
  local copies, waits for them, and re-layouts  15.8 us (4%)
  other arithmetic  11.6 us (3%)
  blocking collectives  9.07 us (2%)
    pallas_call x20, Pallas kernels, run(): call(body, grid, ins, outs, shapes, scratch, len(extra), self.cover)  169 us
    ppermute x23, waiting for transfers between devices, to_batch(): return lax.ppermute(value, 'batch', [(i, i ^ s) for i in range(nb)])  60.9 us
    ppermute x23, starting transfers between devices, to_batch(): return lax.ppermute(value, 'batch', [(i, i ^ s) for i in range(nb)])  37.3 us
    ppermute x3, waiting for transfers between devices, to_y(): return lax.ppermute(value, 'mp', cross)  23.4 us
    ppermute x14, waiting for transfers between devices, to_core(): return lax.ppermute(value, 'mp', pair)  17.6 us
    ppermute x4, waiting for transfers between devices, outward(): return lax.ppermute(value, 'batch', outward_link)  13.3 us
    cond x5, local copies, waits for them, and re-layouts  9.16 us
    all_gather x1, blocking collectives, hidden_first(): return (g, slope, lax.all_gather(stats_g, 'mp'), b, dy_core)  9.07 us
  transfers between devices with their start and end apart: 48, of which 21 were waited for; matrix products, arithmetic and copies ran while one was open for 6% of the time, Pallas kernels for 44%

profile of v4, /device:TPU:0, one launch (start us, length us, event | category | flops | bytes accessed | tf_op | source)
XLA Modules:
  0.0 378.4 jit_solution(14670276605481061456)
XLA Ops:
  9.3 18.1 %conditional.9 = (bf16[256,2048]{1,0:T(8,128)(2,1)}, bf16[256,512]{1,0:T(8,128)(2,1)}, bf16[256,512]{1,0:T(8,128)(2,1)}, bf16[256,512]{1,0:T(8,128)(2,1)}, f32[8...) conditional(s32[]{:T(128)} %bitcast.8, () %tuple.93, ...), branch_computations={%region_0.1_spmd, %region_1.2_spmd} | conditional | flops 278528 | bytes 7798904 | solution.py:844
  9.3 12.7 %branch_1_fun.12 = (bf16[256,2048]{1,0:T(8,128)(2,1)}, bf16[256,512]{1,0:T(8,128)(2,1)}, bf16[256,512]{1,0:T(8,128)(2,1)}, bf16[256,512]{1,0:T(8,128)(2,1)}, f32...) custom-call(s32[3]{0:T(128)} %get-tuple-element.162.meta, ...), custom_call_target="tpu_custom_call" | custom-call | tf_op jit(solution)/shard_map/cond/branch_1_fun/pallas_call | solution.py:128
  34.0 7.9 %collective-permute-start.21 = (f32[128,512]{1,0:T(8,128)}, f32[128,512]{1,0:T(8,128)}, u32[]{:S(2)}, u32[]{:S(2)}) collective-permute-start(f32[128,512]{1,0:T(8,128)} %get-tuple-element.453), channel_id=1, source_target_pairs={{0,8},{4,12},{8,0},{12,4},{16,24},{20,28},{24,16},{28,20},{1,9},{5... | collective-permute-start | bytes 786440 | tf_op jit(solution)/shard_map/ppermute | solution.py:789
  42.9 30.1 %conditional.10 = (bf16[256,2048]{1,0:T(8,128)(2,1)}, bf16[256,2048]{1,0:T(8,128)(2,1)}, f32[128,2048]{1,0:T(8,128)}, f32[128,2048]{1,0:T(8,128)}, f32[128,2048]...) conditional(s32[]{:T(128)} %bitcast.8, () %tuple.96, (s32[3]{0:T(128)}, bf16[256,2048]{1,0:T(8,128)(2,1)}, ...), branch_computations={%region_2.3_spmd, %region_3.4_spmd} | conditional | bytes 5310544 | solution.py:844
  52.0 15.8 %collective-permute-done.1.refs_1_.refs_3_ = f32[136,2048]{1,0:T(8,128)} collective-permute-done((f32[136,2048]{1,0:T(8,128)}, f32[136,2048]{1,0:T(8,128)}, u32[]{:S(2)}, u32[]{:S(2)}) %collective-permute-start.1) | collective-permute-done | bytes 1114144 | tf_op jit(solution)/shard_map/cond/branch_1_fun/ppermute | solution.py:786
  76.9 21.9 %conditional.11 = (bf16[256,2048]{1,0:T(8,128)(2,1)}, bf16[256,2048]{1,0:T(8,128)(2,1)}, f32[4,256,4]{2,1,0:T(8,128)}, bf16[256,2048]{1,0:T(8,128)(2,1)}, f32[128,2048]{1,0:T(8,128)}) conditional(s32[]{:T(128)} %bitcast.8, () %tuple.99, (f32[128,2048]{1,0:T(8,128)}, s32[3]{0:T(128)}, bf16[2048,2048]{1,0:T(8,128)(2,1)}, f32[1,2048]{1,0:T(1,128)}, ...), branch_computations={%region_4.5_spmd, %region_5.6_spmd} | conditional | bytes 8409208 | solution.py:844
  79.9 9.8 %branch_1_fun.15 = (bf16[256,2048]{1,0:T(8,128)(2,1)}, bf16[256,2048]{1,0:T(8,128)(2,1)}, f32[256,4]{1,0:T(8,128)}, bf16[256,2048]{1,0:T(8,128)(2,1)}) custom-call(s32[3]{0:T(128)} %get-tuple-element.201.meta, f32[128,2048]{1,0:T(8,128)} %get-tuple-element.202.refs_0_, f32[128,2048]{1,0:T(8,128)} %collective-permute-done.2.refs_1_, ...), custom_call_target="tpu_custom_call" | custom-call | tf_op jit(solution)/shard_map/cond/branch_1_fun/pallas_call | solution.py:128
  89.7 9.1 %all-gather = f32[1024,4]{1,0:T(8,128)} all-gather(f32[256,4]{1,0:T(8,128)} %get-tuple-element.209), channel_id=2, replica_groups=mesh['batch'=8,'mp'=4] {'mp'}, dimensions={0}, use_global_device_ids=true | all-gather | bytes 20480 | tf_op jit(solution)/shard_map/cond/branch_1_fun/all_gather | solution.py:958
  101.8 16.4 %conditional.12 = (bf16[256,2048]{1,0:T(8,128)(2,1)}, bf16[256,2048]{1,0:T(8,128)(2,1)}, f32[256,4]{1,0:T(8,128)}, f32[8,2048]{1,0:T(8,128)}, f32[128,2048]{1,0:...) conditional(s32[]{:T(128)} %bitcast.8, () %tuple.92, (s32[3]{0:T(128)}, bf16[256,2048]{1,0:T(8,128)(2,1)}, ...), branch_computations={%region_6.7_spmd, %region_7.8_spmd} | conditional | flops 262144 | bytes 12583088 | solution.py:844
  101.8 11.1 %branch_1_fun.16 = (bf16[256,2048]{1,0:T(8,128)(2,1)}, bf16[256,2048]{1,0:T(8,128)(2,1)}, f32[256,4]{1,0:T(8,128)}, f32[8,2048]{1,0:T(8,128)}, f32[128,2048]{1,0:T(8,128)}, /*index=5*/f32[128,2048]{1,0:T(8,128)}) custom-call(s32[3]{0:T(128)} %get-tuple-element.212.meta, bf16[256,2048]{1,0:T(8,128)(2,1)} %get-tuple-element.213.refs_0_, ...), custom_call_target="tpu_custom_call" | custom-call | tf_op jit(solution)/shard_map/cond/branch_1_fun/pallas_call | solution.py:128
  133.9 17.5 %shard_map.337 = (f32[256,2048]{1,0:T(8,128)}, f32[256,2048]{1,0:T(8,128)}, f32[520,2048]{1,0:T(8,128)}) custom-call(s32[3]{0:T(128)} %pad_add_fusion.meta, f32[128,2048]{1,0:T(8,128)} %collective-permute-done.23.refs_0_, f32[128,2048]{1,0:T(8,128)} %get-tuple-element.480.refs_1_, f32[128,2048]{1,0:T(8,128)} %collective-permute-done.17.refs_2_, ...), custom_call_target="tpu_custom_call" | custom-call | flops 99999997952 | tf_op jit(solution)/shard_map/pallas_call | solution.py:128
  162.2 12.5 %conditional.13 = (f32[256,1024]{1,0:T(8,128)}, f32[256,1024]{1,0:T(8,128)}, f32[8,512]{1,0:T(8,128)}, bf16[256,2048]{1,0:T(8,128)(2,1)}, f32[128,512]{1,0:T(8,128)}, /*index=5*/f32[128,512]{1,0:T(8,128)}) conditional(s32[]{:T(128)} %bitcast.8, () %tuple.106, (f32[128,2176]{1,0:T(8,128)}, s32[3]{0:T(128)}, f32[256,512]{1,0:T(8,128)}, ...), branch_computations={%region_8.9_spmd, %region_9.10_spmd} | conditional | bytes 6553768 | solution.py:844
  165.3 9.4 %branch_1_fun.17 = (f32[256,1024]{1,0:T(8,128)}, f32[256,1024]{1,0:T(8,128)}, f32[8,512]{1,0:T(8,128)}, bf16[256,2048]{1,0:T(8,128)(2,1)}) custom-call(s32[3]{0:T(128)} %get-tuple-element.228.meta, f32[128,2176]{1,0:T(8,128)} %get-tuple-element.229.refs_0_, f32[128,2176]{1,0:T(8,128)} %collective-permute-done.7.refs_1_, ...), custom_call_target="tpu_custom_call" | custom-call | tf_op jit(solution)/shard_map/cond/branch_1_fun/pallas_call | solution.py:128
  174.7 9.7 %collective-permute-done.29 = f32[128,2048]{1,0:T(8,128)} collective-permute-done((f32[128,2048]{1,0:T(8,128)}, f32[128,2048]{1,0:T(8,128)}, u32[]{:S(2)}, u32[]{:S(2)}) %collective-permute-start.29) | collective-permute-done | bytes 1048608 | tf_op jit(solution)/shard_map/ppermute | solution.py:795
  187.9 22.7 %conditional.14 = (f32[512,2048]{1,0:T(8,128)}, f32[512,2048]{1,0:T(8,128)}, f32[256,2048]{1,0:T(8,128)}) conditional(s32[]{:T(128)} %bitcast.8, () %tuple.109, (s32[3]{0:T(128)}, f32[128,2048]{1,0:T(8,128)}, f32[128,2048]{1,0:T(8,128)}, f32[128,2048]{1,0:T(8,128)}, f32[128,2048]{1,0:T(8,128)}, /*index=5*/f32[128,2048]{1,0:T(8,128)}, ...), branch_computations={%region_10.11_spmd, %region_11.12_spmd} | conditional | flops 524288 | bytes 31457384 | solution.py:844
  192.1 10.9 %branch_1_fun.19 = (f32[256,2048]{1,0:T(8,128)}, f32[256,2048]{1,0:T(8,128)}) custom-call(s32[3]{0:T(128)} %get-tuple-element.246.meta, f32[256,1024]{1,0:T(8,128)} %get-tuple-element.255.refs_0_, f32[256,1024]{1,0:T(8,128)} %get-tuple-element.256.refs_1_, bf16[3,2048,512]{2,1,0:T(8,128)(2,1)} %get-tuple-element.257.refs_2_, ...), custom_call_target="tpu_custom_call" | custom-call | tf_op jit(solution)/shard_map/cond/branch_1_fun/pallas_call | solution.py:128
  220.8 24.7 %shard_map.339 = (f32[256,2048]{1,0:T(8,128)}, f32[256,2048]{1,0:T(8,128)}, f32[520,2048]{1,0:T(8,128)}) custom-call(s32[3]{0:T(128)} %pad_add_fusion.meta, f32[512,2048]{1,0:T(8,128)} %get-tuple-element.532.refs_0_.refs_2_, f32[512,2048]{1,0:T(8,128)} %get-tuple-element.533.refs_1_.refs_3_, f32[512,2048]{1,0:T(8,128)} %get-tuple-element.532.refs_0_.refs_2_, ...), custom_call_target="tpu_custom_call" | custom-call | flops 99999997952 | tf_op jit(solution)/shard_map/pallas_call | solution.py:128
  263.5 19.5 %conditional.15 = (f32[256,2048]{1,0:T(8,128)}, f32[8,2048]{1,0:T(8,128)}, f32[384,512]{1,0:T(8,128)}, f32[384,512]{1,0:T(8,128)}, f32[384,512]{1,0:T(8,128)}, /...) conditional(s32[]{:T(128)} %bitcast.8, () %tuple.91, (f32[2048]{0:T(1024)}, f32[2048]{0:T(1024)}, ...), branch_computations={%region_12.13_spmd, %region_13.14_spmd} | conditional | bytes 9437288 | solution.py:844
  270.3 8.5 %branch_1_fun.20 = (f32[256,2048]{1,0:T(8,128)}, f32[8,2048]{1,0:T(8,128)}) custom-call(s32[3]{0:T(128)} %get-tuple-element.262.meta, f32[256,2048]{1,0:T(8,128)} %get-tuple-element.263.refs_0_, f32[256,2048]{1,0:T(8,128)} %get-tuple-element.264.refs_1_, f32[128,2048]{1,0:T(8,128)} %get-tuple-element.265.refs_2_, ...), custom_call_target="tpu_custom_call" | custom-call | tf_op jit(solution)/shard_map/cond/branch_1_fun/pallas_call | solution.py:128
  283.0 16.3 %collective-permute-done.43.refs_16_ = f32[256,1024]{1,0:T(8,128)} collective-permute-done((f32[256,1024]{1,0:T(8,128)}, f32[256,1024]{1,0:T(8,128)}, u32[]{:S(2)}, u32[]{:S(2)}) %collective-permute-start.43) | collective-permute-done | bytes 1048608 | tf_op jit(solution)/shard_map/ppermute | solution.py:789
  299.3 17.3 %collective-permute-done.44.refs_17_ = f32[256,1024]{1,0:T(8,128)} collective-permute-done((f32[256,1024]{1,0:T(8,128)}, f32[256,1024]{1,0:T(8,128)}, u32[]{:S(2)}, u32[]{:S(2)}) %collective-permute-start.44) | collective-permute-done | bytes 1048608 | tf_op jit(solution)/shard_map/ppermute | solution.py:789
  323.3 18.6 %conditional.16 = (bf16[256,2048]{1,0:T(8,128)(2,1)}, bf16[256,2048]{1,0:T(8,128)(2,1)}, f32[8,2048]{1,0:T(8,128)}) conditional(s32[]{:T(128)} %bitcast.8, () %tuple.90, (f32[256,2048]{1,0:T(8,128)}, s32[3]{0:T(128)}, f32[8,2048]{1,0:T(8,128)}) %tuple.114), branch_computations={%region_14.15_spmd, %region_15.16_spmd} | conditional | flops 16384 | bytes 8847464 | solution.py:844
  350.9 17.5 %conditional.17 = (f32[8,2560]{1,0:T(8,128)}) conditional(s32[]{:T(128)} %bitcast.8, () %tuple.115, (f32[8,2048]{1,0:T(8,128)}, f32[8,512]{1,0:T(8,128)}) %tuple.119), branch_computations={%region_16.17_spmd, %region_17.18_spmd} | conditional | flops 40960 | bytes 1310808 | solution.py:844
  359.2 8.5 %collective-permute-done.16 = f32[8,2560]{1,0:T(8,128)S(1)} collective-permute-done((f32[8,2560]{1,0:T(8,128)S(1)}, f32[8,2560]{1,0:T(8,128)S(1)}, u32[]{:S(2)}, u32[]{:S(2)}) %collective-permute-start.16) | collective-permute-done | bytes 81952 | tf_op jit(solution)/shard_map/cond/branch_1_fun/ppermute | solution.py:789
  (129 shorter events, 187.7 us)
Async XLA Ops:
  4.6 26.5 %collective-permute-start.17 = (f32[128,2048]{1,0:T(8,128)}, f32[128,2048]{1,0:T(8,128)}, u32[]{:S(2)}, u32[]{:S(2)}) collective-permute-start(f32[128,2048]{1,0:T(8,128)} %shard_map.336.refs_3_), channel_id=1, source_target_pairs={{0,8},{4,12},{8,0},{12,4},{16,24},{20,28},{24,16},{28,20},{1,9},{5... | collective-permute-start | bytes 3145736 | tf_op jit(solution)/shard_map/ppermute | solution.py:789
  31.1 41.9 %collective-permute-start.19 = (f32[128,2048]{1,0:T(8,128)}, f32[128,2048]{1,0:T(8,128)}, u32[]{:S(2)}, u32[]{:S(2)}) collective-permute-start(f32[128,2048]{1,0:T(8,128)} %collective-permute-done.18), channel_id=1, source_target_pairs={{8,0},{12,4},{16,24},{20,28},{9,1},{13,5},{17,25},{21,29},{10,2},{... | collective-permute-start | bytes 3145736 | tf_op jit(solution)/shard_map/ppermute | solution.py:795
  32.4 40.6 %collective-permute-start.20 = (f32[128,2048]{1,0:T(8,128)}, f32[128,2048]{1,0:T(8,128)}, u32[]{:S(2)}, u32[]{:S(2)}) collective-permute-start(f32[128,2048]{1,0:T(8,128)} %collective-permute-done.17.refs_2_), channel_id=1, source_target_pairs={{8,16},{12,20},{16,8},{20,12},{9,17},{13,21},{17,9},{21,13},{10,18... | collective-permute-start | bytes 3145736 | tf_op jit(solution)/shard_map/ppermute | solution.py:792
  34.0 39.0 %collective-permute-start.21 = (f32[128,512]{1,0:T(8,128)}, f32[128,512]{1,0:T(8,128)}, u32[]{:S(2)}, u32[]{:S(2)}) collective-permute-start(f32[128,512]{1,0:T(8,128)} %get-tuple-element.453), channel_id=1, source_target_pairs={{0,8},{4,12},{8,0},{12,4},{16,24},{20,28},{24,16},{28,20},{1,9},{5... | collective-permute-start | bytes 786440 | tf_op jit(solution)/shard_map/ppermute | solution.py:789
  41.9 31.1 %collective-permute-start.22 = (f32[128,512]{1,0:T(8,128)}, f32[128,512]{1,0:T(8,128)}, u32[]{:S(2)}, u32[]{:S(2)}) collective-permute-start(f32[128,512]{1,0:T(8,128)} %get-tuple-element.454), channel_id=1, source_target_pairs={{0,12},{4,8},{8,4},{12,0},{16,28},{20,24},{24,20},{28,16},{1,13},{... | collective-permute-start | bytes 786440 | tf_op jit(solution)/shard_map/ppermute | solution.py:789
  73.0 25.8 %collective-permute-start.23 = (f32[128,2048]{1,0:T(8,128)}, f32[128,2048]{1,0:T(8,128)}, u32[]{:S(2)}, u32[]{:S(2)}) collective-permute-start(f32[128,2048]{1,0:T(8,128)} %get-tuple-element.455), channel_id=1, source_target_pairs={{0,8},{4,12},{8,0},{12,4},{16,24},{20,28},{24,16},{28,20},{1,9},{5... | collective-permute-start | bytes 3145736 | tf_op jit(solution)/shard_map/ppermute | solution.py:789
  98.8 28.2 %collective-permute-start.27 = (f32[128,2048]{1,0:T(8,128)}, f32[128,2048]{1,0:T(8,128)}, u32[]{:S(2)}, u32[]{:S(2)}) collective-permute-start(f32[128,2048]{1,0:T(8,128)} %collective-permute-done.24), channel_id=1, source_target_pairs={{8,0},{12,4},{16,24},{20,28},{9,1},{13,5},{17,25},{21,29},{10,2},{... | collective-permute-start | bytes 3145736 | tf_op jit(solution)/shard_map/ppermute | solution.py:795
  100.1 26.9 %collective-permute-start.28 = (f32[128,2048]{1,0:T(8,128)}, f32[128,2048]{1,0:T(8,128)}, u32[]{:S(2)}, u32[]{:S(2)}) collective-permute-start(f32[128,2048]{1,0:T(8,128)} %collective-permute-done.23.refs_0_), channel_id=1, source_target_pairs={{8,16},{12,20},{16,8},{20,12},{9,17},{13,21},{17,9},{21,13},{10,18... | collective-permute-start | bytes 3145736 | tf_op jit(solution)/shard_map/ppermute | solution.py:792
  129.8 30.8 %collective-permute-start.31 = (f32[128,2048]{1,0:T(8,128)}, f32[128,2048]{1,0:T(8,128)}, u32[]{:S(2)}, u32[]{:S(2)}) collective-permute-start(f32[128,2048]{1,0:T(8,128)} %collective-permute-done.20), channel_id=1, source_target_pairs={{8,0},{12,4},{16,24},{20,28},{9,1},{13,5},{17,25},{21,29},{10,2},{... | collective-permute-start | bytes 3145736 | tf_op jit(solution)/shard_map/ppermute | solution.py:795
  131.1 29.2 %collective-permute-start.30 = (f32[256,4]{1,0:T(8,128)}, f32[256,4]{1,0:T(8,128)}, u32[]{:S(2)}, u32[]{:S(2)}) collective-permute-start(f32[256,4]{1,0:T(8,128)} %get-tuple-element.494), channel_id=1, source_target_pairs={{0,24},{4,28},{8,16},{12,20},{16,8},{20,12},{24,0},{28,4},{1,25},{... | collective-permute-start | bytes 12296 | tf_op jit(solution)/shard_map/ppermute | solution.py:789
  132.6 51.8 %collective-permute-start.29 = (f32[128,2048]{1,0:T(8,128)}, f32[128,2048]{1,0:T(8,128)}, u32[]{:S(2)}, u32[]{:S(2)}) collective-permute-start(f32[128,2048]{1,0:T(8,128)} %collective-permute-done.28), channel_id=1, source_target_pairs={{8,0},{12,4},{16,24},{20,28},{9,1},{13,5},{17,25},{21,29},{10,2},{... | collective-permute-start | bytes 3145736 | tf_op jit(solution)/shard_map/ppermute | solution.py:795
  184.4 30.9 %collective-permute-start.34 = (f32[256,1024]{1,0:T(8,128)}, f32[256,1024]{1,0:T(8,128)}, u32[]{:S(2)}, u32[]{:S(2)}) collective-permute-start(f32[256,1024]{1,0:T(8,128)} %get-tuple-element.541.refs_7_), channel_id=1, source_target_pairs={{0,4},{4,0},{8,12},{12,8},{16,20},{20,16},{24,28},{28,24},{1,5},{5... | collective-permute-start | bytes 3145736 | tf_op jit(solution)/shard_map/ppermute | solution.py:789
  185.9 29.4 %collective-permute-start.35 = (f32[256,1024]{1,0:T(8,128)}, f32[256,1024]{1,0:T(8,128)}, u32[]{:S(2)}, u32[]{:S(2)}) collective-permute-start(f32[256,1024]{1,0:T(8,128)} %get-tuple-element.541.refs_7_), channel_id=1, source_target_pairs={{0,8},{4,12},{8,0},{12,4},{16,24},{20,28},{24,16},{28,20},{1,9},{5... | collective-permute-start | bytes 3145736 | tf_op jit(solution)/shard_map/ppermute | solution.py:789
  185.9 29.4 %collective-permute-start.36 = (f32[128,512]{1,0:T(8,128)}, f32[128,512]{1,0:T(8,128)}, u32[]{:S(2)}, u32[]{:S(2)}) collective-permute-start(f32[128,512]{1,0:T(8,128)} %get-tuple-element.510), channel_id=1, source_target_pairs={{0,8},{4,12},{8,0},{12,4},{16,24},{20,28},{24,16},{28,20},{1,9},{5... | collective-permute-start | bytes 786440 | tf_op jit(solution)/shard_map/ppermute | solution.py:789
  215.3 34.5 %collective-permute-start.38 = (f32[256,1024]{1,0:T(8,128)}, f32[256,1024]{1,0:T(8,128)}, u32[]{:S(2)}, u32[]{:S(2)}) collective-permute-start(f32[256,1024]{1,0:T(8,128)} %get-tuple-element.561.refs_14_), channel_id=1, source_target_pairs={{0,4},{4,0},{8,12},{12,8},{16,20},{20,16},{24,28},{28,24},{1,5},{5... | collective-permute-start | bytes 3145736 | tf_op jit(solution)/shard_map/ppermute | solution.py:789
  215.8 34.0 %collective-permute-start.39 = (f32[256,1024]{1,0:T(8,128)}, f32[256,1024]{1,0:T(8,128)}, u32[]{:S(2)}, u32[]{:S(2)}) collective-permute-start(f32[256,1024]{1,0:T(8,128)} %collective-permute-done.34.refs_8_), channel_id=1, source_target_pairs={{0,8},{4,12},{8,0},{12,4},{16,24},{20,28},{24,16},{28,20},{1,9},{5... | collective-permute-start | bytes 3145736 | tf_op jit(solution)/shard_map/ppermute | solution.py:789
  216.1 33.6 %collective-permute-start.40 = (f32[128,512]{1,0:T(8,128)}, f32[128,512]{1,0:T(8,128)}, u32[]{:S(2)}, u32[]{:S(2)}) collective-permute-start(f32[128,512]{1,0:T(8,128)} %get-tuple-element.529), channel_id=1, source_target_pairs={{0,4},{4,0},{8,12},{12,8},{16,20},{20,16},{24,28},{28,24},{1,5},{5... | collective-permute-start | bytes 786440 | tf_op jit(solution)/shard_map/ppermute | solution.py:789
  217.6 32.1 %collective-permute-start.41 = (f32[128,512]{1,0:T(8,128)}, f32[128,512]{1,0:T(8,128)}, u32[]{:S(2)}, u32[]{:S(2)}) collective-permute-start(f32[128,512]{1,0:T(8,128)} %get-tuple-element.531), channel_id=1, source_target_pairs={{0,12},{4,8},{8,4},{12,0},{16,28},{20,24},{24,20},{28,16},{1,13},{... | collective-permute-start | bytes 786440 | tf_op jit(solution)/shard_map/ppermute | solution.py:789
  219.3 44.2 %collective-permute-start.37 = (f32[256,2048]{1,0:T(8,128)}, f32[256,2048]{1,0:T(8,128)}, u32[]{:S(2)}, u32[]{:S(2)}) collective-permute-start(f32[256,2048]{1,0:T(8,128)} %get-tuple-element.521), channel_id=1, source_target_pairs={{0,2},{1,3},{2,0},{3,1},{4,6},{5,7},{6,4},{7,5},{8,10},{9,11},{10,... | collective-permute-start | bytes 6291464 | tf_op jit(solution)/shard_map/ppermute | solution.py:786
  249.8 92.2 %collective-permute-start.42 = (f32[520,2048]{1,0:T(8,128)}, f32[520,2048]{1,0:T(8,128)}, u32[]{:S(2)}, u32[]{:S(2)}) collective-permute-start(f32[520,2048]{1,0:T(8,128)} %get-tuple-element.586), channel_id=1, source_target_pairs={{0,4},{4,0},{8,12},{12,8},{16,20},{20,16},{24,28},{28,24},{1,5},{5... | collective-permute-start | bytes 12779528 | tf_op jit(solution)/shard_map/ppermute | solution.py:789
  250.4 48.9 %collective-permute-start.43 = (f32[256,1024]{1,0:T(8,128)}, f32[256,1024]{1,0:T(8,128)}, u32[]{:S(2)}, u32[]{:S(2)}) collective-permute-start(f32[256,1024]{1,0:T(8,128)} %get-tuple-element.561.refs_14_), channel_id=1, source_target_pairs={{0,8},{4,12},{8,0},{12,4},{16,24},{20,28},{24,16},{28,20},{1,9},{5... | collective-permute-start | bytes 3145736 | tf_op jit(solution)/shard_map/ppermute | solution.py:789
  250.7 65.9 %collective-permute-start.44 = (f32[256,1024]{1,0:T(8,128)}, f32[256,1024]{1,0:T(8,128)}, u32[]{:S(2)}, u32[]{:S(2)}) collective-permute-start(f32[256,1024]{1,0:T(8,128)} %collective-permute-done.38.refs_15_), channel_id=1, source_target_pairs={{0,8},{4,12},{8,0},{12,4},{16,24},{20,28},{24,16},{28,20},{1,9},{5... | collective-permute-start | bytes 3145736 | tf_op jit(solution)/shard_map/ppermute | solution.py:789
  258.3 110.3 %collective-permute-start.46 = (f32[256,1024]{1,0:T(8,128)}, f32[256,1024]{1,0:T(8,128)}, u32[]{:S(2)}, u32[]{:S(2)}) collective-permute-start(f32[256,1024]{1,0:T(8,128)} %get-tuple-element.581), channel_id=1, source_target_pairs={{0,16},{4,20},{8,24},{12,28},{16,0},{20,4},{24,8},{28,12},{1,17},{... | collective-permute-start | bytes 3145736 | tf_op jit(solution)/shard_map/ppermute | solution.py:789
  323.3 45.3 %collective-permute-start.47 = (f32[256,1024]{1,0:T(8,128)}, f32[256,1024]{1,0:T(8,128)}, u32[]{:S(2)}, u32[]{:S(2)}) collective-permute-start(f32[256,1024]{1,0:T(8,128)} %get-tuple-element.582), channel_id=1, source_target_pairs={{0,16},{4,20},{8,24},{12,28},{16,0},{20,4},{24,8},{28,12},{1,17},{... | collective-permute-start | bytes 3145736 | tf_op jit(solution)/shard_map/ppermute | solution.py:789
  (24 other events, 290.5 us)

commit v5 on v4

--- a/solution.py
+++ b/solution.py
@@ -581,7 +581,7 @@
 
 
 def attend_back_kernel(attn_width, meta, dh_mine, dh_other, o_all, stats, sub_gain, sub_shift, out_w, q_all,
-                       k_all, v_all, probs_all, table, dm_out, dv_out, sum_out, dhl_out, do_all):
+                       k_all, v_all, probs_all, table, dm_out, z_out, sum_out, dhl_out, do_all):
     rows, width = o_all.shape
     half = rows // 2
     full = out_w.shape[1]
@@ -605,7 +605,7 @@
             - unit * (sums[:, 1:2] * (1.0 / attn_width))
         )
         do_all[...] = do.astype(bf16)
-        dv_out[:, width:] = unit * gain_row + spread(sub_shift, heads)
+        z_out[...] = unit * gain_row + spread(sub_shift, heads)
         sum_out[0:1, :] = jnp.sum(dz * unit, axis=0, keepdims=True)
         sum_out[1:2, :] = jnp.sum(dz, axis=0, keepdims=True)
         sum_out[5:8, :] = jnp.zeros((3, width), f32)
@@ -651,23 +651,19 @@
                 s = jnp.concatenate([table[2 * j + 1, at, :]] * 2, axis=1)
                 parts.append(grad[here] * c - flipped[here] * s)
             grad = jnp.concatenate(parts, axis=0)
-        if j < 2:
-            dm_out[:, pl.ds(pl.multiple_of(j * width + step * QUAD, QUAD), QUAD)] = grad
-        else:
-            dv_out[:, quad] = grad
+        dm_out[:, pl.ds(pl.multiple_of(j * width + step * QUAD, QUAD), QUAD)] = grad
         sum_out[2 + j : 3 + j, quad] = jnp.sum(
             grad.astype(bf16).astype(f32), axis=0, keepdims=True
         )
 
 
-def tail_kernel(meta, dm, dv, weight, w, down_w, mine, other, low):
+def tail_kernel(meta, dm, weight, w, down_w, mine, other, low):
     half = mine.shape[0] // 2
     width = weight.shape[2]
 
     @pl.when(pl.program_id(0) == 0)
     def _():
-        low[:, 0 : 2 * width] = dm[...].astype(bf16)
-        low[:, 2 * width :] = dv[...].astype(bf16)
+        low[...] = dm[...].astype(bf16)
 
     total = mm_nt(low[:, 0:width], weight[0])
     for j in (1, 2):
@@ -731,40 +727,29 @@
         store.wait()
 
 
-def square_kernel(nb, part, meta, *refs):
-    lists, rest = refs[: 7 * (part + 1)], refs[7 * (part + 1) :]
-    sides, (own_out, mirror_out), lows = rest[:4], rest[4:6], rest[6:]
-    right = lows[-1]
-    rows, full = lists[0].shape
+def square_kernel(nb, meta, own, *refs):
+    mine, other, sides, (own_out, mirror_out, left, right) = refs[:3], refs[3:6], refs[6:10], refs[10:]
+    rows, full = own.shape
     half, block = rows // 2, full // nb
-    width = own_out.shape[1] // 2
-    for n, low in enumerate(lows[:-1]):
-        own, mine, other = lists[7 * n], lists[7 * n + 1 : 7 * n + 4], lists[7 * n + 4 : 7 * n + 7]
-        for which, at in ((0, meta[2]), (1, meta[2] ^ 4)):
-            cols = pl.ds(pl.multiple_of(at * block, block), block)
-            low[0:rows, which * block : (which + 1) * block] = own[:, cols]
-        for s in range(3):
-            here = rows * (s + 1)
-            low[here : here + half, :] = mine[s][...].astype(bf16)
-            low[here + half : here + rows, :] = other[s][...].astype(bf16)
+    for part, at in ((0, meta[2]), (1, meta[2] ^ 4)):
+        cols = pl.ds(pl.multiple_of(at * block, block), block)
+        left[0:rows, part * block : (part + 1) * block] = own[:, cols]
+    for s in range(3):
+        here = rows * (s + 1)
+        left[here : here + half, :] = mine[s][...].astype(bf16)
+        left[here + half : here + rows, :] = other[s][...].astype(bf16)
     for s in range(4):
         right[rows * s : rows * (s + 1), :] = sides[s][...].astype(bf16)
-    for out, first in ((mirror_out, block), (own_out, 0)):
-        left = lows[0][:, first : first + block]
-        if part == 0:
-            out[...] = mm_tn(left, right[...])
-        else:
-            out[:, 0:width] = mm_tn(left, right[:, 0:width])
-            out[:, width:] = mm_tn(lows[1][:, first : first + block], right[:, width:])
+    for out, part in ((mirror_out, block), (own_out, 0)):
+        out[...] = mm_tn(left[:, part : part + block], right[...])
 
 
 def final_square_kernel(meta, one_own, one_got, two_own, two_got, m_out, o_out):
     width = m_out.shape[2]
-    for j in range(2):
+    for j in range(3):
         cols = slice(j * width, (j + 1) * width)
         m_out[j] = one_own[:, cols] + one_got[:, cols]
-    m_out[2] = two_own[:, 0:width] + two_got[:, 0:width]
-    o_out[...] = (two_own[:, width:] + two_got[:, width:]).T
+    o_out[...] = (two_own[...] + two_got[...]).T
 
 
 def final_hidden_kernel(meta, up_own, up_got, down_own, down_got, up_out, down_out):
@@ -1045,8 +1030,8 @@
                 (quads,),
                 [dh_spec, dh_spec, wide_spec, whole((rows, 2)), whole((heads, HD)),
                  whole((heads, HD)), whole((width, D)), quad, quad, quad, probs_spec, table_spec],
-                [whole((rows, 2 * width))] * 2 + [whole((8, width)), whole((rows, D))],
-                [shape_of((rows, 2 * width))] * 2 + [shape_of((8, width)), low_rows],
+                [whole((rows, 3 * width)), wide_spec, whole((8, width)), whole((rows, D))],
+                [shape_of((rows, 3 * width)), wide_shape, shape_of((8, width)), low_rows],
                 (dh_mine, dh_other, o, stats, sub1_gain, sub1_shift, out_weight, q, k, v, probs,
                  table),
                 [pltpu.VMEM((rows, width), bf16)],
@@ -1079,24 +1064,22 @@
             tail_mine, tail_other = order.run(
                 tail_kernel,
                 (parts,),
-                [whole((rows, 2 * width)), pl.BlockSpec((rows, width), lambda i, *_: (0, 0)),
+                [whole((rows, 3 * width)),
                  pl.BlockSpec((3, span, width), lambda i, *_: (0, i, 0)),
                  whole((rows, hidden)), pl.BlockSpec((hidden, span), rolled(1))],
                 [both] * 2,
                 [shape_of((rows, D))] * 2,
-                (dm, dv, weight, w, down_weight),
+                (dm, weight, w, down_weight),
                 [pltpu.VMEM((rows, 3 * width), bf16)],
             )
             return packed, tail_mine + to_core(tail_other)
 
         packed, da_pair = segment(prepare)
         if full:
-            dm_x, dm_z, dh_got[1], packed, dv, dh_sent, da_pair = meet(
-                dm_x, dm_z, dh_got[1], packed, dv, dh_sent, da_pair
-            )
+            dm_x, dm_z, packed, dv, dh_sent, da_pair = meet(dm_x, dm_z, packed, dv, dh_sent, da_pair)
             dv_x = to_batch(dv, 1)
             dm_d = to_batch(dm_x, 2)
-            dh_got[0], dh_got[2] = to_batch(dh_sent[0], 1), to_batch(dh_sent[2], 3)
+            dh_got[0] = to_batch(dh_sent[0], 1)
             da_cross = to_y(da_pair)
             sums = far_pass(
                 main, packed, packed, (((0, 0), (1, 0)), ((0, half), (1, half))), rows,
@@ -1104,32 +1087,33 @@
             )
 
         if full:
-            dv_x, dm_d, dh_got, sums, dm, dv = meet(dv_x, dm_d, dh_got, sums, dm, dv)
-            near_got, dv_z, dv_d = to_batch(sums[2], 1), to_batch(dv, 2), to_batch(dv_x, 2)
-            cut = 2 * width
+            dv_x, sums = meet(dv_x, sums)
+            near_got = to_batch(sums[2], 1)
+            dm_d, dh_got[0], dh_got[1], dm, dv, dv_x, dh_sent = meet(
+                dm_d, dh_got[0], dh_got[1], dm, dv, dv_x, dh_sent
+            )
+            dh_got[2] = to_batch(dh_sent[2], 3)
+            dv_z, dv_d = to_batch(dv, 2), to_batch(dv_x, 2)
             a_join = [*a_got, a_late[0], *a_core, a_late[1]]
 
-            def square(part, lefts, sides):
+            def square(left, got, sides):
                 def piece(array, s):
                     at = s if array.shape[0] > half else 0
                     return pl.BlockSpec((half, 2 * block), lambda i, *_: (at, 0))
 
-                specs = []
-                for _, got in lefts:
-                    specs += [whole((rows, D))] + [piece(got[i], i % 3) for i in range(6)]
-                lists = [array for own, got in lefts for array in (own, *got)]
+                cut = sides[0].shape[1]
                 return main.run(
-                    functools.partial(square_kernel, nb, part),
+                    functools.partial(square_kernel, nb),
                     (1,),
-                    specs + [whole((rows, cut))] * 4,
+                    [whole((rows, D))] + [piece(got[i], i % 3) for i in range(6)]
+                    + [whole((rows, cut))] * 4,
                     [whole((block, cut))] * 2,
                     [shape_of((block, cut))] * 2,
-                    (*lists, *sides),
-                    [pltpu.VMEM((4 * rows, 2 * block), bf16)] * len(lefts)
-                    + [pltpu.VMEM((4 * rows, cut), bf16)],
+                    (left, *got, *sides),
+                    [pltpu.VMEM((4 * rows, 2 * block), bf16), pltpu.VMEM((4 * rows, cut), bf16)],
                 )
 
-            one_own, one_mirror = square(0, [(a, a_join)], [dm, dm_x, dm_z, dm_d])
+            one_own, one_mirror = square(a, a_join, [dm, dm_x, dm_z, dm_d])
             one_got = to_batch(one_mirror, 4)
         else:
             da_cross = to_y(da_pair)
@@ -1169,9 +1153,7 @@
         (mine, d_sums), dh_join = segment(input_norm_back)
         if full:
             dv_z, dv_d, dh_join = meet(dv_z, dv_d, dh_join)
-            two_own, two_mirror = square(
-                1, [(a, a_join), (dhl, dh_join)], [dv, dv_x, dv_z, dv_d]
-            )
+            two_own, two_mirror = square(dhl, dh_join, [dv, dv_x, dv_z, dv_d])
             two_got = to_batch(two_mirror, 4)
 
         def place():
@@ -1194,12 +1176,6 @@
 
         result, tokens_grad, d_sums = segment(place)
 
-        def small_sums():
-            comb = jnp.concatenate([d_sums, h_sums], axis=1)
-            for s in (1, 2):
-                comb = comb + to_batch(comb, s)
-            return comb
-
         lanes = hidden // 128
         per = 128 // nb
         if not full:
@@ -1210,8 +1186,7 @@
             d_sums = scatter(d_sums, 1)
             h_sums = lax.psum(h_sums, "batch")
             h_parts = scatter(h_sum[:3].reshape(3, lanes, 128), 2)
-            dm_low = jnp.concatenate([dm, dv[:, :width]], axis=1).astype(bf16)
-            z = dv[:, width:]
+            dm_low, z = dm.astype(bf16), dv
             grad_qkv = scatter(
                 jnp.stack([mm_tn(a, dm_low[:, j * width : (j + 1) * width]) for j in range(3)], 1), 0
             )
@@ -1219,7 +1194,8 @@
             grad_up = scatter(mm_tn(b, du), 0)
             grad_down = scatter(mm_tn(w, dyl), 1)
         else:
-            near_got, sums, d_sums = meet(near_got, sums, d_sums)
+            comb = jnp.concatenate([d_sums, h_sums], axis=1)
+            comb_x = to_batch(comb, 1)
             h_parts = (sums[2][2 * block :] + near_got[2 * block :])[:3]
             h_parts = lax.dynamic_slice_in_dim(
                 h_parts.reshape(3, lanes, 128), index * per, per, 2
@@ -1234,14 +1210,19 @@
                 [shape_of((block, hidden)), shape_of((hidden, block))],
                 (sums[0], near_got, sums[1], near_got),
             )
-            d_sums, grad_up = meet(d_sums, grad_up)
+            comb, comb_x, grad_up = meet(comb, comb_x, grad_up)
+
+            def small_sums():
+                total = comb + comb_x
+                return total + to_batch(total, 2)
+
             comb = segment(small_sums)
             comb_far = to_batch(comb, 4)
             main.last = [comb]
             grad_qkv, grad_out = main.run(
                 final_square_kernel,
                 (1,),
-                [whole((block, cut))] * 4,
+                [whole((block, 3 * width))] * 2 + [whole((block, width))] * 2,
                 [whole((3, block, width)), whole((width, block))],
                 [shape_of((3, block, width)), shape_of((width, block))],
                 (one_own, one_got, two_own, two_got),

time: 380 us -> 377 us (level)
  waiting for transfers between devices: 115 us -> 108 us
  local copies, waits for them, and re-layouts: 15.8 us -> 20.5 us
    ppermute x3, waiting for transfers between devices: 23.4 us -> 18.6 us  [to_y(): return lax.ppermute(value, 'mp', cross)]
    cond x5 -> x10, local copies, waits for them, and re-layouts: 9.16 us -> 11.1 us
  transfers between devices with their start and end apart: 48 -> 48, of which waited for: 21 -> 22; matrix products, arithmetic and copies ran while one was open for 6% -> 7% of each run, Pallas kernels for 44% -> 44%
where the time goes in v5:
time: 377 us; the launch traced here: 375 us
  Pallas kernels  168 us (45%)
  waiting for transfers between devices  108 us (29%)
  starting transfers between devices  54.4 us (14%)
  local copies, waits for them, and re-layouts  20.5 us (5%)
  other arithmetic  13.4 us (4%)
  blocking collectives  9.06 us (2%)
    pallas_call x20, Pallas kernels, run(): call(body, grid, ins, outs, shapes, scratch, len(extra), self.cover)  168 us
    ppermute x23, waiting for transfers between devices, to_batch(): return lax.ppermute(value, 'batch', [(i, i ^ s) for i in range(nb)])  58.1 us
    ppermute x23, starting transfers between devices, to_batch(): return lax.ppermute(value, 'batch', [(i, i ^ s) for i in range(nb)])  35.9 us
    ppermute x3, waiting for transfers between devices, to_y(): return lax.ppermute(value, 'mp', cross)  18.6 us
    ppermute x14, waiting for transfers between devices, to_core(): return lax.ppermute(value, 'mp', pair)  17.6 us
    ppermute x4, waiting for transfers between devices, outward(): return lax.ppermute(value, 'batch', outward_link)  13.6 us
    cond x10, local copies, waits for them, and re-layouts  11.1 us
    all_gather x1, blocking collectives, hidden_first(): return (g, slope, lax.all_gather(stats_g, 'mp'), b, dy_core)  9.06 us
  transfers between devices with their start and end apart: 48, of which 22 were waited for; matrix products, arithmetic and copies ran while one was open for 7% of the time, Pallas kernels for 44%

profile of v5, /device:TPU:0, one launch (start us, length us, event | category | flops | bytes accessed | tf_op | source)
XLA Modules:
  0.0 374.9 jit_solution(11037166455570262985)
XLA Ops:
  9.3 18.1 %conditional.9 = (bf16[256,2048]{1,0:T(8,128)(2,1)}, bf16[256,512]{1,0:T(8,128)(2,1)}, bf16[256,512]{1,0:T(8,128)(2,1)}, bf16[256,512]{1,0:T(8,128)(2,1)}, f32[8...) conditional(s32[]{:T(128)} %bitcast.8, () %tuple.94, ...), branch_computations={%region_0.1_spmd, %region_1.2_spmd} | conditional | flops 278528 | bytes 7798904 | solution.py:829
  9.3 12.7 %branch_1_fun.12 = (bf16[256,2048]{1,0:T(8,128)(2,1)}, bf16[256,512]{1,0:T(8,128)(2,1)}, bf16[256,512]{1,0:T(8,128)(2,1)}, bf16[256,512]{1,0:T(8,128)(2,1)}, f32...) custom-call(s32[3]{0:T(128)} %get-tuple-element.160.meta, ...), custom_call_target="tpu_custom_call" | custom-call | tf_op jit(solution)/shard_map/cond/branch_1_fun/pallas_call | solution.py:128
  34.1 7.8 %collective-permute-start.20 = (f32[128,512]{1,0:T(8,128)}, f32[128,512]{1,0:T(8,128)}, u32[]{:S(2)}, u32[]{:S(2)}) collective-permute-start(f32[128,512]{1,0:T(8,128)} %get-tuple-element.446), channel_id=1, source_target_pairs={{0,8},{4,12},{8,0},{12,4},{16,24},{20,28},{24,16},{28,20},{1,9},{5... | collective-permute-start | bytes 786440 | tf_op jit(solution)/shard_map/ppermute | solution.py:774
  42.9 30.1 %conditional.10 = (bf16[256,2048]{1,0:T(8,128)(2,1)}, bf16[256,2048]{1,0:T(8,128)(2,1)}, f32[128,2048]{1,0:T(8,128)}, f32[128,2048]{1,0:T(8,128)}, f32[128,2048]...) conditional(s32[]{:T(128)} %bitcast.8, () %tuple.97, (s32[3]{0:T(128)}, bf16[256,2048]{1,0:T(8,128)(2,1)}, ...), branch_computations={%region_2.3_spmd, %region_3.4_spmd} | conditional | bytes 5310544 | solution.py:829
  51.9 15.8 %collective-permute-done.1.refs_1_.refs_3_ = f32[136,2048]{1,0:T(8,128)} collective-permute-done((f32[136,2048]{1,0:T(8,128)}, f32[136,2048]{1,0:T(8,128)}, u32[]{:S(2)}, u32[]{:S(2)}) %collective-permute-start.1) | collective-permute-done | bytes 1114144 | tf_op jit(solution)/shard_map/cond/branch_1_fun/ppermute | solution.py:771
  76.9 21.9 %conditional.11 = (bf16[256,2048]{1,0:T(8,128)(2,1)}, bf16[256,2048]{1,0:T(8,128)(2,1)}, f32[4,256,4]{2,1,0:T(8,128)}, bf16[256,2048]{1,0:T(8,128)(2,1)}, f32[128,2048]{1,0:T(8,128)}) conditional(s32[]{:T(128)} %bitcast.8, () %tuple.100, (f32[128,2048]{1,0:T(8,128)}, s32[3]{0:T(128)}, bf16[2048,2048]{1,0:T(8,128)(2,1)}, f32[1,2048]{1,0:T(1,128)}, ...), branch_computations={%region_4.5_spmd, %region_5.6_spmd} | conditional | bytes 8409208 | solution.py:829
  79.9 9.9 %branch_1_fun.15 = (bf16[256,2048]{1,0:T(8,128)(2,1)}, bf16[256,2048]{1,0:T(8,128)(2,1)}, f32[256,4]{1,0:T(8,128)}, bf16[256,2048]{1,0:T(8,128)(2,1)}) custom-call(s32[3]{0:T(128)} %get-tuple-element.199.meta, f32[128,2048]{1,0:T(8,128)} %get-tuple-element.200.refs_0_, f32[128,2048]{1,0:T(8,128)} %collective-permute-done.2.refs_1_, ...), custom_call_target="tpu_custom_call" | custom-call | tf_op jit(solution)/shard_map/cond/branch_1_fun/pallas_call | solution.py:128
  89.8 9.1 %all-gather = f32[1024,4]{1,0:T(8,128)} all-gather(f32[256,4]{1,0:T(8,128)} %get-tuple-element.207), channel_id=2, replica_groups=mesh['batch'=8,'mp'=4] {'mp'}, dimensions={0}, use_global_device_ids=true | all-gather | bytes 20480 | tf_op jit(solution)/shard_map/cond/branch_1_fun/all_gather | solution.py:943
  101.8 16.3 %conditional.12 = (bf16[256,2048]{1,0:T(8,128)(2,1)}, bf16[256,2048]{1,0:T(8,128)(2,1)}, f32[256,4]{1,0:T(8,128)}, f32[8,2048]{1,0:T(8,128)}, f32[128,2048]{1,0:...) conditional(s32[]{:T(128)} %bitcast.8, () %tuple.93, (s32[3]{0:T(128)}, bf16[256,2048]{1,0:T(8,128)(2,1)}, ...), branch_computations={%region_6.7_spmd, %region_7.8_spmd} | conditional | flops 262144 | bytes 12583088 | solution.py:829
  101.8 11.1 %branch_1_fun.16 = (bf16[256,2048]{1,0:T(8,128)(2,1)}, bf16[256,2048]{1,0:T(8,128)(2,1)}, f32[256,4]{1,0:T(8,128)}, f32[8,2048]{1,0:T(8,128)}, f32[128,2048]{1,0:T(8,128)}, /*index=5*/f32[128,2048]{1,0:T(8,128)}) custom-call(s32[3]{0:T(128)} %get-tuple-element.210.meta, bf16[256,2048]{1,0:T(8,128)(2,1)} %get-tuple-element.211.refs_0_, ...), custom_call_target="tpu_custom_call" | custom-call | tf_op jit(solution)/shard_map/cond/branch_1_fun/pallas_call | solution.py:128
  133.9 17.5 %shard_map.337 = (f32[256,2048]{1,0:T(8,128)}, f32[256,2048]{1,0:T(8,128)}, f32[520,2048]{1,0:T(8,128)}) custom-call(s32[3]{0:T(128)} %pad_add_fusion.meta, f32[128,2048]{1,0:T(8,128)} %collective-permute-done.22.refs_0_, f32[128,2048]{1,0:T(8,128)} %get-tuple-element.473.refs_1_, f32[128,2048]{1,0:T(8,128)} %collective-permute-done.16.refs_2_, ...), custom_call_target="tpu_custom_call" | custom-call | flops 99999997952 | tf_op jit(solution)/shard_map/pallas_call | solution.py:128
  162.2 12.3 %conditional.13 = (f32[256,1536]{1,0:T(8,128)}, f32[256,512]{1,0:T(8,128)}, f32[8,512]{1,0:T(8,128)}, bf16[256,2048]{1,0:T(8,128)(2,1)}, f32[128,512]{1,0:T(8,128)}, /*index=5*/f32[128,512]{1,0:T(8,128)}) conditional(s32[]{:T(128)} %bitcast.8, () %tuple.107, (f32[128,2176]{1,0:T(8,128)}, s32[3]{0:T(128)}, f32[256,512]{1,0:T(8,128)}, ...), branch_computations={%region_8.9_spmd, %region_9.10_spmd} | conditional | bytes 6553768 | solution.py:829
  165.3 9.2 %branch_1_fun.17 = (f32[256,1536]{1,0:T(8,128)}, f32[256,512]{1,0:T(8,128)}, f32[8,512]{1,0:T(8,128)}, bf16[256,2048]{1,0:T(8,128)(2,1)}) custom-call(s32[3]{0:T(128)} %get-tuple-element.226.meta, f32[128,2176]{1,0:T(8,128)} %get-tuple-element.227.refs_0_, f32[128,2176]{1,0:T(8,128)} %collective-permute-done.7.refs_1_, ...), custom_call_target="tpu_custom_call" | custom-call | tf_op jit(solution)/shard_map/cond/branch_1_fun/pallas_call | solution.py:128
  174.6 9.8 %collective-permute-done.28 = f32[128,2048]{1,0:T(8,128)} collective-permute-done((f32[128,2048]{1,0:T(8,128)}, f32[128,2048]{1,0:T(8,128)}, u32[]{:S(2)}, u32[]{:S(2)}) %collective-permute-start.28) | collective-permute-done | bytes 1048608 | tf_op jit(solution)/shard_map/ppermute | solution.py:780
  187.9 22.8 %conditional.14 = (f32[512,2048]{1,0:T(8,128)}, f32[512,2048]{1,0:T(8,128)}, f32[256,2048]{1,0:T(8,128)}) conditional(s32[]{:T(128)} %bitcast.8, () %tuple.110, (s32[3]{0:T(128)}, f32[128,2048]{1,0:T(8,128)}, f32[128,2048]{1,0:T(8,128)}, f32[128,2048]{1,0:T(8,128)}, f32[128,2048]{1,0:T(8,128)}, /*index=5*/f32[128,2048]{1,0:T(8,128)}, ...), branch_computations={%region_10.11_spmd, %region_11.12_spmd} | conditional | flops 524288 | bytes 31457384 | solution.py:829
  192.1 10.9 %branch_1_fun.19 = (f32[256,2048]{1,0:T(8,128)}, f32[256,2048]{1,0:T(8,128)}) custom-call(s32[3]{0:T(128)} %get-tuple-element.244.meta, f32[256,1536]{1,0:T(8,128)} %get-tuple-element.253.refs_0_, bf16[3,2048,512]{2,1,0:T(8,128)(2,1)} %get-tuple-element.254.refs_1_, bf16[256,2048]{1,0:T(8,128)(2,1)} %get-tuple-element.255.refs_2_, ...), custom_call_target="tpu_custom_call" | custom-call | tf_op jit(solution)/shard_map/cond/branch_1_fun/pallas_call | solution.py:128
  210.7 9.0 %collective-permute-done.33.refs_8_ = f32[256,1536]{1,0:T(8,128)} collective-permute-done((f32[256,1536]{1,0:T(8,128)}, f32[256,1536]{1,0:T(8,128)}, u32[]{:S(2)}, u32[]{:S(2)}) %collective-permute-start.33) | collective-permute-done | bytes 1572896 | tf_op jit(solution)/shard_map/ppermute | solution.py:774
  227.1 24.6 %shard_map.339 = (f32[256,2048]{1,0:T(8,128)}, f32[256,2048]{1,0:T(8,128)}, f32[520,2048]{1,0:T(8,128)}) custom-call(s32[3]{0:T(128)} %pad_add_fusion.meta, f32[512,2048]{1,0:T(8,128)} %get-tuple-element.523.refs_0_.refs_2_, f32[512,2048]{1,0:T(8,128)} %get-tuple-element.524.refs_1_.refs_3_, f32[512,2048]{1,0:T(8,128)} %get-tuple-element.523.refs_0_.refs_2_, ...), custom_call_target="tpu_custom_call" | custom-call | flops 99999997952 | tf_op jit(solution)/shard_map/pallas_call | solution.py:128
  271.6 19.7 %conditional.15 = (f32[256,2048]{1,0:T(8,128)S(1)}, f32[8,2048]{1,0:T(8,128)}, f32[384,512]{1,0:T(8,128)}, f32[384,512]{1,0:T(8,128)}, f32[384,512]{1,0:T(8,128)...) conditional(s32[]{:T(128)} %bitcast.8, () %tuple.92, (f32[2048]{0:T(1024)}, ...), branch_computations={%region_12.13_spmd, %region_13.14_spmd} | conditional | bytes 17825924 | solution.py:829
  278.5 8.5 %branch_1_fun.20 = (f32[256,2048]{1,0:T(8,128)}, f32[8,2048]{1,0:T(8,128)}) custom-call(s32[3]{0:T(128)} %get-tuple-element.259.meta, f32[256,2048]{1,0:T(8,128)} %get-tuple-element.260.refs_0_, f32[256,2048]{1,0:T(8,128)} %get-tuple-element.261.refs_1_, f32[128,2048]{1,0:T(8,128)} %get-tuple-element.262.refs_2_, ...), custom_call_target="tpu_custom_call" | custom-call | tf_op jit(solution)/shard_map/cond/branch_1_fun/pallas_call | solution.py:128
  291.3 7.9 %collective-permute-done.43.refs_9_ = f32[256,512]{1,0:T(8,128)} collective-permute-done((f32[256,512]{1,0:T(8,128)}, f32[256,512]{1,0:T(8,128)}, u32[]{:S(2)}, u32[]{:S(2)}) %collective-permute-start.43) | collective-permute-done | bytes 524320 | tf_op jit(solution)/shard_map/ppermute | solution.py:774
  307.0 21.2 %conditional.16 = (bf16[256,2048]{1,0:T(8,128)(2,1)}, bf16[256,2048]{1,0:T(8,128)(2,1)}, f32[8,2048]{1,0:T(8,128)}) conditional(s32[]{:T(128)} %bitcast.8, () %tuple.91, (f32[256,2048]{1,0:T(8,128)S(1)}, s32[3]{0:T(128)}, f32[8,2048]{1,0:T(8,128)}) %tuple.116), branch_computations={%region_14.15_spmd, %region_15.16_spmd} | conditional | flops 16384 | bytes 25624736 | solution.py:829
  337.4 9.5 %collective-permute-done.42.refs_1_.refs_3_ = f32[520,2048]{1,0:T(8,128)} collective-permute-done((f32[520,2048]{1,0:T(8,128)}, f32[520,2048]{1,0:T(8,128)}, u32[]{:S(2)}, u32[]{:S(2)}) %collective-permute-start.42) | collective-permute-done | bytes 4259872 | tf_op jit(solution)/shard_map/ppermute | solution.py:774
  355.7 9.6 %conditional.17 = (f32[8,2560]{1,0:T(8,128)}) conditional(s32[]{:T(128)} %bitcast.8, () %tuple.117, (f32[8,2560]{1,0:T(8,128)}, f32[8,2560]{1,0:T(8,128)}) %tuple.120), branch_computations={%region_16.17_spmd, %region_17.18_spmd} | conditional | flops 40960 | bytes 819248 | solution.py:829
  (135 shorter events, 200.0 us)
Async XLA Ops:
  4.6 26.5 %collective-permute-start.16 = (f32[128,2048]{1,0:T(8,128)}, f32[128,2048]{1,0:T(8,128)}, u32[]{:S(2)}, u32[]{:S(2)}) collective-permute-start(f32[128,2048]{1,0:T(8,128)} %shard_map.336.refs_3_), channel_id=1, source_target_pairs={{0,8},{4,12},{8,0},{12,4},{16,24},{20,28},{24,16},{28,20},{1,9},{5... | collective-permute-start | bytes 3145736 | tf_op jit(solution)/shard_map/ppermute | solution.py:774
  31.1 41.9 %collective-permute-start.18 = (f32[128,2048]{1,0:T(8,128)}, f32[128,2048]{1,0:T(8,128)}, u32[]{:S(2)}, u32[]{:S(2)}) collective-permute-start(f32[128,2048]{1,0:T(8,128)} %collective-permute-done.17), channel_id=1, source_target_pairs={{8,0},{12,4},{16,24},{20,28},{9,1},{13,5},{17,25},{21,29},{10,2},{... | collective-permute-start | bytes 3145736 | tf_op jit(solution)/shard_map/ppermute | solution.py:780
  32.4 40.6 %collective-permute-start.19 = (f32[128,2048]{1,0:T(8,128)}, f32[128,2048]{1,0:T(8,128)}, u32[]{:S(2)}, u32[]{:S(2)}) collective-permute-start(f32[128,2048]{1,0:T(8,128)} %collective-permute-done.16.refs_2_), channel_id=1, source_target_pairs={{8,16},{12,20},{16,8},{20,12},{9,17},{13,21},{17,9},{21,13},{10,18... | collective-permute-start | bytes 3145736 | tf_op jit(solution)/shard_map/ppermute | solution.py:777
  34.1 38.9 %collective-permute-start.20 = (f32[128,512]{1,0:T(8,128)}, f32[128,512]{1,0:T(8,128)}, u32[]{:S(2)}, u32[]{:S(2)}) collective-permute-start(f32[128,512]{1,0:T(8,128)} %get-tuple-element.446), channel_id=1, source_target_pairs={{0,8},{4,12},{8,0},{12,4},{16,24},{20,28},{24,16},{28,20},{1,9},{5... | collective-permute-start | bytes 786440 | tf_op jit(solution)/shard_map/ppermute | solution.py:774
  41.9 31.1 %collective-permute-start.21 = (f32[128,512]{1,0:T(8,128)}, f32[128,512]{1,0:T(8,128)}, u32[]{:S(2)}, u32[]{:S(2)}) collective-permute-start(f32[128,512]{1,0:T(8,128)} %get-tuple-element.447), channel_id=1, source_target_pairs={{0,12},{4,8},{8,4},{12,0},{16,28},{20,24},{24,20},{28,16},{1,13},{... | collective-permute-start | bytes 786440 | tf_op jit(solution)/shard_map/ppermute | solution.py:774
  73.0 25.9 %collective-permute-start.22 = (f32[128,2048]{1,0:T(8,128)}, f32[128,2048]{1,0:T(8,128)}, u32[]{:S(2)}, u32[]{:S(2)}) collective-permute-start(f32[128,2048]{1,0:T(8,128)} %get-tuple-element.448), channel_id=1, source_target_pairs={{0,8},{4,12},{8,0},{12,4},{16,24},{20,28},{24,16},{28,20},{1,9},{5... | collective-permute-start | bytes 3145736 | tf_op jit(solution)/shard_map/ppermute | solution.py:774
  98.8 28.2 %collective-permute-start.26 = (f32[128,2048]{1,0:T(8,128)}, f32[128,2048]{1,0:T(8,128)}, u32[]{:S(2)}, u32[]{:S(2)}) collective-permute-start(f32[128,2048]{1,0:T(8,128)} %collective-permute-done.23), channel_id=1, source_target_pairs={{8,0},{12,4},{16,24},{20,28},{9,1},{13,5},{17,25},{21,29},{10,2},{... | collective-permute-start | bytes 3145736 | tf_op jit(solution)/shard_map/ppermute | solution.py:780
  100.1 26.9 %collective-permute-start.27 = (f32[128,2048]{1,0:T(8,128)}, f32[128,2048]{1,0:T(8,128)}, u32[]{:S(2)}, u32[]{:S(2)}) collective-permute-start(f32[128,2048]{1,0:T(8,128)} %collective-permute-done.22.refs_0_), channel_id=1, source_target_pairs={{8,16},{12,20},{16,8},{20,12},{9,17},{13,21},{17,9},{21,13},{10,18... | collective-permute-start | bytes 3145736 | tf_op jit(solution)/shard_map/ppermute | solution.py:777
  129.3 24.9 %collective-permute-start.31 = (f32[128,2048]{1,0:T(8,128)}, f32[128,2048]{1,0:T(8,128)}, u32[]{:S(2)}, u32[]{:S(2)}) collective-permute-start(f32[128,2048]{1,0:T(8,128)} %get-tuple-element.469.refs_0_), channel_id=1, source_target_pairs={{0,2},{1,3},{2,0},{3,1},{4,6},{5,7},{6,4},{7,5},{8,10},{9,11},{10,... | collective-permute-start | bytes 3145736 | tf_op jit(solution)/shard_map/ppermute | solution.py:771
  129.8 30.8 %collective-permute-start.30 = (f32[128,2048]{1,0:T(8,128)}, f32[128,2048]{1,0:T(8,128)}, u32[]{:S(2)}, u32[]{:S(2)}) collective-permute-start(f32[128,2048]{1,0:T(8,128)} %collective-permute-done.19), channel_id=1, source_target_pairs={{8,0},{12,4},{16,24},{20,28},{9,1},{13,5},{17,25},{21,29},{10,2},{... | collective-permute-start | bytes 3145736 | tf_op jit(solution)/shard_map/ppermute | solution.py:780
  131.1 29.2 %collective-permute-start.29 = (f32[256,4]{1,0:T(8,128)}, f32[256,4]{1,0:T(8,128)}, u32[]{:S(2)}, u32[]{:S(2)}) collective-permute-start(f32[256,4]{1,0:T(8,128)} %get-tuple-element.487), channel_id=1, source_target_pairs={{0,24},{4,28},{8,16},{12,20},{16,8},{20,12},{24,0},{28,4},{1,25},{... | collective-permute-start | bytes 12296 | tf_op jit(solution)/shard_map/ppermute | solution.py:774
  132.7 51.8 %collective-permute-start.28 = (f32[128,2048]{1,0:T(8,128)}, f32[128,2048]{1,0:T(8,128)}, u32[]{:S(2)}, u32[]{:S(2)}) collective-permute-start(f32[128,2048]{1,0:T(8,128)} %collective-permute-done.27), channel_id=1, source_target_pairs={{8,0},{12,4},{16,24},{20,28},{9,1},{13,5},{17,25},{21,29},{10,2},{... | collective-permute-start | bytes 3145736 | tf_op jit(solution)/shard_map/ppermute | solution.py:780
  184.4 35.3 %collective-permute-start.33 = (f32[256,1536]{1,0:T(8,128)}, f32[256,1536]{1,0:T(8,128)}, u32[]{:S(2)}, u32[]{:S(2)}) collective-permute-start(f32[256,1536]{1,0:T(8,128)} %get-tuple-element.534.refs_7_), channel_id=1, source_target_pairs={{0,4},{4,0},{8,12},{12,8},{16,20},{20,16},{24,28},{28,24},{1,5},{5... | collective-permute-start | bytes 4718600 | tf_op jit(solution)/shard_map/ppermute | solution.py:774
  185.9 37.6 %collective-permute-start.34 = (f32[256,1536]{1,0:T(8,128)}, f32[256,1536]{1,0:T(8,128)}, u32[]{:S(2)}, u32[]{:S(2)}) collective-permute-start(f32[256,1536]{1,0:T(8,128)} %get-tuple-element.534.refs_7_), channel_id=1, source_target_pairs={{0,8},{4,12},{8,0},{12,4},{16,24},{20,28},{24,16},{28,20},{1,9},{5... | collective-permute-start | bytes 4718600 | tf_op jit(solution)/shard_map/ppermute | solution.py:774
  185.9 68.1 %collective-permute-start.38 = (f32[128,512]{1,0:T(8,128)}, f32[128,512]{1,0:T(8,128)}, u32[]{:S(2)}, u32[]{:S(2)}) collective-permute-start(f32[128,512]{1,0:T(8,128)} %get-tuple-element.511), channel_id=1, source_target_pairs={{0,8},{4,12},{8,0},{12,4},{16,24},{20,28},{24,16},{28,20},{1,9},{5... | collective-permute-start | bytes 786440 | tf_op jit(solution)/shard_map/ppermute | solution.py:774
  223.6 28.2 %collective-permute-start.39 = (f32[256,512]{1,0:T(8,128)}, f32[256,512]{1,0:T(8,128)}, u32[]{:S(2)}, u32[]{:S(2)}) collective-permute-start(f32[256,512]{1,0:T(8,128)} %get-tuple-element.551.refs_7_), channel_id=1, source_target_pairs={{0,4},{4,0},{8,12},{12,8},{16,20},{20,16},{24,28},{28,24},{1,5},{5... | collective-permute-start | bytes 1572872 | tf_op jit(solution)/shard_map/ppermute | solution.py:774
  224.1 36.2 %collective-permute-start.36 = (f32[256,1536]{1,0:T(8,128)}, f32[256,1536]{1,0:T(8,128)}, u32[]{:S(2)}, u32[]{:S(2)}) collective-permute-start(f32[256,1536]{1,0:T(8,128)} %collective-permute-done.33.refs_8_), channel_id=1, source_target_pairs={{0,8},{4,12},{8,0},{12,4},{16,24},{20,28},{24,16},{28,20},{1,9},{5... | collective-permute-start | bytes 4718600 | tf_op jit(solution)/shard_map/ppermute | solution.py:774
  224.1 29.9 %collective-permute-start.37 = (f32[128,512]{1,0:T(8,128)}, f32[128,512]{1,0:T(8,128)}, u32[]{:S(2)}, u32[]{:S(2)}) collective-permute-start(f32[128,512]{1,0:T(8,128)} %get-tuple-element.521), channel_id=1, source_target_pairs={{0,4},{4,0},{8,12},{12,8},{16,20},{20,16},{24,28},{28,24},{1,5},{5... | collective-permute-start | bytes 786440 | tf_op jit(solution)/shard_map/ppermute | solution.py:774
  225.6 46.0 %collective-permute-start.35 = (f32[256,2048]{1,0:T(8,128)}, f32[256,2048]{1,0:T(8,128)}, u32[]{:S(2)}, u32[]{:S(2)}) collective-permute-start(f32[256,2048]{1,0:T(8,128)} %get-tuple-element.514), channel_id=1, source_target_pairs={{0,2},{1,3},{2,0},{3,1},{4,6},{5,7},{6,4},{7,5},{8,10},{9,11},{10,... | collective-permute-start | bytes 6291464 | tf_op jit(solution)/shard_map/ppermute | solution.py:771
  251.8 95.0 %collective-permute-start.42 = (f32[520,2048]{1,0:T(8,128)}, f32[520,2048]{1,0:T(8,128)}, u32[]{:S(2)}, u32[]{:S(2)}) collective-permute-start(f32[520,2048]{1,0:T(8,128)} %get-tuple-element.548), channel_id=1, source_target_pairs={{0,4},{4,0},{8,12},{12,8},{16,20},{20,16},{24,28},{28,24},{1,5},{5... | collective-permute-start | bytes 12779528 | tf_op jit(solution)/shard_map/ppermute | solution.py:774
  260.5 38.7 %collective-permute-start.43 = (f32[256,512]{1,0:T(8,128)}, f32[256,512]{1,0:T(8,128)}, u32[]{:S(2)}, u32[]{:S(2)}) collective-permute-start(f32[256,512]{1,0:T(8,128)} %get-tuple-element.551.refs_7_), channel_id=1, source_target_pairs={{0,8},{4,12},{8,0},{12,4},{16,24},{20,28},{24,16},{28,20},{1,9},{5... | collective-permute-start | bytes 1572872 | tf_op jit(solution)/shard_map/ppermute | solution.py:774
  262.2 44.7 %collective-permute-start.44 = (f32[256,512]{1,0:T(8,128)}, f32[256,512]{1,0:T(8,128)}, u32[]{:S(2)}, u32[]{:S(2)}) collective-permute-start(f32[256,512]{1,0:T(8,128)} %collective-permute-done.39.refs_8_), channel_id=1, source_target_pairs={{0,8},{4,12},{8,0},{12,4},{16,24},{20,28},{24,16},{28,20},{1,9},{5... | collective-permute-start | bytes 1572872 | tf_op jit(solution)/shard_map/ppermute | solution.py:774
  270.7 94.6 %collective-permute-start.46 = (f32[256,1536]{1,0:T(8,128)}, f32[256,1536]{1,0:T(8,128)}, u32[]{:S(2)}, u32[]{:S(2)}) collective-permute-start(f32[256,1536]{1,0:T(8,128)} %get-tuple-element.571), channel_id=1, source_target_pairs={{0,16},{4,20},{8,24},{12,28},{16,0},{20,4},{24,8},{28,12},{1,17},{... | collective-permute-start | bytes 4718600 | tf_op jit(solution)/shard_map/ppermute | solution.py:774
  337.0 28.3 %collective-permute-start.47 = (f32[256,512]{1,0:T(8,128)}, f32[256,512]{1,0:T(8,128)}, u32[]{:S(2)}, u32[]{:S(2)}) collective-permute-start(f32[256,512]{1,0:T(8,128)} %get-tuple-element.572), channel_id=1, source_target_pairs={{0,16},{4,20},{8,24},{12,28},{16,0},{20,4},{24,8},{28,12},{1,17},{... | collective-permute-start | bytes 1572872 | tf_op jit(solution)/shard_map/ppermute | solution.py:774
  (27 other events, 299.8 us)

commit v6 on v5

--- a/solution.py
+++ b/solution.py
@@ -1210,7 +1210,7 @@
                 [shape_of((block, hidden)), shape_of((hidden, block))],
                 (sums[0], near_got, sums[1], near_got),
             )
-            comb, comb_x, grad_up = meet(comb, comb_x, grad_up)
+            comb, comb_x, grad_up, h_parts = meet(comb, comb_x, grad_up, h_parts)
 
             def small_sums():
                 total = comb + comb_x

time: 377 us -> 377 us (level)
  no operation moved by 1% of the time
where the time goes in v6:
time: 377 us; the launch traced here: 375 us
  Pallas kernels  168 us (45%)
  waiting for transfers between devices  108 us (29%)
  starting transfers between devices  54.4 us (14%)
  local copies, waits for them, and re-layouts  20.5 us (5%)
  other arithmetic  13.4 us (4%)
  blocking collectives  9.06 us (2%)
    pallas_call x20, Pallas kernels, run(): call(body, grid, ins, outs, shapes, scratch, len(extra), self.cover)  168 us
    ppermute x23, waiting for transfers between devices, to_batch(): return lax.ppermute(value, 'batch', [(i, i ^ s) for i in range(nb)])  58 us
    ppermute x23, starting transfers between devices, to_batch(): return lax.ppermute(value, 'batch', [(i, i ^ s) for i in range(nb)])  35.9 us
    ppermute x3, waiting for transfers between devices, to_y(): return lax.ppermute(value, 'mp', cross)  18.6 us
    ppermute x14, waiting for transfers between devices, to_core(): return lax.ppermute(value, 'mp', pair)  17.6 us
    ppermute x4, waiting for transfers between devices, outward(): return lax.ppermute(value, 'batch', outward_link)  13.6 us
    cond x10, local copies, waits for them, and re-layouts  11.1 us
    all_gather x1, blocking collectives, hidden_first(): return (g, slope, lax.all_gather(stats_g, 'mp'), b, dy_core)  9.06 us
  transfers between devices with their start and end apart: 48, of which 22 were waited for; matrix products, arithmetic and copies ran while one was open for 7% of the time, Pallas kernels for 44%

profile of v6, /device:TPU:0, one launch (start us, length us, event | category | flops | bytes accessed | tf_op | source)
XLA Modules:
  0.0 374.9 jit_solution(4497476446931943350)
XLA Ops:
  9.3 18.1 %conditional.9 = (bf16[256,2048]{1,0:T(8,128)(2,1)}, bf16[256,512]{1,0:T(8,128)(2,1)}, bf16[256,512]{1,0:T(8,128)(2,1)}, bf16[256,512]{1,0:T(8,128)(2,1)}, f32[8...) conditional(s32[]{:T(128)} %bitcast.8, () %tuple.94, ...), branch_computations={%region_0.1_spmd, %region_1.2_spmd} | conditional | flops 278528 | bytes 7798904 | solution.py:829
  9.3 12.7 %branch_1_fun.12 = (bf16[256,2048]{1,0:T(8,128)(2,1)}, bf16[256,512]{1,0:T(8,128)(2,1)}, bf16[256,512]{1,0:T(8,128)(2,1)}, bf16[256,512]{1,0:T(8,128)(2,1)}, f32...) custom-call(s32[3]{0:T(128)} %get-tuple-element.160.meta, ...), custom_call_target="tpu_custom_call" | custom-call | tf_op jit(solution)/shard_map/cond/branch_1_fun/pallas_call | solution.py:128
  34.1 7.8 %collective-permute-start.20 = (f32[128,512]{1,0:T(8,128)}, f32[128,512]{1,0:T(8,128)}, u32[]{:S(2)}, u32[]{:S(2)}) collective-permute-start(f32[128,512]{1,0:T(8,128)} %get-tuple-element.447), channel_id=1, source_target_pairs={{0,8},{4,12},{8,0},{12,4},{16,24},{20,28},{24,16},{28,20},{1,9},{5... | collective-permute-start | bytes 786440 | tf_op jit(solution)/shard_map/ppermute | solution.py:774
  42.9 30.1 %conditional.10 = (bf16[256,2048]{1,0:T(8,128)(2,1)}, bf16[256,2048]{1,0:T(8,128)(2,1)}, f32[128,2048]{1,0:T(8,128)}, f32[128,2048]{1,0:T(8,128)}, f32[128,2048]...) conditional(s32[]{:T(128)} %bitcast.8, () %tuple.97, (s32[3]{0:T(128)}, bf16[256,2048]{1,0:T(8,128)(2,1)}, ...), branch_computations={%region_2.3_spmd, %region_3.4_spmd} | conditional | bytes 5310544 | solution.py:829
  51.9 15.8 %collective-permute-done.1.refs_1_.refs_3_ = f32[136,2048]{1,0:T(8,128)} collective-permute-done((f32[136,2048]{1,0:T(8,128)}, f32[136,2048]{1,0:T(8,128)}, u32[]{:S(2)}, u32[]{:S(2)}) %collective-permute-start.1) | collective-permute-done | bytes 1114144 | tf_op jit(solution)/shard_map/cond/branch_1_fun/ppermute | solution.py:771
  76.9 21.9 %conditional.11 = (bf16[256,2048]{1,0:T(8,128)(2,1)}, bf16[256,2048]{1,0:T(8,128)(2,1)}, f32[4,256,4]{2,1,0:T(8,128)}, bf16[256,2048]{1,0:T(8,128)(2,1)}, f32[128,2048]{1,0:T(8,128)}) conditional(s32[]{:T(128)} %bitcast.8, () %tuple.100, (f32[128,2048]{1,0:T(8,128)}, s32[3]{0:T(128)}, bf16[2048,2048]{1,0:T(8,128)(2,1)}, f32[1,2048]{1,0:T(1,128)}, ...), branch_computations={%region_4.5_spmd, %region_5.6_spmd} | conditional | bytes 8409208 | solution.py:829
  79.9 9.9 %branch_1_fun.15 = (bf16[256,2048]{1,0:T(8,128)(2,1)}, bf16[256,2048]{1,0:T(8,128)(2,1)}, f32[256,4]{1,0:T(8,128)}, bf16[256,2048]{1,0:T(8,128)(2,1)}) custom-call(s32[3]{0:T(128)} %get-tuple-element.199.meta, f32[128,2048]{1,0:T(8,128)} %get-tuple-element.200.refs_0_, f32[128,2048]{1,0:T(8,128)} %collective-permute-done.2.refs_1_, ...), custom_call_target="tpu_custom_call" | custom-call | tf_op jit(solution)/shard_map/cond/branch_1_fun/pallas_call | solution.py:128
  89.8 9.1 %all-gather = f32[1024,4]{1,0:T(8,128)} all-gather(f32[256,4]{1,0:T(8,128)} %get-tuple-element.207), channel_id=2, replica_groups=mesh['batch'=8,'mp'=4] {'mp'}, dimensions={0}, use_global_device_ids=true | all-gather | bytes 20480 | tf_op jit(solution)/shard_map/cond/branch_1_fun/all_gather | solution.py:943
  101.8 16.3 %conditional.12 = (bf16[256,2048]{1,0:T(8,128)(2,1)}, bf16[256,2048]{1,0:T(8,128)(2,1)}, f32[256,4]{1,0:T(8,128)}, f32[8,2048]{1,0:T(8,128)}, f32[128,2048]{1,0:...) conditional(s32[]{:T(128)} %bitcast.8, () %tuple.93, (s32[3]{0:T(128)}, bf16[256,2048]{1,0:T(8,128)(2,1)}, ...), branch_computations={%region_6.7_spmd, %region_7.8_spmd} | conditional | flops 262144 | bytes 12583088 | solution.py:829
  101.8 11.1 %branch_1_fun.16 = (bf16[256,2048]{1,0:T(8,128)(2,1)}, bf16[256,2048]{1,0:T(8,128)(2,1)}, f32[256,4]{1,0:T(8,128)}, f32[8,2048]{1,0:T(8,128)}, f32[128,2048]{1,0:T(8,128)}, /*index=5*/f32[128,2048]{1,0:T(8,128)}) custom-call(s32[3]{0:T(128)} %get-tuple-element.210.meta, bf16[256,2048]{1,0:T(8,128)(2,1)} %get-tuple-element.211.refs_0_, ...), custom_call_target="tpu_custom_call" | custom-call | tf_op jit(solution)/shard_map/cond/branch_1_fun/pallas_call | solution.py:128
  133.9 17.5 %shard_map.337 = (f32[256,2048]{1,0:T(8,128)}, f32[256,2048]{1,0:T(8,128)}, f32[520,2048]{1,0:T(8,128)}) custom-call(s32[3]{0:T(128)} %pad_add_fusion.meta, f32[128,2048]{1,0:T(8,128)} %collective-permute-done.22.refs_0_, f32[128,2048]{1,0:T(8,128)} %get-tuple-element.474.refs_1_, f32[128,2048]{1,0:T(8,128)} %collective-permute-done.16.refs_2_, ...), custom_call_target="tpu_custom_call" | custom-call | flops 99999997952 | tf_op jit(solution)/shard_map/pallas_call | solution.py:128
  162.2 12.3 %conditional.13 = (f32[256,1536]{1,0:T(8,128)}, f32[256,512]{1,0:T(8,128)}, f32[8,512]{1,0:T(8,128)}, bf16[256,2048]{1,0:T(8,128)(2,1)}, f32[128,512]{1,0:T(8,128)}, /*index=5*/f32[128,512]{1,0:T(8,128)}) conditional(s32[]{:T(128)} %bitcast.8, () %tuple.107, (f32[128,2176]{1,0:T(8,128)}, s32[3]{0:T(128)}, f32[256,512]{1,0:T(8,128)}, ...), branch_computations={%region_8.9_spmd, %region_9.10_spmd} | conditional | bytes 6553768 | solution.py:829
  165.3 9.2 %branch_1_fun.17 = (f32[256,1536]{1,0:T(8,128)}, f32[256,512]{1,0:T(8,128)}, f32[8,512]{1,0:T(8,128)}, bf16[256,2048]{1,0:T(8,128)(2,1)}) custom-call(s32[3]{0:T(128)} %get-tuple-element.226.meta, f32[128,2176]{1,0:T(8,128)} %get-tuple-element.227.refs_0_, f32[128,2176]{1,0:T(8,128)} %collective-permute-done.7.refs_1_, ...), custom_call_target="tpu_custom_call" | custom-call | tf_op jit(solution)/shard_map/cond/branch_1_fun/pallas_call | solution.py:128
  174.6 9.8 %collective-permute-done.28 = f32[128,2048]{1,0:T(8,128)} collective-permute-done((f32[128,2048]{1,0:T(8,128)}, f32[128,2048]{1,0:T(8,128)}, u32[]{:S(2)}, u32[]{:S(2)}) %collective-permute-start.28) | collective-permute-done | bytes 1048608 | tf_op jit(solution)/shard_map/ppermute | solution.py:780
  187.9 22.8 %conditional.14 = (f32[512,2048]{1,0:T(8,128)}, f32[512,2048]{1,0:T(8,128)}, f32[256,2048]{1,0:T(8,128)}) conditional(s32[]{:T(128)} %bitcast.8, () %tuple.110, (s32[3]{0:T(128)}, f32[128,2048]{1,0:T(8,128)}, f32[128,2048]{1,0:T(8,128)}, f32[128,2048]{1,0:T(8,128)}, f32[128,2048]{1,0:T(8,128)}, /*index=5*/f32[128,2048]{1,0:T(8,128)}, ...), branch_computations={%region_10.11_spmd, %region_11.12_spmd} | conditional | flops 524288 | bytes 31457384 | solution.py:829
  192.1 10.9 %branch_1_fun.19 = (f32[256,2048]{1,0:T(8,128)}, f32[256,2048]{1,0:T(8,128)}) custom-call(s32[3]{0:T(128)} %get-tuple-element.244.meta, f32[256,1536]{1,0:T(8,128)} %get-tuple-element.253.refs_0_, bf16[3,2048,512]{2,1,0:T(8,128)(2,1)} %get-tuple-element.254.refs_1_, bf16[256,2048]{1,0:T(8,128)(2,1)} %get-tuple-element.255.refs_2_, ...), custom_call_target="tpu_custom_call" | custom-call | tf_op jit(solution)/shard_map/cond/branch_1_fun/pallas_call | solution.py:128
  210.7 9.0 %collective-permute-done.33.refs_8_ = f32[256,1536]{1,0:T(8,128)} collective-permute-done((f32[256,1536]{1,0:T(8,128)}, f32[256,1536]{1,0:T(8,128)}, u32[]{:S(2)}, u32[]{:S(2)}) %collective-permute-start.33) | collective-permute-done | bytes 1572896 | tf_op jit(solution)/shard_map/ppermute | solution.py:774
  227.1 24.6 %shard_map.339 = (f32[256,2048]{1,0:T(8,128)}, f32[256,2048]{1,0:T(8,128)}, f32[520,2048]{1,0:T(8,128)}) custom-call(s32[3]{0:T(128)} %pad_add_fusion.meta, f32[512,2048]{1,0:T(8,128)} %get-tuple-element.524.refs_0_.refs_2_, f32[512,2048]{1,0:T(8,128)} %get-tuple-element.525.refs_1_.refs_3_, f32[512,2048]{1,0:T(8,128)} %get-tuple-element.524.refs_0_.refs_2_, ...), custom_call_target="tpu_custom_call" | custom-call | flops 99999997952 | tf_op jit(solution)/shard_map/pallas_call | solution.py:128
  271.6 19.7 %conditional.15 = (f32[256,2048]{1,0:T(8,128)S(1)}, f32[8,2048]{1,0:T(8,128)}, f32[384,512]{1,0:T(8,128)}, f32[384,512]{1,0:T(8,128)}, f32[384,512]{1,0:T(8,128)...) conditional(s32[]{:T(128)} %bitcast.8, () %tuple.92, (f32[2048]{0:T(1024)}, ...), branch_computations={%region_12.13_spmd, %region_13.14_spmd} | conditional | bytes 17825924 | solution.py:829
  278.5 8.5 %branch_1_fun.20 = (f32[256,2048]{1,0:T(8,128)}, f32[8,2048]{1,0:T(8,128)}) custom-call(s32[3]{0:T(128)} %get-tuple-element.259.meta, f32[256,2048]{1,0:T(8,128)} %get-tuple-element.260.refs_0_, f32[256,2048]{1,0:T(8,128)} %get-tuple-element.261.refs_1_, f32[128,2048]{1,0:T(8,128)} %get-tuple-element.262.refs_2_, ...), custom_call_target="tpu_custom_call" | custom-call | tf_op jit(solution)/shard_map/cond/branch_1_fun/pallas_call | solution.py:128
  291.3 7.9 %collective-permute-done.43.refs_9_ = f32[256,512]{1,0:T(8,128)} collective-permute-done((f32[256,512]{1,0:T(8,128)}, f32[256,512]{1,0:T(8,128)}, u32[]{:S(2)}, u32[]{:S(2)}) %collective-permute-start.43) | collective-permute-done | bytes 524320 | tf_op jit(solution)/shard_map/ppermute | solution.py:774
  307.0 21.2 %conditional.16 = (bf16[256,2048]{1,0:T(8,128)(2,1)}, bf16[256,2048]{1,0:T(8,128)(2,1)}, f32[8,2048]{1,0:T(8,128)}) conditional(s32[]{:T(128)} %bitcast.8, () %tuple.91, (f32[256,2048]{1,0:T(8,128)S(1)}, s32[3]{0:T(128)}, f32[8,2048]{1,0:T(8,128)}) %tuple.116), branch_computations={%region_14.15_spmd, %region_15.16_spmd} | conditional | flops 16384 | bytes 25624736 | solution.py:829
  337.4 9.5 %collective-permute-done.42.refs_1_.refs_3_ = f32[520,2048]{1,0:T(8,128)} collective-permute-done((f32[520,2048]{1,0:T(8,128)}, f32[520,2048]{1,0:T(8,128)}, u32[]{:S(2)}, u32[]{:S(2)}) %collective-permute-start.42) | collective-permute-done | bytes 4259872 | tf_op jit(solution)/shard_map/ppermute | solution.py:774
  355.8 9.5 %conditional.17 = (f32[8,2560]{1,0:T(8,128)}) conditional(s32[]{:T(128)} %bitcast.8, () %tuple.117, (f32[8,2560]{1,0:T(8,128)}, f32[8,2560]{1,0:T(8,128)}) %tuple.120), branch_computations={%region_16.17_spmd, %region_17.18_spmd} | conditional | flops 40960 | bytes 819248 | solution.py:829
  (136 shorter events, 200.0 us)
Async XLA Ops:
  4.6 26.5 %collective-permute-start.16 = (f32[128,2048]{1,0:T(8,128)}, f32[128,2048]{1,0:T(8,128)}, u32[]{:S(2)}, u32[]{:S(2)}) collective-permute-start(f32[128,2048]{1,0:T(8,128)} %shard_map.336.refs_3_), channel_id=1, source_target_pairs={{0,8},{4,12},{8,0},{12,4},{16,24},{20,28},{24,16},{28,20},{1,9},{5... | collective-permute-start | bytes 3145736 | tf_op jit(solution)/shard_map/ppermute | solution.py:774
  31.1 41.9 %collective-permute-start.18 = (f32[128,2048]{1,0:T(8,128)}, f32[128,2048]{1,0:T(8,128)}, u32[]{:S(2)}, u32[]{:S(2)}) collective-permute-start(f32[128,2048]{1,0:T(8,128)} %collective-permute-done.17), channel_id=1, source_target_pairs={{8,0},{12,4},{16,24},{20,28},{9,1},{13,5},{17,25},{21,29},{10,2},{... | collective-permute-start | bytes 3145736 | tf_op jit(solution)/shard_map/ppermute | solution.py:780
  32.4 40.6 %collective-permute-start.19 = (f32[128,2048]{1,0:T(8,128)}, f32[128,2048]{1,0:T(8,128)}, u32[]{:S(2)}, u32[]{:S(2)}) collective-permute-start(f32[128,2048]{1,0:T(8,128)} %collective-permute-done.16.refs_2_), channel_id=1, source_target_pairs={{8,16},{12,20},{16,8},{20,12},{9,17},{13,21},{17,9},{21,13},{10,18... | collective-permute-start | bytes 3145736 | tf_op jit(solution)/shard_map/ppermute | solution.py:777
  34.1 38.9 %collective-permute-start.20 = (f32[128,512]{1,0:T(8,128)}, f32[128,512]{1,0:T(8,128)}, u32[]{:S(2)}, u32[]{:S(2)}) collective-permute-start(f32[128,512]{1,0:T(8,128)} %get-tuple-element.447), channel_id=1, source_target_pairs={{0,8},{4,12},{8,0},{12,4},{16,24},{20,28},{24,16},{28,20},{1,9},{5... | collective-permute-start | bytes 786440 | tf_op jit(solution)/shard_map/ppermute | solution.py:774
  41.9 31.1 %collective-permute-start.21 = (f32[128,512]{1,0:T(8,128)}, f32[128,512]{1,0:T(8,128)}, u32[]{:S(2)}, u32[]{:S(2)}) collective-permute-start(f32[128,512]{1,0:T(8,128)} %get-tuple-element.448), channel_id=1, source_target_pairs={{0,12},{4,8},{8,4},{12,0},{16,28},{20,24},{24,20},{28,16},{1,13},{... | collective-permute-start | bytes 786440 | tf_op jit(solution)/shard_map/ppermute | solution.py:774
  73.0 25.9 %collective-permute-start.22 = (f32[128,2048]{1,0:T(8,128)}, f32[128,2048]{1,0:T(8,128)}, u32[]{:S(2)}, u32[]{:S(2)}) collective-permute-start(f32[128,2048]{1,0:T(8,128)} %get-tuple-element.449), channel_id=1, source_target_pairs={{0,8},{4,12},{8,0},{12,4},{16,24},{20,28},{24,16},{28,20},{1,9},{5... | collective-permute-start | bytes 3145736 | tf_op jit(solution)/shard_map/ppermute | solution.py:774
  98.8 28.2 %collective-permute-start.26 = (f32[128,2048]{1,0:T(8,128)}, f32[128,2048]{1,0:T(8,128)}, u32[]{:S(2)}, u32[]{:S(2)}) collective-permute-start(f32[128,2048]{1,0:T(8,128)} %collective-permute-done.23), channel_id=1, source_target_pairs={{8,0},{12,4},{16,24},{20,28},{9,1},{13,5},{17,25},{21,29},{10,2},{... | collective-permute-start | bytes 3145736 | tf_op jit(solution)/shard_map/ppermute | solution.py:780
  100.1 26.9 %collective-permute-start.27 = (f32[128,2048]{1,0:T(8,128)}, f32[128,2048]{1,0:T(8,128)}, u32[]{:S(2)}, u32[]{:S(2)}) collective-permute-start(f32[128,2048]{1,0:T(8,128)} %collective-permute-done.22.refs_0_), channel_id=1, source_target_pairs={{8,16},{12,20},{16,8},{20,12},{9,17},{13,21},{17,9},{21,13},{10,18... | collective-permute-start | bytes 3145736 | tf_op jit(solution)/shard_map/ppermute | solution.py:777
  129.3 24.9 %collective-permute-start.31 = (f32[128,2048]{1,0:T(8,128)}, f32[128,2048]{1,0:T(8,128)}, u32[]{:S(2)}, u32[]{:S(2)}) collective-permute-start(f32[128,2048]{1,0:T(8,128)} %get-tuple-element.470.refs_0_), channel_id=1, source_target_pairs={{0,2},{1,3},{2,0},{3,1},{4,6},{5,7},{6,4},{7,5},{8,10},{9,11},{10,... | collective-permute-start | bytes 3145736 | tf_op jit(solution)/shard_map/ppermute | solution.py:771
  129.8 30.8 %collective-permute-start.30 = (f32[128,2048]{1,0:T(8,128)}, f32[128,2048]{1,0:T(8,128)}, u32[]{:S(2)}, u32[]{:S(2)}) collective-permute-start(f32[128,2048]{1,0:T(8,128)} %collective-permute-done.19), channel_id=1, source_target_pairs={{8,0},{12,4},{16,24},{20,28},{9,1},{13,5},{17,25},{21,29},{10,2},{... | collective-permute-start | bytes 3145736 | tf_op jit(solution)/shard_map/ppermute | solution.py:780
  131.1 29.2 %collective-permute-start.29 = (f32[256,4]{1,0:T(8,128)}, f32[256,4]{1,0:T(8,128)}, u32[]{:S(2)}, u32[]{:S(2)}) collective-permute-start(f32[256,4]{1,0:T(8,128)} %get-tuple-element.488), channel_id=1, source_target_pairs={{0,24},{4,28},{8,16},{12,20},{16,8},{20,12},{24,0},{28,4},{1,25},{... | collective-permute-start | bytes 12296 | tf_op jit(solution)/shard_map/ppermute | solution.py:774
  132.7 51.8 %collective-permute-start.28 = (f32[128,2048]{1,0:T(8,128)}, f32[128,2048]{1,0:T(8,128)}, u32[]{:S(2)}, u32[]{:S(2)}) collective-permute-start(f32[128,2048]{1,0:T(8,128)} %collective-permute-done.27), channel_id=1, source_target_pairs={{8,0},{12,4},{16,24},{20,28},{9,1},{13,5},{17,25},{21,29},{10,2},{... | collective-permute-start | bytes 3145736 | tf_op jit(solution)/shard_map/ppermute | solution.py:780
  184.4 35.3 %collective-permute-start.33 = (f32[256,1536]{1,0:T(8,128)}, f32[256,1536]{1,0:T(8,128)}, u32[]{:S(2)}, u32[]{:S(2)}) collective-permute-start(f32[256,1536]{1,0:T(8,128)} %get-tuple-element.535.refs_7_), channel_id=1, source_target_pairs={{0,4},{4,0},{8,12},{12,8},{16,20},{20,16},{24,28},{28,24},{1,5},{5... | collective-permute-start | bytes 4718600 | tf_op jit(solution)/shard_map/ppermute | solution.py:774
  185.9 37.6 %collective-permute-start.34 = (f32[256,1536]{1,0:T(8,128)}, f32[256,1536]{1,0:T(8,128)}, u32[]{:S(2)}, u32[]{:S(2)}) collective-permute-start(f32[256,1536]{1,0:T(8,128)} %get-tuple-element.535.refs_7_), channel_id=1, source_target_pairs={{0,8},{4,12},{8,0},{12,4},{16,24},{20,28},{24,16},{28,20},{1,9},{5... | collective-permute-start | bytes 4718600 | tf_op jit(solution)/shard_map/ppermute | solution.py:774
  185.9 68.1 %collective-permute-start.38 = (f32[128,512]{1,0:T(8,128)}, f32[128,512]{1,0:T(8,128)}, u32[]{:S(2)}, u32[]{:S(2)}) collective-permute-start(f32[128,512]{1,0:T(8,128)} %get-tuple-element.512), channel_id=1, source_target_pairs={{0,8},{4,12},{8,0},{12,4},{16,24},{20,28},{24,16},{28,20},{1,9},{5... | collective-permute-start | bytes 786440 | tf_op jit(solution)/shard_map/ppermute | solution.py:774
  223.6 28.2 %collective-permute-start.39 = (f32[256,512]{1,0:T(8,128)}, f32[256,512]{1,0:T(8,128)}, u32[]{:S(2)}, u32[]{:S(2)}) collective-permute-start(f32[256,512]{1,0:T(8,128)} %get-tuple-element.552.refs_7_), channel_id=1, source_target_pairs={{0,4},{4,0},{8,12},{12,8},{16,20},{20,16},{24,28},{28,24},{1,5},{5... | collective-permute-start | bytes 1572872 | tf_op jit(solution)/shard_map/ppermute | solution.py:774
  224.1 36.2 %collective-permute-start.36 = (f32[256,1536]{1,0:T(8,128)}, f32[256,1536]{1,0:T(8,128)}, u32[]{:S(2)}, u32[]{:S(2)}) collective-permute-start(f32[256,1536]{1,0:T(8,128)} %collective-permute-done.33.refs_8_), channel_id=1, source_target_pairs={{0,8},{4,12},{8,0},{12,4},{16,24},{20,28},{24,16},{28,20},{1,9},{5... | collective-permute-start | bytes 4718600 | tf_op jit(solution)/shard_map/ppermute | solution.py:774
  224.1 29.9 %collective-permute-start.37 = (f32[128,512]{1,0:T(8,128)}, f32[128,512]{1,0:T(8,128)}, u32[]{:S(2)}, u32[]{:S(2)}) collective-permute-start(f32[128,512]{1,0:T(8,128)} %get-tuple-element.522), channel_id=1, source_target_pairs={{0,4},{4,0},{8,12},{12,8},{16,20},{20,16},{24,28},{28,24},{1,5},{5... | collective-permute-start | bytes 786440 | tf_op jit(solution)/shard_map/ppermute | solution.py:774
  225.6 46.0 %collective-permute-start.35 = (f32[256,2048]{1,0:T(8,128)}, f32[256,2048]{1,0:T(8,128)}, u32[]{:S(2)}, u32[]{:S(2)}) collective-permute-start(f32[256,2048]{1,0:T(8,128)} %get-tuple-element.515), channel_id=1, source_target_pairs={{0,2},{1,3},{2,0},{3,1},{4,6},{5,7},{6,4},{7,5},{8,10},{9,11},{10,... | collective-permute-start | bytes 6291464 | tf_op jit(solution)/shard_map/ppermute | solution.py:771
  251.8 95.0 %collective-permute-start.42 = (f32[520,2048]{1,0:T(8,128)}, f32[520,2048]{1,0:T(8,128)}, u32[]{:S(2)}, u32[]{:S(2)}) collective-permute-start(f32[520,2048]{1,0:T(8,128)} %get-tuple-element.549), channel_id=1, source_target_pairs={{0,4},{4,0},{8,12},{12,8},{16,20},{20,16},{24,28},{28,24},{1,5},{5... | collective-permute-start | bytes 12779528 | tf_op jit(solution)/shard_map/ppermute | solution.py:774
  260.5 38.7 %collective-permute-start.43 = (f32[256,512]{1,0:T(8,128)}, f32[256,512]{1,0:T(8,128)}, u32[]{:S(2)}, u32[]{:S(2)}) collective-permute-start(f32[256,512]{1,0:T(8,128)} %get-tuple-element.552.refs_7_), channel_id=1, source_target_pairs={{0,8},{4,12},{8,0},{12,4},{16,24},{20,28},{24,16},{28,20},{1,9},{5... | collective-permute-start | bytes 1572872 | tf_op jit(solution)/shard_map/ppermute | solution.py:774
  262.2 44.7 %collective-permute-start.44 = (f32[256,512]{1,0:T(8,128)}, f32[256,512]{1,0:T(8,128)}, u32[]{:S(2)}, u32[]{:S(2)}) collective-permute-start(f32[256,512]{1,0:T(8,128)} %collective-permute-done.39.refs_8_), channel_id=1, source_target_pairs={{0,8},{4,12},{8,0},{12,4},{16,24},{20,28},{24,16},{28,20},{1,9},{5... | collective-permute-start | bytes 1572872 | tf_op jit(solution)/shard_map/ppermute | solution.py:774
  270.7 94.6 %collective-permute-start.46 = (f32[256,1536]{1,0:T(8,128)}, f32[256,1536]{1,0:T(8,128)}, u32[]{:S(2)}, u32[]{:S(2)}) collective-permute-start(f32[256,1536]{1,0:T(8,128)} %get-tuple-element.572), channel_id=1, source_target_pairs={{0,16},{4,20},{8,24},{12,28},{16,0},{20,4},{24,8},{28,12},{1,17},{... | collective-permute-start | bytes 4718600 | tf_op jit(solution)/shard_map/ppermute | solution.py:774
  337.0 28.3 %collective-permute-start.47 = (f32[256,512]{1,0:T(8,128)}, f32[256,512]{1,0:T(8,128)}, u32[]{:S(2)}, u32[]{:S(2)}) collective-permute-start(f32[256,512]{1,0:T(8,128)} %get-tuple-element.573), channel_id=1, source_target_pairs={{0,16},{4,20},{8,24},{12,28},{16,0},{20,4},{24,8},{28,12},{1,17},{... | collective-permute-start | bytes 1572872 | tf_op jit(solution)/shard_map/ppermute | solution.py:774
  (27 other events, 299.8 us)
